TPU v7x, 256 devices: a whole 4x4x8 slice. The times are simulated.
256 devices in a mesh: seq: 16 (over z, core), dp: 16 (over x, y).
Axes of the slice: x: 4, y: 4, z: 8, core: 2. Of those that a mesh axis runs over, the one named last changes fastest.
Arguments:
- query_in: bfloat16 [16, 2048, 2048], P('dp', 'seq'), may hold values from -8 to 8
- key_in: bfloat16 [16, 2048, 2048], P('dp', 'seq'), may hold values from -8 to 8
- value_in: bfloat16 [16, 2048, 2048], P('dp', 'seq'), may hold values from -6 to 6
- out_grad: bfloat16 [16, 2048, 2048], P('dp', 'seq'), may hold values from -6 to 6
- out_proj: bfloat16 [2048, 2048], P('seq'), may hold values from -0.125 to 0.125
- key_blocks: int32 [16, 16, 8], P('seq'), may hold values from 0 to 15, as said below
Outputs:
- layer_out: bfloat16 [16, 2048, 2048], P('dp', 'seq')
- query_grad: bfloat16 [16, 2048, 2048], P('dp', 'seq')
- key_grad: bfloat16 [16, 2048, 2048], P('dp', 'seq')
- value_grad: bfloat16 [16, 2048, 2048], P('dp', 'seq')
- proj_grad: float32 [2048, 2048], P('seq')
Inputs may be any that keep to these rules, and one draw needn't show every extreme that they name: `key_blocks`: for each head and query block b the 8 listed key blocks are different from one another and include b, b - 1 and b + 1 (modulo 16) and the blocks 0 and 1.
All inputs are finite; a program needn't handle non-finite values.
Results may differ from a plain program's by a relative error of at most 0.02.
Values may be sent and summed in bfloat16 or wider, within the bound.
No kernel may reach another device: no remote copies, remote signals or barrier semaphores. Data moves between devices by JAX's collectives and lax.ppermute only.
A program may use at most 128 MiB of HBM per device.

v0:
```python
import functools
import math

import jax
import jax.numpy as jnp
from jax import lax
from jax.experimental import pallas as pl
from jax.experimental.pallas import tpu as pltpu
from jax.sharding import Mesh
from jax.sharding import PartitionSpec as P

HEAD_DIM = 128
BLOCK = 128
INV_ROOT = 1.0 / math.sqrt(HEAD_DIM)
LOG2E = 1.0 / math.log(2.0)
BF16 = jnp.bfloat16
F32 = jnp.float32


def column_blocks(ref_value, count):
    return [ref_value[:, j * BLOCK : (j + 1) * BLOCK] for j in range(count)]


def pack_kernel(chunk_ref, q_ref, k_ref, v_ref, g_ref, w_ref, qkv_ref, gw_ref):
    count = qkv_ref.shape[0]
    for j in range(count):
        cols = slice(j * BLOCK, (j + 1) * BLOCK)
        qkv_ref[j, 0] = q_ref[:, cols]
        qkv_ref[j, 1] = k_ref[:, cols]
        qkv_ref[j, 2] = v_ref[:, cols]
        gw_ref[j] = g_ref[:, cols]
    gw_ref[count] = w_ref[:, pl.ds(pl.multiple_of(chunk_ref[0] * BLOCK, BLOCK), BLOCK)]


def pack(chunk, q, k, v, g, w):
    count = q.shape[1] // BLOCK
    vm = pl.BlockSpec(memory_space=pltpu.VMEM)
    return pl.pallas_call(
        pack_kernel,
        out_shape=(
            jax.ShapeDtypeStruct((count, 3, BLOCK, BLOCK), BF16),
            jax.ShapeDtypeStruct((count + 1, BLOCK, BLOCK), BF16),
        ),
        in_specs=[pl.BlockSpec(memory_space=pltpu.SMEM)] + [vm] * 5,
        out_specs=(vm, vm),
        compiler_params=pltpu.CompilerParams(vmem_limit_bytes=24 * 1024 * 1024),
        name="pack",
    )(chunk, q, k, v, g, w)


def attention_kernel(
    blocks_ref, core_ref, qkv_ref, own_ref, other_ref, w_ref, out_ref, pg_ref,
    kv_ref, kt_ref, vt_ref, acc_ref, wt_ref, pg_acc_ref,
):
    step = pl.program_id(0)
    block_count, slot_count = blocks_ref.shape
    half = block_count // 2
    zero = jnp.zeros((BLOCK, HEAD_DIM), BF16)

    @pl.when(step == 0)
    def _():
        def prepare(c, carry):
            rows = pl.ds(pl.multiple_of(c * BLOCK, BLOCK), BLOCK)
            k_one, v_one = qkv_ref[c, 1], qkv_ref[c, 2]
            kv_ref[rows, :] = jnp.concatenate([k_one, v_one], axis=1)
            kt_ref[c] = k_one.T
            vt_ref[c] = v_one.T
            acc_ref[rows, :] = jnp.zeros((BLOCK, 2 * HEAD_DIM), F32)
            return carry

        lax.fori_loop(0, block_count, prepare, 0)
        wt_ref[...] = w_ref[...].T
        pg_acc_ref[...] = jnp.zeros_like(pg_acc_ref)

    def work(g_ref, b):
        g_one = jnp.concatenate([g_ref[0, j] for j in range(block_count)], axis=1)
        d_one = jnp.dot(g_one, wt_ref[...], preferred_element_type=F32).astype(BF16)
        q_one = qkv_ref[b, 0]
        q_t, d_t = q_one.T, d_one.T
        owners = [blocks_ref[b, s] for s in range(slot_count)]
        picks = [pl.ds(pl.multiple_of(c * BLOCK, BLOCK), BLOCK) for c in owners]
        right = jnp.concatenate(
            [jnp.concatenate([q_t, zero], axis=1), jnp.concatenate([zero, d_t], axis=1)], axis=0
        )
        kv = jnp.concatenate([kv_ref[p, :] for p in picks], axis=0)
        both = jnp.dot(kv, right, preferred_element_type=F32)
        scores, prob_grad = both[:, :BLOCK], both[:, BLOCK:]
        top = jnp.max(scores, axis=0, keepdims=True)
        raised = jnp.exp2((scores - top) * (INV_ROOT * LOG2E))
        prob = raised * (1.0 / jnp.sum(raised, axis=0, keepdims=True))
        prob_bf = prob.astype(BF16)
        v_t = jnp.concatenate([vt_ref[c] for c in owners], axis=1)
        attn_t = jnp.dot(v_t, prob_bf, preferred_element_type=F32).astype(BF16)
        row_dot = jnp.sum(attn_t.astype(F32) * d_t.astype(F32), axis=0, keepdims=True)
        score_grad = (prob * (prob_grad - row_dot) * INV_ROOT).astype(BF16)
        k_t = jnp.concatenate([kt_ref[c] for c in owners], axis=1)
        dq_t = jnp.dot(k_t, score_grad, preferred_element_type=F32)
        out_ref[b, 0] = attn_t.T
        out_ref[b, 1] = dq_t.astype(BF16).T
        pg_acc_ref[...] += jnp.dot(attn_t, g_one, preferred_element_type=F32)
        back = jnp.concatenate(
            [jnp.concatenate([q_one, zero], axis=1), jnp.concatenate([zero, d_one], axis=1)], axis=0
        )
        parts = jnp.dot(
            jnp.concatenate([score_grad, prob_bf], axis=1), back, preferred_element_type=F32
        )
        for s, p in enumerate(picks):
            acc_ref[p, :] += parts[s * BLOCK : (s + 1) * BLOCK, :]

    @pl.when(step < half)
    def _():
        work(own_ref, 2 * step + core_ref[0])

    @pl.when(step >= half)
    def _():
        work(other_ref, 2 * (step - half) + 1 - core_ref[0])

    @pl.when(step == block_count - 1)
    def _():
        def finish(c, carry):
            rows = pl.ds(pl.multiple_of(c * BLOCK, BLOCK), BLOCK)
            out_ref[c, 2] = acc_ref[rows, :HEAD_DIM].astype(BF16)
            out_ref[c, 3] = acc_ref[rows, HEAD_DIM:].astype(BF16)
            return carry

        lax.fori_loop(0, block_count, finish, 0)
        for j in range(block_count):
            pg_ref[j] = pg_acc_ref[:, j * BLOCK : (j + 1) * BLOCK].astype(BF16)


def attention(blocks, core, qkv, own, other, w):
    count = qkv.shape[0]
    half = count // 2
    width = w.shape[1]
    chunks = width // BLOCK
    vm = pl.BlockSpec(memory_space=pltpu.VMEM)
    sm = pl.BlockSpec(memory_space=pltpu.SMEM)
    g_block = (1, chunks, BLOCK, BLOCK)
    return pl.pallas_call(
        attention_kernel,
        grid=(count,),
        out_shape=(
            jax.ShapeDtypeStruct((count, 4, BLOCK, HEAD_DIM), BF16),
            jax.ShapeDtypeStruct((chunks, HEAD_DIM, BLOCK), BF16),
        ),
        in_specs=[
            sm,
            sm,
            vm,
            pl.BlockSpec(g_block, lambda i: (jnp.minimum(i, half - 1), 0, 0, 0)),
            pl.BlockSpec(g_block, lambda i: (jnp.maximum(i - half, 0), 0, 0, 0)),
            vm,
        ],
        out_specs=(vm, vm),
        scratch_shapes=[
            pltpu.VMEM((count * BLOCK, 2 * HEAD_DIM), BF16),
            pltpu.VMEM((count, HEAD_DIM, BLOCK), BF16),
            pltpu.VMEM((count, HEAD_DIM, BLOCK), BF16),
            pltpu.VMEM((count * BLOCK, 2 * HEAD_DIM), F32),
            pltpu.VMEM((width, HEAD_DIM), BF16),
            pltpu.VMEM((HEAD_DIM, width), F32),
        ],
        compiler_params=pltpu.CompilerParams(
            dimension_semantics=("arbitrary",), vmem_limit_bytes=40 * 1024 * 1024
        ),
        name="attention",
    )(blocks, core, qkv, own, other, w)


def project_kernel(mine_ref, w_ref, layer_ref, dq_ref, dk_ref, dv_ref, rows_ref):
    count = mine_ref.shape[0]

    @pl.when(pl.program_id(0) == 0)
    def _():
        for h in range(count):
            cols = slice(h * HEAD_DIM, (h + 1) * HEAD_DIM)
            rows_ref[:, cols] = mine_ref[h, 0]
            dq_ref[:, cols] = mine_ref[h, 1]
            dk_ref[:, cols] = mine_ref[h, 2]
            dv_ref[:, cols] = mine_ref[h, 3]

    weights = jnp.concatenate(
        [w_ref[d].reshape(count * HEAD_DIM, BLOCK) for d in range(w_ref.shape[0])], axis=1
    )
    layer_ref[...] = jnp.dot(rows_ref[...], weights, preferred_element_type=F32).astype(BF16)


def project(mine, w):
    heads = mine.shape[0]
    chunks = w.shape[0]
    together = 4
    vm = pl.BlockSpec(memory_space=pltpu.VMEM)
    wide = jax.ShapeDtypeStruct((BLOCK, heads * HEAD_DIM), BF16)
    return pl.pallas_call(
        project_kernel,
        grid=(chunks // together,),
        out_shape=(jax.ShapeDtypeStruct((BLOCK, chunks * BLOCK), BF16), wide, wide, wide),
        in_specs=[
            vm,
            pl.BlockSpec((together, heads, HEAD_DIM, BLOCK), lambda i: (i, 0, 0, 0)),
        ],
        out_specs=(pl.BlockSpec((BLOCK, together * BLOCK), lambda i: (0, i)), vm, vm, vm),
        scratch_shapes=[pltpu.VMEM((BLOCK, heads * HEAD_DIM), BF16)],
        compiler_params=pltpu.CompilerParams(
            dimension_semantics=("arbitrary",), vmem_limit_bytes=40 * 1024 * 1024
        ),
        name="project",
    )(mine, w)


def body(query_in, key_in, value_in, out_grad, out_proj, key_blocks):
    seq, dp = ("z", "c"), ("x", "y")
    core = lax.axis_index("c")
    tokens = lax.axis_size(seq) * lax.axis_size(dp) * query_in.shape[1]
    place = lax.axis_index(dp).astype(jnp.int32)[None]
    qkv_out, gw = pack(place, query_in[0], key_in[0], value_in[0], out_grad[0], out_proj)
    gw_own = lax.all_gather(gw, "z", axis=0)
    qkv = lax.all_to_all(qkv_out, seq, split_axis=0, concat_axis=0, tiled=True)
    gw_other = lax.ppermute(gw_own, "c", [(0, 1), (1, 0)])
    w_own, w_other = gw_own[:, -1], gw_other[:, -1]
    first, second = jnp.where(core == 0, w_own, w_other), jnp.where(core == 0, w_other, w_own)
    w_chunk = jnp.stack([first, second], axis=1).reshape((-1,) + w_own.shape[1:])
    w_all = lax.all_gather(w_chunk, dp, axis=0)
    out, pg = attention(
        key_blocks[0], core.astype(jnp.int32)[None], qkv, gw_own, gw_other, out_proj
    )
    mine = lax.all_to_all(out, seq, split_axis=0, concat_axis=0, tiled=True)
    pg_parts = lax.all_to_all(pg, dp, split_axis=0, concat_axis=0, tiled=True)
    pg_sum = (jnp.sum(pg_parts.astype(F32), axis=0) * (1.0 / math.sqrt(tokens))).astype(BF16)
    pg_all = lax.all_to_all(
        jnp.broadcast_to(pg_sum[None], pg.shape), dp, split_axis=0, concat_axis=0, tiled=True
    )
    proj_grad = pg_all.transpose(1, 0, 2).reshape(out_proj.shape).astype(F32)
    layer, dq, dk, dv = project(mine, w_all)
    return layer[None], dq[None], dk[None], dv[None], proj_grad


def solution(mesh):
    split = Mesh(mesh.devices.reshape(8, 2, 4, 4), ("z", "c", "x", "y"))
    rows = P(("x", "y"), ("z", "c"), None)
    in_specs = (rows, rows, rows, rows, P(("z", "c"), None), P(("z", "c"), None, None))
    out_specs = (rows, rows, rows, rows, P(("z", "c"), None))
    return jax.shard_map(body, mesh=split, in_specs=in_specs, out_specs=out_specs, check_vma=False)
```

profile of v0, /device:TPU:1, one launch (start us, length us, event | category | flops | bytes accessed | tf_op | source)
XLA Modules:
  0.0 260.6 jit_solution(2224114144188138572)
XLA Ops:
  7.2 0.0 all-gather.6.cloned.1.call-start
  7.2 0.0 copy-start.3
  7.2 1.0 copy-done.3
  8.3 0.0 copy-start.6
  8.3 1.0 copy-done.6
  9.3 0.0 copy-start.7
  9.3 1.0 copy-done.7
  10.3 0.0 copy-start.8
  10.3 1.0 copy-done.8
  11.4 0.0 copy-start.9
  11.4 1.0 copy-done.9
  12.4 0.0 copy-start.10
  12.4 0.0 copy-start.4
  12.4 1.2 pack.1
  13.6 0.0 copy-start.5
  13.6 1.2 copy-done.5
  14.8 0.0 all-gather.6.cloned.1.call-update
  14.8 0.0 all-gather.4.cloned.1.call-start
  14.9 61.2 %all-gather.6.cloned.1.call-done = bf16[136,128,128]{2,1,0:T(8,128)(2,1)} async-done(((bf16[17,128,128]{2,1,0:T(8,128)(2,1)}), bf16[136,128,128]{2,1,0:T(8,128)(2,1)}) %all-gather.6.cloned.1.call-update) | async-done | bytes 4456464 | tf_op jit(solution)/shard_map/all_gather | solution.py:217
  76.0 0.7 collective-permute-start
  76.7 7.5 %collective-permute-done.other_ref = bf16[8,17,128,128]{3,2,1,0:T(8,128)(2,1)} collective-permute-done((bf16[8,17,128,128]{3,2,1,0:T(8,128)(2,1)}, bf16[8,17,128,128]{3,2,1,0:T(8,128)(2,1)}, u32[]{:S(2)}, u32[]{:S(2)}) %collective-permute-start) | collective-permute-done | bytes 4456480 | tf_op jit(solution)/shard_map/ppermute | solution.py:219
  84.2 1.1 broadcast_select_fusion.1
  85.3 0.8 pad_maximum_fusion
  86.1 0.0 all-gather.4.cloned.1.call-update
  86.2 4.7 %all-to-all-start = ((bf16[16,3,128,128]{3,2,1,0:T(8,128)(2,1)}), bf16[16,3,128,128]{3,2,1,0:T(8,128)(2,1)S(1)}, u32[]{:S(2)}, u32[]{:S(2)}) async-start(bf16[16,3,128,128]{3,2,1,0:T(8,128)(2,1)} %copy-done.5), calls=%async_computation | async-start | bytes 3145728 | tf_op jit(solution)/shard_map/all_to_all | solution.py:218
  90.9 0.0 copy-done.10
  90.9 0.1 copy.13.blocks_ref
  91.0 38.4 %all-to-all-done.qkv_ref = bf16[16,3,128,128]{3,2,1,0:T(8,128)(2,1)S(1)} async-done(((bf16[16,3,128,128]{3,2,1,0:T(8,128)(2,1)}), bf16[16,3,128,128]{3,2,1,0:T(8,128)(2,1)S(1)}, u32[]{:S(2)}, u32[]{:S(2)}) %all-to-all-start) | async-done | bytes 1572896 | tf_op jit(solution)/shard_map/all_to_all | solution.py:218
  129.3 0.0 copy-done.4
  129.3 0.0 copy-start.1
  129.3 2.4 copy-done.1
  131.8 29.1 %attention.1 = (bf16[16,4,128,128]{3,2,1,0:T(8,128)(2,1)S(1)}, bf16[16,128,128]{2,1,0:T(8,128)(2,1)S(1)}) custom-call(s32[16,8]{1,0:T(8,128)S(1)} %copy.13.blocks_ref, s32[1]{0:T(128)} %bitcast.1.core_ref, bf16[16,3,128,128]{3,2,1,0:T(8,128)(2,1)S(1)} %all-to-all-done.qkv_ref, bf16[8,17,128,128]{3,2,1,0:T(8,128)(2,1)S(1)} %bitcast.18, ...), custom_call_target="tpu_custom_call" | custom-call | tf_op jit(solution)/shard_map/attention/pallas_call | solution.py:139
  160.8 0.0 copy-start.2
  160.8 17.7 %all_to_all.20 = bf16[16,128,128]{2,1,0:T(8,128)(2,1)S(1)} all-to-all(bf16[16,128,128]{2,1,0:T(8,128)(2,1)S(1)} %get-tuple-element.20), channel_id=1, replica_groups=mesh['z'=8,'c'=2,'x'=4,'y'=4] {'x','y'}, dimensions={0} | all-to-all | bytes 1048576 | tf_op jit(solution)/shard_map/all_to_all | solution.py:228
  178.5 0.1 convert_reduce_fusion
  178.6 0.1 broadcast_in_dim.30
  178.7 13.5 %all_to_all.21 = bf16[16,128,128]{2,1,0:T(8,128)(2,1)S(1)} all-to-all(bf16[16,128,128]{2,1,0:T(8,128)(2,1)S(1)} %broadcast_in_dim.30), channel_id=1, replica_groups=mesh['z'=8,'c'=2,'x'=4,'y'=4] {'x','y'}, dimensions={0} | all-to-all | bytes 1048576 | tf_op jit(solution)/shard_map/all_to_all | solution.py:230
  192.3 0.0 copy-done.2
  192.3 5.7 %all-to-all-start.1 = ((bf16[16,4,128,128]{3,2,1,0:T(8,128)(2,1)}), bf16[16,4,128,128]{3,2,1,0:T(8,128)(2,1)S(1)}, u32[]{:S(2)}, u32[]{:S(2)}) async-start(bf16[16,4,128,128]{3,2,1,0:T(8,128)(2,1)} %copy-done.2), calls=%async_computation.1 | async-start | bytes 4194304 | tf_op jit(solution)/shard_map/all_to_all | solution.py:227
  197.9 0.3 copy.14
  198.2 1.1 convert_element_type.25
  199.3 2.5 copy.15
  201.8 45.1 %all-to-all-done.1.mine_ref = bf16[16,4,128,128]{3,2,1,0:T(8,128)(2,1)S(1)} async-done(((bf16[16,4,128,128]{3,2,1,0:T(8,128)(2,1)}), bf16[16,4,128,128]{3,2,1,0:T(8,128)(2,1)S(1)}, u32[]{:S(2)}, u32[]{:S(2)}) %all-to-all-start.1) | async-done | bytes 2097184 | tf_op jit(solution)/shard_map/all_to_all | solution.py:227
  246.9 0.0 all-gather.4.cloned.1.call-done.w_ref
  246.9 0.0 copy-start
  246.9 3.4 %copy-done = bf16[16,16,128,128]{3,2,1,0:T(8,128)(2,1)S(1)} copy-done((bf16[16,16,128,128]{3,2,1,0:T(8,128)(2,1)S(1)}, bf16[16,16,128,128]{3,2,1,0:T(8,128)(2,1)}, u32[]{:S(2)}) %copy-start) | copy-done | bytes 8388632
  250.3 3.4 %project.1 = (bf16[128,2048]{1,0:T(8,128)(2,1)}, bf16[128,2048]{1,0:T(8,128)(2,1)}, bf16[128,2048]{1,0:T(8,128)(2,1)}, bf16[128,2048]{1,0:T(8,128)(2,1)}) custom-call(bf16[16,4,128,128]{3,2,1,0:T(8,128)(2,1)S(1)} %all-to-all-done.1.mine_ref, bf16[16,16,128,128]{3,2,1,0:T(8,128)(2,1)S(1)} %copy-done), custom_call_target="tpu_custom_call" | custom-call | tf_op jit(solution)/shard_map/project/pallas_call | solution.py:194
  (1 shorter events, 0.0 us)
Async XLA Ops:
  7.2 68.9 %all-gather.6.cloned.1.call-start = ((), (), s32[]{:S(2)}) async-start(), calls=%async_computation.5 | async-start | bytes 5013504 | tf_op jit(solution)/shard_map/all_gather | solution.py:217
  7.2 1.0 copy-start.3
  8.3 1.0 copy-start.6
  9.3 1.0 copy-start.7
  10.3 1.0 copy-start.8
  11.4 1.0 copy-start.9
  12.4 78.5 %copy-start.10 = (s32[1,16,8]{1,2,0:T(8,128)S(1)}, s32[1,16,8]{1,2,0:T(8,128)}, u32[]{:S(2)}) copy-start(s32[1,16,8]{1,2,0:T(8,128)} %param.11) | copy-start | bytes 1540
  12.4 116.9 %copy-start.4 = (bf16[128,2048]{1,0:T(8,128)(2,1)S(1)}, bf16[128,2048]{1,0:T(8,128)(2,1)}, u32[]{:S(2)}) copy-start(bf16[128,2048]{1,0:T(8,128)(2,1)} %w_ref.3) | copy-start | bytes 1572868
  13.6 1.2 copy-start.5
  14.8 232.1 %all-gather.4.cloned.1.call-start = ((), (), s32[]{:S(2)}) async-start(), calls=%async_computation.4 | async-start | bytes 8912896 | tf_op jit(solution)/shard_map/all_gather | solution.py:223
  76.0 8.2 %collective-permute-start = (bf16[8,17,128,128]{3,2,1,0:T(8,128)(2,1)}, bf16[8,17,128,128]{3,2,1,0:T(8,128)(2,1)}, u32[]{:S(2)}, u32[]{:S(2)}) collective-permute-start(bf16[8,17,128,128]{3,2,1,0:T(8,128)(2,1)} %bitcast.16), channel_id=1, source_target_pairs={{0,16},{16,0},{1,17},{17,1},{2,18},{18,2},{3,19},{19,3},{4,20},{20... | collective-permute-start | bytes 13369352 | tf_op jit(solution)/shard_map/ppermute | solution.py:219
  86.2 43.2 %all-to-all-start = ((bf16[16,3,128,128]{3,2,1,0:T(8,128)(2,1)}), bf16[16,3,128,128]{3,2,1,0:T(8,128)(2,1)S(1)}, u32[]{:S(2)}, u32[]{:S(2)}) async-start(bf16[16,3,128,128]{3,2,1,0:T(8,128)(2,1)} %copy-done.5), calls=%async_computation | async-start | bytes 3145728 | tf_op jit(solution)/shard_map/all_to_all | solution.py:218
  129.3 2.4 copy-start.1
  160.8 31.4 %copy-start.2 = (bf16[16,4,128,128]{3,2,1,0:T(8,128)(2,1)}, bf16[16,4,128,128]{3,2,1,0:T(8,128)(2,1)S(1)}, u32[]{:S(2)}) copy-start(bf16[16,4,128,128]{3,2,1,0:T(8,128)(2,1)S(1)} %get-tuple-element.15) | copy-start | bytes 6291460
  192.3 54.6 %all-to-all-start.1 = ((bf16[16,4,128,128]{3,2,1,0:T(8,128)(2,1)}), bf16[16,4,128,128]{3,2,1,0:T(8,128)(2,1)S(1)}, u32[]{:S(2)}, u32[]{:S(2)}) async-start(bf16[16,4,128,128]{3,2,1,0:T(8,128)(2,1)} %copy-done.2), calls=%async_computation.1 | async-start | bytes 4194304 | tf_op jit(solution)/shard_map/all_to_all | solution.py:227
  246.9 3.4 %copy-start = (bf16[16,16,128,128]{3,2,1,0:T(8,128)(2,1)S(1)}, bf16[16,16,128,128]{3,2,1,0:T(8,128)(2,1)}, u32[]{:S(2)}) copy-start(bf16[16,16,128,128]{3,2,1,0:T(8,128)(2,1)} %all-gather.4.cloned.1.call-done.w_ref) | copy-start | bytes 25165828
Sparse Core Ops, SparseCore 0:
  14.9 61.0 all-gather.5
  86.3 74.0 all-gather.3
where the time goes:
time: 261 us
  waiting for transfers between devices  152 us (58%)
  Pallas kernels  33.7 us (13%)
  blocking collectives  31.2 us (12%)
  local copies, waits for them, and re-layouts  15.2 us (6%)
  between operations  14.1 us (5%)
  starting transfers between devices  11.1 us (4%)
  other arithmetic  3.09 us (1%)
    all_gather x1, waiting for transfers between devices, body(): gw_own = lax.all_gather(gw, 'z', axis=0)  61.2 us
    all_to_all x1, waiting for transfers between devices, body(): mine = lax.all_to_all(out, seq, split_axis=0, concat_axis=0, tiled=True)  45.1 us
    all_to_all x1, waiting for transfers between devices, body(): qkv = lax.all_to_all(qkv_out, seq, split_axis=0, concat_axis=0, tiled=True)  38.4 us
    pallas_call x1, Pallas kernels, attention(): pl.pallas_call(attention_kernel, grid=(count,), out_shape=(jax.ShapeDtype...  29.1 us
    all_to_all x1, blocking collectives, body(): pg_parts = lax.all_to_all(pg, dp, split_axis=0, concat_axis=0, tiled=True)  17.7 us
    unnamed x23, local copies, waits for them, and re-layouts  14.7 us
    all_to_all x1, blocking collectives, body(): lax.all_to_all(jnp.broadcast_to(pg_sum[None], pg.shape), dp, split_axis=0...  13.5 us
    ppermute x1, waiting for transfers between devices, body(): gw_other = lax.ppermute(gw_own, 'c', [(0, 1), (1, 0)])  7.5 us
  transfers between devices with their start and end apart: 5, of which 4 were waited for; matrix products, arithmetic and copies ran while one was open for 2% of the time, Pallas kernels for 11%

commit v1 on v0

v1 whole, which is shorter than its diff:
```python
import functools
import math

import jax
import jax.numpy as jnp
from jax import lax
from jax.experimental import pallas as pl
from jax.experimental.pallas import tpu as pltpu
from jax.sharding import Mesh
from jax.sharding import PartitionSpec as P

HEAD_DIM = 128
BLOCK = 128
INV_ROOT = 1.0 / math.sqrt(HEAD_DIM)
LOG2E = 1.0 / math.log(2.0)
BF16 = jnp.bfloat16
F32 = jnp.float32
VM = pl.BlockSpec(memory_space=pltpu.VMEM)
SM = pl.BlockSpec(memory_space=pltpu.SMEM)
ANY = pl.BlockSpec(memory_space=pl.ANY)
MIB = 1024 * 1024


def like(*shape, dtype=BF16):
    return jax.ShapeDtypeStruct(shape, dtype)


def pack_kernel(place_ref, q_ref, k_ref, v_ref, g_ref, w_ref, qkv_ref, gw_ref, sem):
    count = qkv_ref.shape[0]
    copies = []

    def send(source, target):
        copy = pltpu.make_async_copy(source, target, sem.at[len(copies)])
        copy.start()
        copies.append(copy)

    send(w_ref.at[:, pl.ds(pl.multiple_of(place_ref[0] * BLOCK, BLOCK), BLOCK)], gw_ref.at[count])
    for j in range(count):
        cols = pl.ds(j * BLOCK, BLOCK)
        send(g_ref.at[:, cols], gw_ref.at[j])
        send(q_ref.at[:, cols], qkv_ref.at[j, 0])
        send(k_ref.at[:, cols], qkv_ref.at[j, 1])
        send(v_ref.at[:, cols], qkv_ref.at[j, 2])
    for copy in copies:
        copy.wait()


def pack(place, q, k, v, g, w):
    count = q.shape[1] // BLOCK
    return pl.pallas_call(
        pack_kernel,
        out_shape=(like(count, 3, BLOCK, BLOCK), like(count + 1, BLOCK, BLOCK)),
        in_specs=[SM] + [ANY] * 5,
        out_specs=(ANY, ANY),
        scratch_shapes=[pltpu.SemaphoreType.DMA((4 * count + 1,))],
        name="pack",
    )(place, q, k, v, g, w)


def rows_of(c):
    return pl.ds(pl.multiple_of(c * BLOCK, BLOCK), BLOCK)


def forward_kernel(blocks_ref, qkv_ref, attn_ref, attn_t_ref, lse_ref, vt_ref):
    block_count, slot_count = blocks_ref.shape

    def prepare(c, carry):
        vt_ref[c] = qkv_ref[c, 2].T
        return carry

    lax.fori_loop(0, block_count, prepare, 0, unroll=4)

    def one(b):
        owners = [blocks_ref[b, s] for s in range(slot_count)]
        keys = jnp.concatenate([qkv_ref[c, 1] for c in owners], axis=0)
        scores = jnp.dot(keys, qkv_ref[b, 0].T, preferred_element_type=F32)
        top = jnp.max(scores, axis=0, keepdims=True)
        raised = jnp.exp2((scores - top) * (INV_ROOT * LOG2E))
        total = jnp.sum(raised, axis=0, keepdims=True)
        prob = (raised * (1.0 / total)).astype(BF16)
        v_t = jnp.concatenate([vt_ref[c] for c in owners], axis=1)
        attn_t = jnp.dot(v_t, prob, preferred_element_type=F32).astype(BF16)
        attn_t_ref[b] = attn_t
        attn_ref[b] = attn_t.T
        lse_ref[b] = top * (INV_ROOT * LOG2E) + jnp.log2(total)

    def step(i, carry):
        one(2 * i)
        one(2 * i + 1)
        return carry

    lax.fori_loop(0, block_count // 2, step, 0)


def forward(blocks, qkv):
    count = qkv.shape[0]
    return pl.pallas_call(
        forward_kernel,
        out_shape=(
            like(count, BLOCK, HEAD_DIM),
            like(count, HEAD_DIM, BLOCK),
            like(count, 1, BLOCK, dtype=F32),
        ),
        in_specs=[SM, VM],
        out_specs=(VM, VM, VM),
        scratch_shapes=[pltpu.VMEM((count, HEAD_DIM, BLOCK), BF16)],
        compiler_params=pltpu.CompilerParams(vmem_limit_bytes=24 * MIB),
        name="forward",
    )(blocks, qkv)


def backward_kernel(parts, blocks_ref, place_ref, qkv_ref, attn_t_ref, lse_ref, w_ref, *refs):
    g_refs = refs[: len(parts)]
    out_ref, pg_ref, kv_ref, kt_ref, acc_ref, wt_ref, pg_acc_ref, g_buf, sem = refs[len(parts) :]
    block_count, slot_count = blocks_ref.shape
    half = block_count // 2
    zero = jnp.zeros((BLOCK, HEAD_DIM), BF16)

    def fetch(pair, act):
        for n, (shift, side, low, high) in enumerate(parts):
            if isinstance(pair, int) and pair != shift:
                continue

            def go(n=n, shift=shift, side=side, low=low, high=high):
                slot = shift % 2
                act(
                    pltpu.make_async_copy(
                        g_refs[n].at[pl.ds(0, high - low)],
                        g_buf.at[slot, side, pl.ds(low, high - low)],
                        sem.at[slot, side, 0 if low == 0 else 1],
                    )
                )

            if isinstance(pair, int):
                go()
            else:
                pl.when(pair == shift)(go)

    fetch(0, lambda copy: copy.start())

    def prepare(c, carry):
        k_one, v_one = qkv_ref[c, 1], qkv_ref[c, 2]
        kv_ref[rows_of(c), :] = jnp.concatenate([k_one, v_one], axis=1)
        kt_ref[c] = k_one.T
        acc_ref[rows_of(c), :] = jnp.zeros((BLOCK, 2 * HEAD_DIM), F32)
        return carry

    lax.fori_loop(0, block_count, prepare, 0, unroll=2)
    wt_ref[...] = w_ref[...].T
    pg_acc_ref[...] = jnp.zeros_like(pg_acc_ref)

    def one(b, d_one):
        q_one = qkv_ref[b, 0]
        q_t, d_t = q_one.T, d_one.T
        owners = [blocks_ref[b, s] for s in range(slot_count)]
        right = jnp.concatenate(
            [jnp.concatenate([q_t, zero], axis=1), jnp.concatenate([zero, d_t], axis=1)], axis=0
        )
        kv = jnp.concatenate([kv_ref[rows_of(c), :] for c in owners], axis=0)
        both = jnp.dot(kv, right, preferred_element_type=F32)
        scores, prob_grad = both[:, :BLOCK], both[:, BLOCK:]
        prob = jnp.exp2(scores * (INV_ROOT * LOG2E) - lse_ref[b])
        row_dot = jnp.sum(attn_t_ref[b].astype(F32) * d_t.astype(F32), axis=0, keepdims=True)
        score_grad = (prob * (prob_grad - row_dot) * INV_ROOT).astype(BF16)
        k_t = jnp.concatenate([kt_ref[c] for c in owners], axis=1)
        dq_t = jnp.dot(k_t, score_grad, preferred_element_type=F32)
        out_ref[b, 0] = dq_t.astype(BF16).T
        back = jnp.concatenate(
            [jnp.concatenate([q_one, zero], axis=1), jnp.concatenate([zero, d_one], axis=1)], axis=0
        )
        return owners, jnp.dot(
            jnp.concatenate([score_grad, prob.astype(BF16)], axis=1),
            back,
            preferred_element_type=F32,
        )

    def step(i, carry):
        slot = lax.rem(i, 2)
        fetch(i, lambda copy: copy.wait())
        fetch(i + 1, lambda copy: copy.start())
        chip = lax.rem(place_ref[0] + place_ref[2 + i], half)
        mine = 2 * chip + place_ref[1]
        theirs = 2 * chip + 1 - place_ref[1]
        g_two = jnp.concatenate(
            [
                jnp.concatenate([g_buf[slot, side, j] for j in range(pg_ref.shape[0])], axis=1)
                for side in range(2)
            ],
            axis=0,
        )
        d_two = jnp.dot(g_two, wt_ref[...], preferred_element_type=F32).astype(BF16)
        results = [one(mine, d_two[:BLOCK]), one(theirs, d_two[BLOCK:])]
        for owners, found in results:
            for s, c in enumerate(owners):
                acc_ref[rows_of(c), :] += found[s * BLOCK : (s + 1) * BLOCK, :]
        attn_two = jnp.concatenate([attn_t_ref[mine], attn_t_ref[theirs]], axis=1)
        pg_acc_ref[...] += jnp.dot(attn_two, g_two, preferred_element_type=F32)
        return carry

    lax.fori_loop(0, half, step, 0)

    def finish(c, carry):
        out_ref[c, 1] = acc_ref[rows_of(c), :HEAD_DIM].astype(BF16)
        out_ref[c, 2] = acc_ref[rows_of(c), HEAD_DIM:].astype(BF16)
        return carry

    lax.fori_loop(0, block_count, finish, 0, unroll=2)
    for j in range(pg_ref.shape[0]):
        pg_ref[j] = pg_acc_ref[:, j * BLOCK : (j + 1) * BLOCK].astype(BF16)


def backward(blocks, place, qkv, attn_t, lse, w, parts, shards):
    count = qkv.shape[0]
    width = w.shape[1]
    chunks = width // BLOCK
    return pl.pallas_call(
        functools.partial(backward_kernel, parts),
        out_shape=(like(count, 3, BLOCK, HEAD_DIM), like(chunks, HEAD_DIM, BLOCK)),
        in_specs=[SM, SM] + [VM] * 4 + [ANY] * len(shards),
        out_specs=(VM, VM),
        scratch_shapes=[
            pltpu.VMEM((count * BLOCK, 2 * HEAD_DIM), BF16),
            pltpu.VMEM((count, HEAD_DIM, BLOCK), BF16),
            pltpu.VMEM((count * BLOCK, 2 * HEAD_DIM), F32),
            pltpu.VMEM((width, HEAD_DIM), BF16),
            pltpu.VMEM((HEAD_DIM, width), F32),
            pltpu.VMEM((2, 2, chunks, BLOCK, BLOCK), BF16),
            pltpu.SemaphoreType.DMA((2, 2, 2)),
        ],
        compiler_params=pltpu.CompilerParams(vmem_limit_bytes=32 * MIB),
        name="backward",
    )(blocks, place, qkv, attn_t, lse, w, *shards)


def project_kernel(groups, heads_ref, cols_ref, mine_ref, *refs):
    w_refs, layer_ref, rows_ref = refs[:-2], refs[-2], refs[-1]
    count = mine_ref.shape[0]
    for e in range(count):
        rows_ref[:, e * HEAD_DIM : (e + 1) * HEAD_DIM] = mine_ref[heads_ref[e]]
    half = count // 2
    rows = rows_ref[...]
    for i in range(groups):
        for j in range(0, groups, 2):
            weights = jnp.concatenate(
                [
                    jnp.concatenate(
                        [
                            w_refs[i][t].reshape(half * HEAD_DIM, BLOCK),
                            w_refs[groups + t][i].reshape(half * HEAD_DIM, BLOCK),
                        ],
                        axis=0,
                    )
                    for t in (j, j + 1)
                ],
                axis=1,
            )
            found = jnp.dot(rows, weights, preferred_element_type=F32).astype(BF16)
            for n in range(2):
                at = pl.multiple_of(cols_ref[i * groups + j + n] * BLOCK, BLOCK)
                layer_ref[:, pl.ds(at, BLOCK)] = found[:, n * BLOCK : (n + 1) * BLOCK]


def project(heads, cols, mine, pieces):
    count = mine.shape[0]
    groups = len(pieces) // 2
    return pl.pallas_call(
        functools.partial(project_kernel, groups),
        out_shape=like(BLOCK, groups * groups * BLOCK),
        in_specs=[SM, SM, VM] + [VM] * len(pieces),
        out_specs=VM,
        scratch_shapes=[pltpu.VMEM((BLOCK, count * HEAD_DIM), BF16)],
        compiler_params=pltpu.CompilerParams(vmem_limit_bytes=32 * MIB),
        name="project",
    )(heads, cols, mine, *pieces)


def unpack_kernel(cols_ref, grads_ref, *refs):
    pg_refs = refs[:-4]
    dq_ref, dk_ref, dv_ref, pg_ref = refs[-4:]
    for h in range(grads_ref.shape[0]):
        cols = slice(h * HEAD_DIM, (h + 1) * HEAD_DIM)
        dq_ref[:, cols] = grads_ref[h, 0]
        dk_ref[:, cols] = grads_ref[h, 1]
        dv_ref[:, cols] = grads_ref[h, 2]
    groups = len(pg_refs)
    for i in range(groups):
        for j in range(groups):
            at = pl.multiple_of(cols_ref[i * groups + j] * BLOCK, BLOCK)
            pg_ref[:, pl.ds(at, BLOCK)] = pg_refs[i][j].astype(F32)


def unpack(cols, grads, pg_pieces):
    wide = like(BLOCK, grads.shape[0] * HEAD_DIM)
    groups = len(pg_pieces)
    return pl.pallas_call(
        unpack_kernel,
        out_shape=(wide, wide, wide, like(HEAD_DIM, groups * groups * BLOCK, dtype=F32)),
        in_specs=[SM, VM] + [VM] * groups,
        out_specs=(VM,) * 4,
        compiler_params=pltpu.CompilerParams(vmem_limit_bytes=24 * MIB),
        name="unpack",
    )(cols, grads, *pg_pieces)


def shifted(value, axis, by):
    size = lax.axis_size(axis)
    return lax.ppermute(value, axis, [(i, (i + by) % size) for i in range(size)])


def from_others(value, axis):
    return [value] + [shifted(value, axis, i) for i in range(1, lax.axis_size(axis))]


def spread(value, axis):
    size = lax.axis_size(axis)
    here = lax.axis_index(axis)
    total = lax.dynamic_index_in_dim(value, here, 0, keepdims=False).astype(F32)
    for i in range(1, size):
        piece = lax.dynamic_index_in_dim(value, (here + i) % size, 0, keepdims=False)
        total = total + shifted(piece, axis, i).astype(F32)
    return total


def ring(gw):
    size = lax.axis_size("z")
    found = [(0, 0, gw.shape[0], gw)]
    up = down = gw
    for k in range(1, size // 2):
        up, down = shifted(up, "z", 1), shifted(down, "z", -1)
        found += [(-k, 0, gw.shape[0], up), (k, 0, gw.shape[0], down)]
    cut = gw.shape[0] // 2
    found.append((size // 2, 0, cut, shifted(up[:cut], "z", 1)))
    found.append((size // 2, cut, gw.shape[0], shifted(down[cut:], "z", -1)))
    return found


def body(query_in, key_in, value_in, out_grad, out_proj, key_blocks):
    seq, dp = ("z", "c"), ("x", "y")
    chips = lax.axis_size("z")
    core, z = lax.axis_index("c").astype(jnp.int32), lax.axis_index("z").astype(jnp.int32)
    x, y = lax.axis_index("x").astype(jnp.int32), lax.axis_index("y").astype(jnp.int32)
    tokens = lax.axis_size(seq) * lax.axis_size(dp) * query_in.shape[1]
    groups = lax.axis_size("x")
    place = (x * groups + y)[None]
    qkv_out, gw = pack(place, query_in[0], key_in[0], value_in[0], out_grad[0], out_proj)
    qkv = lax.all_to_all(qkv_out, seq, split_axis=0, concat_axis=0, tiled=True)
    last = gw.shape[0] - 1

    shifts = []
    parts, shards, w_blocks, heads = [], [], [], []
    for shift, low, high, array in ring(gw):
        if shift not in shifts:
            shifts.append(shift)
        pair = shifts.index(shift)
        other = lax.ppermute(array, "c", [(0, 1), (1, 0)])
        for side, piece in enumerate((array, other)):
            parts.append((pair, side, low, min(high, last)))
            shards.append(piece)
            if high == last + 1:
                w_blocks.append(piece[last - low])
                owner = 2 * ((z + shift) % chips)
                heads.append(owner + (core if side == 0 else 1 - core))
    heads = jnp.stack(heads)
    w_low, w_high = jnp.stack(w_blocks[: chips]), jnp.stack(w_blocks[chips:])
    w_pieces = from_others(jnp.stack(from_others(w_low, "y")), "x")
    w_pieces += from_others(jnp.stack(from_others(w_high, "x")), "y")
    index = jnp.arange(groups, dtype=jnp.int32)
    cols = (((x - index) % groups)[:, None] * groups + ((y - index) % groups)[None]).reshape(-1)

    blocks = key_blocks[0]
    attn, attn_t, lse = forward(blocks, qkv)
    attn_rows = lax.all_to_all(attn, seq, split_axis=0, concat_axis=0, tiled=True)
    spot = jnp.stack([z, core] + [jnp.int32(s % chips) for s in shifts])
    grads, pg = backward(blocks, spot, qkv, attn_t, lse, out_proj, tuple(parts), shards)
    grad_rows = lax.all_to_all(grads, seq, split_axis=0, concat_axis=0, tiled=True)
    pg = spread(pg.reshape((groups, groups) + pg.shape[1:]), "x").astype(BF16)
    pg = (spread(pg, "y") * (1.0 / math.sqrt(tokens))).astype(BF16)
    pg_pieces = from_others(jnp.stack(from_others(pg, "y")), "x")
    layer = project(heads, cols, attn_rows, w_pieces)
    dq, dk, dv, proj_grad = unpack(cols, grad_rows, pg_pieces)
    return layer[None], dq[None], dk[None], dv[None], proj_grad


def solution(mesh):
    split = Mesh(mesh.devices.reshape(8, 2, 4, 4), ("z", "c", "x", "y"))
    rows = P(("x", "y"), ("z", "c"), None)
    in_specs = (rows, rows, rows, rows, P(("z", "c"), None), P(("z", "c"), None, None))
    out_specs = (rows, rows, rows, rows, P(("z", "c"), None))
    return jax.shard_map(body, mesh=split, in_specs=in_specs, out_specs=out_specs, check_vma=False)
```

time: 261 us -> 366 us (1.40); the launches traced: 261 us -> 362 us
  Pallas kernels: 33.7 us -> 103 us
  starting transfers between devices: 11.1 us -> 66.8 us
  blocking collectives: 31.2 us -> 0 us
  between operations: 14.1 us -> 0.92 us
  local copies, waits for them, and re-layouts: 15.2 us -> 27.1 us
  waiting for transfers between devices: 152 us -> 160 us
    ppermute x1 -> x41, waiting for transfers between devices: 7.5 us -> 160 us  [the longest x32 160 us: shifted(): lax.ppermute(value, axis, [(i, (i + by) % size) for i in range(size)])]
    pallas_call x3 -> x5, Pallas kernels: 33.7 us -> 103 us  [the longest x1 66.2 us: pack(): pl.pallas_call(pack_kernel, out_shape=(like(count, 3, BLOCK, BLOCK), like...]
    all_gather x2 -> x0, waiting for transfers between devices: 61.2 us -> none  [the longest x1 61.2 us: body(): gw_own = lax.all_gather(gw, 'z', axis=0)]
    all_to_all x1 -> x2, waiting for transfers between devices: 45.1 us -> 0.01 us  [the longest x1 0.01 us: body(): lax.all_to_all(grads, seq, split_axis=0, concat_axis=0, tiled=True)]
    ppermute x1 -> x41, starting transfers between devices: 0.68 us -> 44.5 us  [the longest x32 38.2 us: shifted(): lax.ppermute(value, axis, [(i, (i + by) % size) for i in range(size)])]
    all_to_all x1, waiting for transfers between devices: 38.4 us -> 0.01 us  [body(): qkv = lax.all_to_all(qkv_out, seq, split_axis=0, concat_axis=0, tiled=True)]
    all_to_all x2 -> x0, blocking collectives: 31.2 us -> none  [the longest x1 17.7 us: body(): pg_parts = lax.all_to_all(pg, dp, split_axis=0, concat_axis=0, tiled=True)]
    all_to_all x1 -> x2, starting transfers between devices: 5.66 us -> 12.2 us  [the longest x1 6.29 us: body(): lax.all_to_all(grads, seq, split_axis=0, concat_axis=0, tiled=True)]
  transfers between devices with their start and end apart: 5 -> 44, of which waited for: 4 -> 12; matrix products, arithmetic and copies ran while one was open for 2% -> 6% of each run, Pallas kernels for 11% -> 9%
where the time goes in v1:
time: 366 us; the launch traced here: 362 us
  waiting for transfers between devices  160 us (44%)
  Pallas kernels  103 us (28%)
  starting transfers between devices  66.8 us (18%)
  local copies, waits for them, and re-layouts  27.1 us (7%)
  other arithmetic  4.39 us (1%)
    ppermute x32, waiting for transfers between devices, shifted(): lax.ppermute(value, axis, [(i, (i + by) % size) for i in range(size)])  160 us
    pallas_call x1, Pallas kernels, pack(): pl.pallas_call(pack_kernel, out_shape=(like(count, 3, BLOCK, BLOCK), like...  66.2 us
    ppermute x32, starting transfers between devices, shifted(): lax.ppermute(value, axis, [(i, (i + by) % size) for i in range(size)])  38.2 us
    unnamed x50, local copies, waits for them, and re-layouts  20.9 us
    pallas_call x1, Pallas kernels, backward(): pl.pallas_call(functools.partial(backward_kernel, parts), out_shape=(like...  16.4 us
    pallas_call x1, Pallas kernels, forward(): pl.pallas_call(forward_kernel, out_shape=(like(count, BLOCK, HEAD_DIM), l...  11.7 us
    all_to_all x1, starting transfers between devices, body(): qkv = lax.all_to_all(qkv_out, seq, split_axis=0, concat_axis=0, tiled=True)  10.1 us
  transfers between devices with their start and end apart: 44, of which 12 were waited for; matrix products, arithmetic and copies ran while one was open for 6% of the time, Pallas kernels for 9%

profile of v1, /device:TPU:1, one launch (start us, length us, event | category | flops | bytes accessed | tf_op | source)
XLA Modules:
  0.0 361.7 jit_solution(4786268762104914462)
XLA Ops:
  0.6 66.2 %pack.1 = (bf16[16,3,128,128]{3,2,1,0:T(8,128)(2,1)}, bf16[17,128,128]{2,1,0:T(8,128)(2,1)}) custom-call(s32[1]{0:T(128)} %bitcast.17.place_ref, bf16[128,2048]{1,0:T(8,128)(2,1)} %bitcast.62, bf16[128,2048]{1,0:T(8,128)(2,1)} %bitcast.63, bf16[128,2048]{1,0:T(8,128)(2,1)} %bitcast.64, bf16[128,2048]{1,0:T(8,128)(2,1)} %bitcast.65, bf16[128,2048]{1,0:T(8,128)(2,1)} %w_ref.3), custom_call_target="tpu_custom_call" | custom-call | tf_op jit(solution)/shard_map/pack/pallas_call | solution.py:50
  66.9 10.1 %all-to-all-start = ((bf16[16,3,128,128]{3,2,1,0:T(8,128)(2,1)}), bf16[16,3,128,128]{3,2,1,0:T(8,128)(2,1)S(1)}, u32[]{:S(2)}, u32[]{:S(2)}) async-start(bf16[16,3,128,128]{3,2,1,0:T(8,128)(2,1)} %get-tuple-element.16), calls=%async_computation | async-start | bytes 3145728 | tf_op jit(solution)/shard_map/all_to_all | solution.py:346
  77.0 1.5 collective-permute-start.1
  78.5 1.3 collective-permute-start.3
  80.4 45.8 %collective-permute-done.1.refs_2_ = bf16[17,128,128]{2,1,0:T(8,128)(2,1)S(1)} collective-permute-done((bf16[17,128,128]{2,1,0:T(8,128)(2,1)S(1)}, bf16[17,128,128]{2,1,0:T(8,128)(2,1)S(1)}, u32[]{:S(2)}, u32[]{:S(2)}) %collective-permute-start.1) | collective-permute-done | bytes 557088 | tf_op jit(solution)/shard_map/ppermute | solution.py:307
  127.1 3.0 collective-permute-start.13
  131.2 11.2 %collective-permute-done.13.refs_8_ = bf16[17,128,128]{2,1,0:T(8,128)(2,1)} collective-permute-done((bf16[17,128,128]{2,1,0:T(8,128)(2,1)}, bf16[17,128,128]{2,1,0:T(8,128)(2,1)}, u32[]{:S(2)}, u32[]{:S(2)}) %collective-permute-start.13) | collective-permute-done | bytes 557088 | tf_op jit(solution)/shard_map/ppermute | solution.py:307
  142.4 3.4 collective-permute-start.17
  150.1 12.6 %collective-permute-done.15.refs_10_ = bf16[17,128,128]{2,1,0:T(8,128)(2,1)} collective-permute-done((bf16[17,128,128]{2,1,0:T(8,128)(2,1)}, bf16[17,128,128]{2,1,0:T(8,128)(2,1)}, u32[]{:S(2)}, u32[]{:S(2)}) %collective-permute-start.15) | collective-permute-done | bytes 557088 | tf_op jit(solution)/shard_map/ppermute | solution.py:307
  162.7 1.7 slice.88
  164.4 11.7 %forward.1 = (bf16[16,128,128]{2,1,0:T(8,128)(2,1)S(1)}, bf16[16,128,128]{2,1,0:T(8,128)(2,1)S(1)}, f32[16,1,128]{2,1,0:T(1,128)S(1)}) custom-call(s32[16,8]{1,0:T(8,128)S(1)} %copy.11.blocks_ref, bf16[16,3,128,128]{3,2,1,0:T(8,128)(2,1)S(1)} %all-to-all-done.qkv_ref), custom_call_target="tpu_custom_call" | custom-call | tf_op jit(solution)/shard_map/forward/pallas_call | solution.py:97
  176.9 5.9 %all-to-all-start.1 = ((bf16[16,128,128]{2,1,0:T(8,128)(2,1)}), bf16[16,128,128]{2,1,0:T(8,128)(2,1)S(1)}, u32[]{:S(2)}, u32[]{:S(2)}) async-start(bf16[16,128,128]{2,1,0:T(8,128)(2,1)} %copy-done.12), calls=%async_computation.1 | async-start | bytes 1048576 | tf_op jit(solution)/shard_map/all_to_all | solution.py:372
  183.5 1.3 collective-permute-start.7
  184.9 2.7 collective-permute-start.8
  188.6 2.8 collective-permute-start.19
  192.2 1.1 collective-permute-start.9
  193.3 1.5 collective-permute-start.16
  195.6 3.9 %collective-permute-done.8 = bf16[8,128,128]{2,1,0:T(8,128)(2,1)S(1)} collective-permute-done((bf16[8,128,128]{2,1,0:T(8,128)(2,1)S(1)}, bf16[8,128,128]{2,1,0:T(8,128)(2,1)S(1)}, u32[]{:S(2)}, u32[]{:S(2)}) %collective-permute-start.8) | collective-permute-done | bytes 262176 | tf_op jit(solution)/shard_map/ppermute | solution.py:307
  200.3 2.4 collective-permute-done.19.refs_16_
  205.1 1.2 pad_maximum_fusion.refs_0_
  206.3 1.3 collective-permute-start.10
  207.6 2.5 collective-permute-start.11
  214.3 16.4 %backward.1 = (bf16[16,3,128,128]{3,2,1,0:T(8,128)(2,1)S(1)}, bf16[16,128,128]{2,1,0:T(8,128)(2,1)S(1)}) custom-call(s32[16,8]{1,0:T(8,128)S(1)} %copy.11.blocks_ref, s32[10]{0:T(128)S(1)} %stack.142.place_ref, bf16[16,3,128,128]{3,2,1,0:T(8,128)(2,1)S(1)} %all-to-all-done.qkv_ref, bf16[16,128,128]{2,1,0:T(8,128)(2,1)S(1)} %copy-done.11, ...), custom_call_target="tpu_custom_call" | custom-call | tf_op jit(solution)/shard_map/backward/pallas_call | solution.py:216
  230.6 1.1 copy-done.1
  235.0 6.3 %all-to-all-start.2 = ((bf16[16,3,128,128]{3,2,1,0:T(8,128)(2,1)}), bf16[16,3,128,128]{3,2,1,0:T(8,128)(2,1)S(1)}, u32[]{:S(2)}, u32[]{:S(2)}) async-start(bf16[16,3,128,128]{3,2,1,0:T(8,128)(2,1)} %copy-done.1), calls=%async_computation.2 | async-start | bytes 3145728 | tf_op jit(solution)/shard_map/all_to_all | solution.py:375
  241.2 1.4 constant_dynamic-update-slice_fusion.12
  242.6 1.4 constant_dynamic-update-slice_fusion.11
  244.0 1.4 constant_dynamic-update-slice_fusion.10
  247.1 2.3 collective-permute-start.30
  249.8 1.4 constant_dynamic-update-slice_fusion.8
  251.2 8.1 %collective-permute-done.29 = bf16[4,128,128]{2,1,0:T(8,128)(2,1)S(1)} collective-permute-done((bf16[4,128,128]{2,1,0:T(8,128)(2,1)S(1)}, bf16[4,128,128]{2,1,0:T(8,128)(2,1)S(1)}, u32[]{:S(2)}, u32[]{:S(2)}) %collective-permute-start.29) | collective-permute-done | bytes 131104 | tf_op jit(solution)/shard_map/ppermute | solution.py:307
  259.3 2.2 collective-permute-done.30
  263.0 10.6 %collective-permute-done.21 = bf16[8,128,128]{2,1,0:T(8,128)(2,1)S(1)} collective-permute-done((bf16[8,128,128]{2,1,0:T(8,128)(2,1)}, bf16[8,128,128]{2,1,0:T(8,128)(2,1)S(1)}, u32[]{:S(2)}, u32[]{:S(2)}) %collective-permute-start.21) | collective-permute-done | bytes 262176 | tf_op jit(solution)/shard_map/ppermute | solution.py:307
  273.7 1.3 collective-permute-start.32
  275.0 2.6 collective-permute-start.33
  277.6 1.1 collective-permute-start.34
  278.7 2.0 pad_maximum_fusion.1.refs_4_
  280.7 1.2 collective-permute-start.12
  282.0 3.8 %collective-permute-start.36 = (bf16[128,128]{1,0:T(8,128)(2,1)S(1)}, bf16[128,128]{1,0:T(8,128)(2,1)S(1)}, u32[]{:S(2)}, u32[]{:S(2)}) collective-permute-start(bf16[128,128]{1,0:T(8,128)(2,1)S(1)} %fusion.6), channel_id=1, source_target_pairs={{0,2},{1,3},{2,0},{3,1},{4,6},{5,7},{6,4},{7,5},{8,10},{9,11},{10,... | collective-permute-start | bytes 98312 | tf_op jit(solution)/shard_map/ppermute | solution.py:307
  285.9 22.0 %collective-permute-done.35 = bf16[128,128]{1,0:T(8,128)(2,1)S(1)} collective-permute-done((bf16[128,128]{1,0:T(8,128)(2,1)S(1)}, bf16[128,128]{1,0:T(8,128)(2,1)S(1)}, u32[]{:S(2)}, u32[]{:S(2)}) %collective-permute-start.35) | collective-permute-done | bytes 32800 | tf_op jit(solution)/shard_map/ppermute | solution.py:307
  307.9 2.7 collective-permute-done.37
  310.6 1.2 collective-permute-start.26
  312.0 1.5 collective-permute-start.39
  313.6 1.2 collective-permute-start.40
  315.0 16.9 %collective-permute-done.25.refs_6_ = bf16[4,8,128,128]{3,2,1,0:T(8,128)(2,1)} collective-permute-done((bf16[4,8,128,128]{3,2,1,0:T(8,128)(2,1)}, bf16[4,8,128,128]{3,2,1,0:T(8,128)(2,1)}, u32[]{:S(2)}, u32[]{:S(2)}) %collective-permute-start.25) | collective-permute-done | bytes 1048608 | tf_op jit(solution)/shard_map/ppermute | solution.py:307
  331.9 21.5 %collective-permute-done.26.refs_7_ = bf16[4,8,128,128]{3,2,1,0:T(8,128)(2,1)} collective-permute-done((bf16[4,8,128,128]{3,2,1,0:T(8,128)(2,1)}, bf16[4,8,128,128]{3,2,1,0:T(8,128)(2,1)}, u32[]{:S(2)}, u32[]{:S(2)}) %collective-permute-start.26) | collective-permute-done | bytes 1048608 | tf_op jit(solution)/shard_map/ppermute | solution.py:307
  353.4 5.3 %project.1 = bf16[128,2048]{1,0:T(8,128)(2,1)} custom-call(s32[16]{0:T(128)S(1)} %stack.127.heads_ref, s32[16]{0:T(128)S(1)} %add.263.cols_ref, bf16[16,128,128]{2,1,0:T(8,128)(2,1)S(1)} %all-to-all-done.1.mine_ref, bf16[4,8,128,128]{3,2,1,0:T(8,128)(2,1)S(1)} %pad_maximum_fusion.refs_0_, bf16[4,8,128,128]{3,2,1,0:T(8,128)(2,1)} %collective-permute-done.10.refs_1_, ...), custom_call_target="tpu_custom_call" | custom-call | tf_op jit(solution)/shard_map/project/pallas_call | solution.py:266
  358.8 2.9 unpack.1
  (113 shorter events, 26.0 us)
Async XLA Ops:
  66.9 63.2 %copy-start.17 = (s32[1,16,8]{1,2,0:T(8,128)S(1)}, s32[1,16,8]{1,2,0:T(8,128)}, u32[]{:S(2)}) copy-start(s32[1,16,8]{1,2,0:T(8,128)} %param.11) | copy-start | bytes 1540
  66.9 97.5 %all-to-all-start = ((bf16[16,3,128,128]{3,2,1,0:T(8,128)(2,1)}), bf16[16,3,128,128]{3,2,1,0:T(8,128)(2,1)S(1)}, u32[]{:S(2)}, u32[]{:S(2)}) async-start(bf16[16,3,128,128]{3,2,1,0:T(8,128)(2,1)} %get-tuple-element.16), calls=%async_computation | async-start | bytes 3145728 | tf_op jit(solution)/shard_map/all_to_all | solution.py:346
  77.0 49.2 %collective-permute-start.1 = (bf16[17,128,128]{2,1,0:T(8,128)(2,1)S(1)}, bf16[17,128,128]{2,1,0:T(8,128)(2,1)S(1)}, u32[]{:S(2)}, u32[]{:S(2)}) collective-permute-start(bf16[17,128,128]{2,1,0:T(8,128)(2,1)S(1)} %copy-done.2), channel_id=1, source_target_pairs={{0,32},{32,64},{64,96},{96,128},{128,160},{160,192},{192,224},{224... | collective-permute-start | bytes 1671176 | tf_op jit(solution)/shard_map/ppermute | solution.py:307
  78.5 48.6 %collective-permute-start.3 = (bf16[17,128,128]{2,1,0:T(8,128)(2,1)S(1)}, bf16[17,128,128]{2,1,0:T(8,128)(2,1)}, u32[]{:S(2)}, u32[]{:S(2)}) collective-permute-start(bf16[17,128,128]{2,1,0:T(8,128)(2,1)S(1)} %copy-done.2), channel_id=1, source_target_pairs={{0,224},{32,0},{64,32},{96,64},{128,96},{160,128},{192,160},{224,1... | collective-permute-start | bytes 1671176 | tf_op jit(solution)/shard_map/ppermute | solution.py:307
  79.8 50.7 %collective-permute-start = (bf16[17,128,128]{2,1,0:T(8,128)(2,1)S(1)}, bf16[17,128,128]{2,1,0:T(8,128)(2,1)}, u32[]{:S(2)}, u32[]{:S(2)}) collective-permute-start(bf16[17,128,128]{2,1,0:T(8,128)(2,1)S(1)} %copy-done.2), channel_id=1, source_target_pairs={{0,16},{16,0},{1,17},{17,1},{2,18},{18,2},{3,19},{19,3},{4,20},{20... | collective-permute-start | bytes 1671176 | tf_op jit(solution)/shard_map/ppermute | solution.py:355
  126.2 38.1 %copy-start.4 = (bf16[17,128,128]{2,1,0:T(8,128)(2,1)}, bf16[17,128,128]{2,1,0:T(8,128)(2,1)S(1)}, u32[]{:S(2)}) copy-start(bf16[17,128,128]{2,1,0:T(8,128)(2,1)S(1)} %collective-permute-done.1.refs_2_) | copy-start | bytes 1671172
  126.2 20.7 %collective-permute-start.5 = (bf16[17,128,128]{2,1,0:T(8,128)(2,1)S(1)}, bf16[17,128,128]{2,1,0:T(8,128)(2,1)}, u32[]{:S(2)}, u32[]{:S(2)}) collective-permute-start(bf16[17,128,128]{2,1,0:T(8,128)(2,1)S(1)} %collective-permute-done.1.refs_2_), channel_id=1, source_target_pairs={{0,32},{32,64},{64,96},{96,128},{128,160},{160,192},{192,224},{224... | collective-permute-start | bytes 1671176 | tf_op jit(solution)/shard_map/ppermute | solution.py:307
  126.2 20.7 %collective-permute-start.2 = (bf16[17,128,128]{2,1,0:T(8,128)(2,1)S(1)}, bf16[17,128,128]{2,1,0:T(8,128)(2,1)}, u32[]{:S(2)}, u32[]{:S(2)}) collective-permute-start(bf16[17,128,128]{2,1,0:T(8,128)(2,1)S(1)} %collective-permute-done.1.refs_2_), channel_id=1, source_target_pairs={{0,16},{16,0},{1,17},{17,1},{2,18},{18,2},{3,19},{19,3},{4,20},{20... | collective-permute-start | bytes 1671176 | tf_op jit(solution)/shard_map/ppermute | solution.py:355
  127.1 15.3 %collective-permute-start.13 = (bf16[17,128,128]{2,1,0:T(8,128)(2,1)}, bf16[17,128,128]{2,1,0:T(8,128)(2,1)}, u32[]{:S(2)}, u32[]{:S(2)}) collective-permute-start(bf16[17,128,128]{2,1,0:T(8,128)(2,1)} %collective-permute-done.3.refs_4_), channel_id=1, source_target_pairs={{0,224},{32,0},{64,32},{96,64},{128,96},{160,128},{192,160},{224,1... | collective-permute-start | bytes 1671176 | tf_op jit(solution)/shard_map/ppermute | solution.py:307
  130.1 18.4 %collective-permute-start.4 = (bf16[17,128,128]{2,1,0:T(8,128)(2,1)}, bf16[17,128,128]{2,1,0:T(8,128)(2,1)S(1)}, u32[]{:S(2)}, u32[]{:S(2)}) collective-permute-start(bf16[17,128,128]{2,1,0:T(8,128)(2,1)} %collective-permute-done.3.refs_4_), channel_id=1, source_target_pairs={{0,16},{16,0},{1,17},{17,1},{2,18},{18,2},{3,19},{19,3},{4,20},{20... | collective-permute-start | bytes 1671176 | tf_op jit(solution)/shard_map/ppermute | solution.py:355
  142.4 45.2 %collective-permute-start.17 = (bf16[17,128,128]{2,1,0:T(8,128)(2,1)}, bf16[17,128,128]{2,1,0:T(8,128)(2,1)}, u32[]{:S(2)}, u32[]{:S(2)}) collective-permute-start(bf16[17,128,128]{2,1,0:T(8,128)(2,1)} %collective-permute-done.13.refs_8_), channel_id=1, source_target_pairs={{0,224},{32,0},{64,32},{96,64},{128,96},{160,128},{192,160},{224,1... | collective-permute-start | bytes 1671176 | tf_op jit(solution)/shard_map/ppermute | solution.py:307
  145.8 46.4 %collective-permute-start.14 = (bf16[17,128,128]{2,1,0:T(8,128)(2,1)}, bf16[17,128,128]{2,1,0:T(8,128)(2,1)}, u32[]{:S(2)}, u32[]{:S(2)}) collective-permute-start(bf16[17,128,128]{2,1,0:T(8,128)(2,1)} %collective-permute-done.13.refs_8_), channel_id=1, source_target_pairs={{0,16},{16,0},{1,17},{17,1},{2,18},{18,2},{3,19},{19,3},{4,20},{20... | collective-permute-start | bytes 1671176 | tf_op jit(solution)/shard_map/ppermute | solution.py:355
  146.9 15.8 %collective-permute-start.15 = (bf16[17,128,128]{2,1,0:T(8,128)(2,1)}, bf16[17,128,128]{2,1,0:T(8,128)(2,1)}, u32[]{:S(2)}, u32[]{:S(2)}) collective-permute-start(bf16[17,128,128]{2,1,0:T(8,128)(2,1)} %collective-permute-done.5.refs_6_), channel_id=1, source_target_pairs={{0,32},{32,64},{64,96},{96,128},{128,160},{160,192},{192,224},{224... | collective-permute-start | bytes 1671176 | tf_op jit(solution)/shard_map/ppermute | solution.py:307
  146.9 35.8 %collective-permute-start.6 = (bf16[17,128,128]{2,1,0:T(8,128)(2,1)}, bf16[17,128,128]{2,1,0:T(8,128)(2,1)}, u32[]{:S(2)}, u32[]{:S(2)}) collective-permute-start(bf16[17,128,128]{2,1,0:T(8,128)(2,1)} %collective-permute-done.5.refs_6_), channel_id=1, source_target_pairs={{0,16},{16,0},{1,17},{17,1},{2,18},{18,2},{3,19},{19,3},{4,20},{20... | collective-permute-start | bytes 1671176 | tf_op jit(solution)/shard_map/ppermute | solution.py:355
  164.4 28.9 %collective-permute-start.27 = (bf16[8,128,128]{2,1,0:T(8,128)(2,1)}, bf16[8,128,128]{2,1,0:T(8,128)(2,1)}, u32[]{:S(2)}, u32[]{:S(2)}) collective-permute-start(bf16[8,128,128]{2,1,0:T(8,128)(2,1)} %slice.88), channel_id=1, source_target_pairs={{0,32},{32,64},{64,96},{96,128},{128,160},{160,192},{192,224},{224... | collective-permute-start | bytes 786440 | tf_op jit(solution)/shard_map/ppermute | solution.py:307
  176.9 27.5 %copy-start.10 = (bf16[16,128,128]{2,1,0:T(8,128)(2,1)}, bf16[16,128,128]{2,1,0:T(8,128)(2,1)S(1)}, u32[]{:S(2)}) copy-start(bf16[16,128,128]{2,1,0:T(8,128)(2,1)S(1)} %get-tuple-element.19.attn_t_ref) | copy-start | bytes 1572868
  176.9 58.1 %all-to-all-start.1 = ((bf16[16,128,128]{2,1,0:T(8,128)(2,1)}), bf16[16,128,128]{2,1,0:T(8,128)(2,1)S(1)}, u32[]{:S(2)}, u32[]{:S(2)}) async-start(bf16[16,128,128]{2,1,0:T(8,128)(2,1)} %copy-done.12), calls=%async_computation.1 | async-start | bytes 1048576 | tf_op jit(solution)/shard_map/all_to_all | solution.py:372
  183.5 20.8 %copy-start.16 = (bf16[8,128,128]{2,1,0:T(8,128)(2,1)}, bf16[8,128,128]{2,1,0:T(8,128)(2,1)S(1)}, u32[]{:S(2)}) copy-start(bf16[8,128,128]{2,1,0:T(8,128)(2,1)S(1)} %constant_dynamic-update-slice_fusion) | copy-start | bytes 786436
  183.5 11.2 %collective-permute-start.7 = (bf16[8,128,128]{2,1,0:T(8,128)(2,1)S(1)}, bf16[8,128,128]{2,1,0:T(8,128)(2,1)}, u32[]{:S(2)}, u32[]{:S(2)}) collective-permute-start(bf16[8,128,128]{2,1,0:T(8,128)(2,1)S(1)} %constant_dynamic-update-slice_fusion), channel_id=1, source_target_pairs={{0,1},{1,2},{2,3},{3,0},{4,5},{5,6},{6,7},{7,4},{8,9},{9,10},{10,1... | collective-permute-start | bytes 786440 | tf_op jit(solution)/shard_map/ppermute | solution.py:307
  184.9 14.5 %collective-permute-start.8 = (bf16[8,128,128]{2,1,0:T(8,128)(2,1)S(1)}, bf16[8,128,128]{2,1,0:T(8,128)(2,1)S(1)}, u32[]{:S(2)}, u32[]{:S(2)}) collective-permute-start(bf16[8,128,128]{2,1,0:T(8,128)(2,1)S(1)} %constant_dynamic-update-slice_fusion), channel_id=1, source_target_pairs={{0,2},{1,3},{2,0},{3,1},{4,6},{5,7},{6,4},{7,5},{8,10},{9,11},{10,... | collective-permute-start | bytes 786440 | tf_op jit(solution)/shard_map/ppermute | solution.py:307
  188.6 14.1 %collective-permute-start.19 = (bf16[9,128,128]{2,1,0:T(8,128)(2,1)S(1)}, bf16[9,128,128]{2,1,0:T(8,128)(2,1)S(1)}, u32[]{:S(2)}, u32[]{:S(2)}) collective-permute-start(bf16[9,128,128]{2,1,0:T(8,128)(2,1)S(1)} %slice.85), channel_id=1, source_target_pairs={{0,224},{32,0},{64,32},{96,64},{128,96},{160,128},{192,160},{224,1... | collective-permute-start | bytes 884744 | tf_op jit(solution)/shard_map/ppermute | solution.py:307
  192.2 12.2 %collective-permute-start.9 = (bf16[8,128,128]{2,1,0:T(8,128)(2,1)S(1)}, bf16[8,128,128]{2,1,0:T(8,128)(2,1)S(1)}, u32[]{:S(2)}, u32[]{:S(2)}) collective-permute-start(bf16[8,128,128]{2,1,0:T(8,128)(2,1)S(1)} %constant_dynamic-update-slice_fusion), channel_id=1, source_target_pairs={{0,3},{1,0},{2,1},{3,2},{4,7},{5,4},{6,5},{7,6},{8,11},{9,8},{10,9... | collective-permute-start | bytes 786440 | tf_op jit(solution)/shard_map/ppermute | solution.py:307
  193.3 16.8 %collective-permute-start.16 = (bf16[17,128,128]{2,1,0:T(8,128)(2,1)}, bf16[17,128,128]{2,1,0:T(8,128)(2,1)S(1)}, u32[]{:S(2)}, u32[]{:S(2)}) collective-permute-start(bf16[17,128,128]{2,1,0:T(8,128)(2,1)} %collective-permute-done.15.refs_10_), channel_id=1, source_target_pairs={{0,16},{16,0},{1,17},{17,1},{2,18},{18,2},{3,19},{19,3},{4,20},{20... | collective-permute-start | bytes 1671176 | tf_op jit(solution)/shard_map/ppermute | solution.py:355
  194.8 15.3 %collective-permute-start.18 = (bf16[17,128,128]{2,1,0:T(8,128)(2,1)}, bf16[17,128,128]{2,1,0:T(8,128)(2,1)S(1)}, u32[]{:S(2)}, u32[]{:S(2)}) collective-permute-start(bf16[17,128,128]{2,1,0:T(8,128)(2,1)} %collective-permute-done.17.refs_12_), channel_id=1, source_target_pairs={{0,16},{16,0},{1,17},{17,1},{2,18},{18,2},{3,19},{19,3},{4,20},{20... | collective-permute-start | bytes 1671176 | tf_op jit(solution)/shard_map/ppermute | solution.py:355
  199.5 8.1 %collective-permute-start.28 = (bf16[8,128,128]{2,1,0:T(8,128)(2,1)}, bf16[8,128,128]{2,1,0:T(8,128)(2,1)S(1)}, u32[]{:S(2)}, u32[]{:S(2)}) collective-permute-start(bf16[8,128,128]{2,1,0:T(8,128)(2,1)} %collective-permute-done.27.refs_14_), channel_id=1, source_target_pairs={{0,16},{16,0},{1,17},{17,1},{2,18},{18,2},{3,19},{19,3},{4,20},{20... | collective-permute-start | bytes 786440 | tf_op jit(solution)/shard_map/ppermute | solution.py:355
  202.7 7.3 %collective-permute-start.20 = (bf16[9,128,128]{2,1,0:T(8,128)(2,1)S(1)}, bf16[9,128,128]{2,1,0:T(8,128)(2,1)S(1)}, u32[]{:S(2)}, u32[]{:S(2)}) collective-permute-start(bf16[9,128,128]{2,1,0:T(8,128)(2,1)S(1)} %collective-permute-done.19.refs_16_), channel_id=1, source_target_pairs={{0,16},{16,0},{1,17},{17,1},{2,18},{18,2},{3,19},{19,3},{4,20},{20... | collective-permute-start | bytes 884744 | tf_op jit(solution)/shard_map/ppermute | solution.py:355
  206.3 75.8 %collective-permute-start.10 = (bf16[4,8,128,128]{3,2,1,0:T(8,128)(2,1)S(1)}, bf16[4,8,128,128]{3,2,1,0:T(8,128)(2,1)}, u32[]{:S(2)}, u32[]{:S(2)}) collective-permute-start(bf16[4,8,128,128]{3,2,1,0:T(8,128)(2,1)S(1)} %pad_maximum_fusion.refs_0_), channel_id=1, source_target_pairs={{0,4},{4,8},{8,12},{12,0},{1,5},{5,9},{9,13},{13,1},{2,6},{6,10},{... | collective-permute-start | bytes 3145736 | tf_op jit(solution)/shard_map/ppermute | solution.py:307
  207.6 104.3 %collective-permute-start.11 = (bf16[4,8,128,128]{3,2,1,0:T(8,128)(2,1)S(1)}, bf16[4,8,128,128]{3,2,1,0:T(8,128)(2,1)}, u32[]{:S(2)}, u32[]{:S(2)}) collective-permute-start(bf16[4,8,128,128]{3,2,1,0:T(8,128)(2,1)S(1)} %pad_maximum_fusion.refs_0_), channel_id=1, source_target_pairs={{0,8},{4,12},{8,0},{12,4},{1,9},{5,13},{9,1},{13,5},{2,10},{6,14},... | collective-permute-start | bytes 3145736 | tf_op jit(solution)/shard_map/ppermute | solution.py:307
  235.0 123.8 %all-to-all-start.2 = ((bf16[16,3,128,128]{3,2,1,0:T(8,128)(2,1)}), bf16[16,3,128,128]{3,2,1,0:T(8,128)(2,1)S(1)}, u32[]{:S(2)}, u32[]{:S(2)}) async-start(bf16[16,3,128,128]{3,2,1,0:T(8,128)(2,1)} %copy-done.1), calls=%async_computation.2 | async-start | bytes 3145728 | tf_op jit(solution)/shard_map/all_to_all | solution.py:375
  247.0 12.2 %collective-permute-start.29 = (bf16[4,128,128]{2,1,0:T(8,128)(2,1)S(1)}, bf16[4,128,128]{2,1,0:T(8,128)(2,1)S(1)}, u32[]{:S(2)}, u32[]{:S(2)}) collective-permute-start(bf16[4,128,128]{2,1,0:T(8,128)(2,1)S(1)} %get-tuple-element.27), channel_id=1, source_target_pairs={{0,4},{4,8},{8,12},{12,0},{1,5},{5,9},{9,13},{13,1},{2,6},{6,10},{... | collective-permute-start | bytes 393224 | tf_op jit(solution)/shard_map/ppermute | solution.py:307
  247.1 14.3 %collective-permute-start.30 = (bf16[4,128,128]{2,1,0:T(8,128)(2,1)S(1)}, bf16[4,128,128]{2,1,0:T(8,128)(2,1)S(1)}, u32[]{:S(2)}, u32[]{:S(2)}) collective-permute-start(bf16[4,128,128]{2,1,0:T(8,128)(2,1)S(1)} %get-tuple-element.29), channel_id=1, source_target_pairs={{0,8},{4,12},{8,0},{12,4},{1,9},{5,13},{9,1},{13,5},{2,10},{6,14},... | collective-permute-start | bytes 393224 | tf_op jit(solution)/shard_map/ppermute | solution.py:307
  249.5 12.5 %collective-permute-start.31 = (bf16[4,128,128]{2,1,0:T(8,128)(2,1)S(1)}, bf16[4,128,128]{2,1,0:T(8,128)(2,1)S(1)}, u32[]{:S(2)}, u32[]{:S(2)}) collective-permute-start(bf16[4,128,128]{2,1,0:T(8,128)(2,1)S(1)} %get-tuple-element.28), channel_id=1, source_target_pairs={{0,12},{4,0},{8,4},{12,8},{1,13},{5,1},{9,5},{13,9},{2,14},{6,2},{... | collective-permute-start | bytes 393224 | tf_op jit(solution)/shard_map/ppermute | solution.py:307
  259.3 14.4 %collective-permute-start.21 = (bf16[8,128,128]{2,1,0:T(8,128)(2,1)}, bf16[8,128,128]{2,1,0:T(8,128)(2,1)S(1)}, u32[]{:S(2)}, u32[]{:S(2)}) collective-permute-start(bf16[8,128,128]{2,1,0:T(8,128)(2,1)} %constant_dynamic-update-slice_fusion.8), channel_id=1, source_target_pairs={{0,4},{4,8},{8,12},{12,0},{1,5},{5,9},{9,13},{13,1},{2,6},{6,10},{... | collective-permute-start | bytes 786440 | tf_op jit(solution)/shard_map/ppermute | solution.py:307
  261.5 13.5 %collective-permute-start.22 = (bf16[8,128,128]{2,1,0:T(8,128)(2,1)}, bf16[8,128,128]{2,1,0:T(8,128)(2,1)S(1)}, u32[]{:S(2)}, u32[]{:S(2)}) collective-permute-start(bf16[8,128,128]{2,1,0:T(8,128)(2,1)} %constant_dynamic-update-slice_fusion.8), channel_id=1, source_target_pairs={{0,8},{4,12},{8,0},{12,4},{1,9},{5,13},{9,1},{13,5},{2,10},{6,14},... | collective-permute-start | bytes 786440 | tf_op jit(solution)/shard_map/ppermute | solution.py:307
  262.0 15.6 %collective-permute-start.23 = (bf16[8,128,128]{2,1,0:T(8,128)(2,1)}, bf16[8,128,128]{2,1,0:T(8,128)(2,1)S(1)}, u32[]{:S(2)}, u32[]{:S(2)}) collective-permute-start(bf16[8,128,128]{2,1,0:T(8,128)(2,1)} %constant_dynamic-update-slice_fusion.8), channel_id=1, source_target_pairs={{0,12},{4,0},{8,4},{12,8},{1,13},{5,1},{9,5},{13,9},{2,14},{6,2},{... | collective-permute-start | bytes 786440 | tf_op jit(solution)/shard_map/ppermute | solution.py:307
  273.7 7.0 %collective-permute-start.32 = (bf16[128,128]{1,0:T(8,128)(2,1)S(1)}, bf16[128,128]{1,0:T(8,128)(2,1)S(1)}, u32[]{:S(2)}, u32[]{:S(2)}) collective-permute-start(bf16[128,128]{1,0:T(8,128)(2,1)S(1)} %get-tuple-element.30), channel_id=1, source_target_pairs={{0,1},{1,2},{2,3},{3,0},{4,5},{5,6},{6,7},{7,4},{8,9},{9,10},{10,1... | collective-permute-start | bytes 98312 | tf_op jit(solution)/shard_map/ppermute | solution.py:307
  275.0 6.9 %collective-permute-start.33 = (bf16[128,128]{1,0:T(8,128)(2,1)S(1)}, bf16[128,128]{1,0:T(8,128)(2,1)S(1)}, u32[]{:S(2)}, u32[]{:S(2)}) collective-permute-start(bf16[128,128]{1,0:T(8,128)(2,1)S(1)} %get-tuple-element.32), channel_id=1, source_target_pairs={{0,2},{1,3},{2,0},{3,1},{4,6},{5,7},{6,4},{7,5},{8,10},{9,11},{10,... | collective-permute-start | bytes 98312 | tf_op jit(solution)/shard_map/ppermute | solution.py:307
  277.6 4.3 %collective-permute-start.34 = (bf16[128,128]{1,0:T(8,128)(2,1)S(1)}, bf16[128,128]{1,0:T(8,128)(2,1)S(1)}, u32[]{:S(2)}, u32[]{:S(2)}) collective-permute-start(bf16[128,128]{1,0:T(8,128)(2,1)S(1)} %get-tuple-element.31), channel_id=1, source_target_pairs={{0,3},{1,0},{2,1},{3,2},{4,7},{5,4},{6,5},{7,6},{8,11},{9,8},{10,9... | collective-permute-start | bytes 98312 | tf_op jit(solution)/shard_map/ppermute | solution.py:307
  280.7 31.3 %collective-permute-start.12 = (bf16[4,8,128,128]{3,2,1,0:T(8,128)(2,1)S(1)}, bf16[4,8,128,128]{3,2,1,0:T(8,128)(2,1)}, u32[]{:S(2)}, u32[]{:S(2)}) collective-permute-start(bf16[4,8,128,128]{3,2,1,0:T(8,128)(2,1)S(1)} %pad_maximum_fusion.refs_0_), channel_id=1, source_target_pairs={{0,12},{4,0},{8,4},{12,8},{1,13},{5,1},{9,5},{13,9},{2,14},{6,2},{... | collective-permute-start | bytes 3145736 | tf_op jit(solution)/shard_map/ppermute | solution.py:307
  281.9 31.7 %collective-permute-start.24 = (bf16[4,8,128,128]{3,2,1,0:T(8,128)(2,1)}, bf16[4,8,128,128]{3,2,1,0:T(8,128)(2,1)}, u32[]{:S(2)}, u32[]{:S(2)}) collective-permute-start(bf16[4,8,128,128]{3,2,1,0:T(8,128)(2,1)} %pad_maximum_fusion.1.refs_4_), channel_id=1, source_target_pairs={{0,1},{1,2},{2,3},{3,0},{4,5},{5,6},{6,7},{7,4},{8,9},{9,10},{10,1... | collective-permute-start | bytes 3145736 | tf_op jit(solution)/shard_map/ppermute | solution.py:307
  281.9 25.9 %collective-permute-start.35 = (bf16[128,128]{1,0:T(8,128)(2,1)S(1)}, bf16[128,128]{1,0:T(8,128)(2,1)S(1)}, u32[]{:S(2)}, u32[]{:S(2)}) collective-permute-start(bf16[128,128]{1,0:T(8,128)(2,1)S(1)} %fusion.6), channel_id=1, source_target_pairs={{0,1},{1,2},{2,3},{3,0},{4,5},{5,6},{6,7},{7,4},{8,9},{9,10},{10,1... | collective-permute-start | bytes 98312 | tf_op jit(solution)/shard_map/ppermute | solution.py:307
  282.0 25.8 %collective-permute-start.36 = (bf16[128,128]{1,0:T(8,128)(2,1)S(1)}, bf16[128,128]{1,0:T(8,128)(2,1)S(1)}, u32[]{:S(2)}, u32[]{:S(2)}) collective-permute-start(bf16[128,128]{1,0:T(8,128)(2,1)S(1)} %fusion.6), channel_id=1, source_target_pairs={{0,2},{1,3},{2,0},{3,1},{4,6},{5,7},{6,4},{7,5},{8,10},{9,11},{10,... | collective-permute-start | bytes 98312 | tf_op jit(solution)/shard_map/ppermute | solution.py:307
  307.9 2.8 collective-permute-start.37
  307.9 24.1 %collective-permute-start.25 = (bf16[4,8,128,128]{3,2,1,0:T(8,128)(2,1)}, bf16[4,8,128,128]{3,2,1,0:T(8,128)(2,1)}, u32[]{:S(2)}, u32[]{:S(2)}) collective-permute-start(bf16[4,8,128,128]{3,2,1,0:T(8,128)(2,1)} %pad_maximum_fusion.1.refs_4_), channel_id=1, source_target_pairs={{0,2},{1,3},{2,0},{3,1},{4,6},{5,7},{6,4},{7,5},{8,10},{9,11},{10,... | collective-permute-start | bytes 3145736 | tf_op jit(solution)/shard_map/ppermute | solution.py:307
  310.6 42.8 %collective-permute-start.26 = (bf16[4,8,128,128]{3,2,1,0:T(8,128)(2,1)}, bf16[4,8,128,128]{3,2,1,0:T(8,128)(2,1)}, u32[]{:S(2)}, u32[]{:S(2)}) collective-permute-start(bf16[4,8,128,128]{3,2,1,0:T(8,128)(2,1)} %pad_maximum_fusion.1.refs_4_), channel_id=1, source_target_pairs={{0,3},{1,0},{2,1},{3,2},{4,7},{5,4},{6,5},{7,6},{8,11},{9,8},{10,9... | collective-permute-start | bytes 3145736 | tf_op jit(solution)/shard_map/ppermute | solution.py:307
  311.9 46.8 %collective-permute-start.38 = (bf16[4,128,128]{2,1,0:T(8,128)(2,1)S(1)}, bf16[4,128,128]{2,1,0:T(8,128)(2,1)S(1)}, u32[]{:S(2)}, u32[]{:S(2)}) collective-permute-start(bf16[4,128,128]{2,1,0:T(8,128)(2,1)S(1)} %pad_maximum_fusion.2.refs_0_), channel_id=1, source_target_pairs={{0,4},{4,8},{8,12},{12,0},{1,5},{5,9},{9,13},{13,1},{2,6},{6,10},{... | collective-permute-start | bytes 393224 | tf_op jit(solution)/shard_map/ppermute | solution.py:307
  312.0 46.7 %collective-permute-start.39 = (bf16[4,128,128]{2,1,0:T(8,128)(2,1)S(1)}, bf16[4,128,128]{2,1,0:T(8,128)(2,1)S(1)}, u32[]{:S(2)}, u32[]{:S(2)}) collective-permute-start(bf16[4,128,128]{2,1,0:T(8,128)(2,1)S(1)} %pad_maximum_fusion.2.refs_0_), channel_id=1, source_target_pairs={{0,8},{4,12},{8,0},{12,4},{1,9},{5,13},{9,1},{13,5},{2,10},{6,14},... | collective-permute-start | bytes 393224 | tf_op jit(solution)/shard_map/ppermute | solution.py:307
  313.6 45.2 %collective-permute-start.40 = (bf16[4,128,128]{2,1,0:T(8,128)(2,1)S(1)}, bf16[4,128,128]{2,1,0:T(8,128)(2,1)}, u32[]{:S(2)}, u32[]{:S(2)}) collective-permute-start(bf16[4,128,128]{2,1,0:T(8,128)(2,1)S(1)} %pad_maximum_fusion.2.refs_0_), channel_id=1, source_target_pairs={{0,12},{4,0},{8,4},{12,8},{1,13},{5,1},{9,5},{13,9},{2,14},{6,2},{... | collective-permute-start | bytes 393224 | tf_op jit(solution)/shard_map/ppermute | solution.py:307
  (14 other events, 26.0 us)

commit v2 on v1

v2 whole, which is shorter than its diff:
```python
import functools
import math

import jax
import jax.numpy as jnp
from jax import lax
from jax.experimental import pallas as pl
from jax.experimental.pallas import tpu as pltpu
from jax.sharding import Mesh
from jax.sharding import PartitionSpec as P

HEAD_DIM = 128
BLOCK = 128
INV_ROOT = 1.0 / math.sqrt(HEAD_DIM)
LOG2E = 1.0 / math.log(2.0)
BF16 = jnp.bfloat16
F32 = jnp.float32
VM = pl.BlockSpec(memory_space=pltpu.VMEM)
SM = pl.BlockSpec(memory_space=pltpu.SMEM)
HBM = pl.BlockSpec(memory_space=pltpu.HBM)
MIB = 1024 * 1024


def in_hbm(value):
    return pltpu.with_memory_space_constraint(value, pltpu.HBM)


def like(*shape, dtype=BF16):
    return jax.ShapeDtypeStruct(shape, dtype)


def pack_kernel(
    place_ref, q_ref, k_ref, v_ref, g_ref, w_ref, qkv_ref, gw_ref, held, qkv_held, gw_held, sem
):
    count = qkv_ref.shape[0]
    cut = pl.ds(pl.multiple_of(place_ref[0] * BLOCK, BLOCK), BLOCK)
    loads = [
        pltpu.make_async_copy(source, held.at[n], sem.at[n])
        for n, source in enumerate((g_ref, q_ref, k_ref, v_ref))
    ]
    loads.append(pltpu.make_async_copy(w_ref.at[:, cut], gw_held.at[count], sem.at[4]))
    for copy in loads:
        copy.start()
    loads[0].wait()
    loads[4].wait()
    for j in range(count):
        gw_held[j] = held[0, :, j * BLOCK : (j + 1) * BLOCK]
    gw_out = pltpu.make_async_copy(gw_held, gw_ref, sem.at[5])
    gw_out.start()
    for n in range(3):
        loads[n + 1].wait()
        for j in range(count):
            qkv_held[j, n] = held[n + 1, :, j * BLOCK : (j + 1) * BLOCK]
    qkv_out = pltpu.make_async_copy(qkv_held, qkv_ref, sem.at[6])
    qkv_out.start()
    gw_out.wait()
    qkv_out.wait()


def pack(place, q, k, v, g, w):
    count = q.shape[1] // BLOCK
    return pl.pallas_call(
        pack_kernel,
        out_shape=(
            pltpu.HBM((count, 3, BLOCK, BLOCK), BF16),
            pltpu.HBM((count + 1, BLOCK, BLOCK), BF16),
        ),
        in_specs=[SM] + [HBM] * 5,
        out_specs=(HBM, HBM),
        scratch_shapes=[
            pltpu.VMEM((4,) + q.shape, BF16),
            pltpu.VMEM((count, 3, BLOCK, BLOCK), BF16),
            pltpu.VMEM((count + 1, BLOCK, BLOCK), BF16),
            pltpu.SemaphoreType.DMA((7,)),
        ],
        compiler_params=pltpu.CompilerParams(vmem_limit_bytes=24 * MIB),
        name="pack",
    )(place, *(in_hbm(value) for value in (q, k, v, g, w)))


def rows_of(c):
    return pl.ds(pl.multiple_of(c * BLOCK, BLOCK), BLOCK)


def forward_kernel(blocks_ref, qkv_ref, attn_ref, attn_t_ref, lse_ref, vt_ref):
    block_count, slot_count = blocks_ref.shape

    def prepare(c, carry):
        vt_ref[c] = qkv_ref[c, 2].T
        return carry

    lax.fori_loop(0, block_count, prepare, 0, unroll=4)

    def one(b):
        owners = [blocks_ref[b, s] for s in range(slot_count)]
        keys = jnp.concatenate([qkv_ref[c, 1] for c in owners], axis=0)
        scores = jnp.dot(keys, qkv_ref[b, 0].T, preferred_element_type=F32)
        top = jnp.max(scores, axis=0, keepdims=True)
        raised = jnp.exp2((scores - top) * (INV_ROOT * LOG2E))
        total = jnp.sum(raised, axis=0, keepdims=True)
        prob = (raised * (1.0 / total)).astype(BF16)
        v_t = jnp.concatenate([vt_ref[c] for c in owners], axis=1)
        attn_t = jnp.dot(v_t, prob, preferred_element_type=F32).astype(BF16)
        attn_t_ref[b] = attn_t
        attn_ref[b] = attn_t.T
        lse_ref[b] = top * (INV_ROOT * LOG2E) + jnp.log2(total)

    def step(i, carry):
        one(2 * i)
        one(2 * i + 1)
        return carry

    lax.fori_loop(0, block_count // 2, step, 0)


def forward(blocks, qkv):
    count = qkv.shape[0]
    return pl.pallas_call(
        forward_kernel,
        out_shape=(
            like(count, BLOCK, HEAD_DIM),
            like(count, HEAD_DIM, BLOCK),
            like(count, 1, BLOCK, dtype=F32),
        ),
        in_specs=[SM, VM],
        out_specs=(VM, VM, VM),
        scratch_shapes=[pltpu.VMEM((count, HEAD_DIM, BLOCK), BF16)],
        compiler_params=pltpu.CompilerParams(vmem_limit_bytes=24 * MIB),
        name="forward",
    )(blocks, qkv)


def loads_of(parts, g_refs, g_buf, sem):
    found = {}
    for n, (pair, low, high) in enumerate(parts):
        copy = pltpu.make_async_copy(
            g_refs[n].at[pl.ds(0, high - low)], g_buf.at[pair, pl.ds(low, high - low)], sem.at[n]
        )
        copy.start()
        found.setdefault(pair, []).append(copy)
    return found


def side_by_side(g_buf, pair):
    return jnp.concatenate([g_buf[pair, j] for j in range(g_buf.shape[1])], axis=1)


def attn_grad_kernel(parts, mine_ref, theirs_ref, *refs):
    g_refs = refs[: len(parts)]
    d_mine_ref, d_theirs_ref, g_buf, wt_ref, sem = refs[len(parts) :]
    loads = loads_of(parts, g_refs, g_buf, sem)
    wt_ref[:, :HEAD_DIM] = mine_ref[...].T
    wt_ref[:, HEAD_DIM:] = theirs_ref[...].T
    for pair, copies in loads.items():
        for copy in copies:
            copy.wait()
        found = jnp.dot(
            side_by_side(g_buf, pair), wt_ref[...], preferred_element_type=F32
        ).astype(BF16)
        d_mine_ref[pair] = found[:, :HEAD_DIM]
        d_theirs_ref[pair] = found[:, HEAD_DIM:]


def shard_scratch(parts, chunks):
    pairs = 1 + max(pair for pair, _, _ in parts)
    return [pltpu.VMEM((pairs, chunks, BLOCK, BLOCK), BF16)], [pltpu.SemaphoreType.DMA((len(parts),))]


def attn_grad(parts, mine, theirs, shards):
    buf, sem = shard_scratch(parts, mine.shape[1] // BLOCK)
    pairs = buf[0].shape[0]
    return pl.pallas_call(
        functools.partial(attn_grad_kernel, parts),
        out_shape=(like(pairs, BLOCK, HEAD_DIM),) * 2,
        in_specs=[VM, VM] + [HBM] * len(shards),
        out_specs=(VM, VM),
        scratch_shapes=buf + [pltpu.VMEM((mine.shape[1], 2 * HEAD_DIM), BF16)] + sem,
        compiler_params=pltpu.CompilerParams(vmem_limit_bytes=24 * MIB),
        name="attn_grad",
    )(mine, theirs, *(in_hbm(shard) for shard in shards))


def weight_grad_kernel(parts, place_ref, attn_ref, other_ref, *refs):
    g_refs = refs[: len(parts)]
    mine_ref, theirs_ref, g_buf, acc_ref, sem = refs[len(parts) :]
    loads = loads_of(parts, g_refs, g_buf, sem)
    pairs = list(loads)
    chips = len(pairs)
    for step in range(0, chips, 2):
        two = pairs[step : step + 2]
        left = []
        for pair in two:
            for copy in loads[pair]:
                copy.wait()
            chip = lax.rem(place_ref[0] + place_ref[2 + pair], chips)
            left.append(
                jnp.concatenate([attn_ref[2 * chip + place_ref[1]], other_ref[chip]], axis=0)
            )
        found = jnp.dot(
            jnp.concatenate(left, axis=1),
            jnp.concatenate([side_by_side(g_buf, pair) for pair in two], axis=0),
            preferred_element_type=F32,
        )
        if step:
            acc_ref[...] += found
        else:
            acc_ref[...] = found
    for j in range(mine_ref.shape[0]):
        cols = slice(j * BLOCK, (j + 1) * BLOCK)
        mine_ref[j] = acc_ref[:HEAD_DIM, cols].astype(BF16)
        theirs_ref[j] = acc_ref[HEAD_DIM:, cols].astype(BF16)


def weight_grad(parts, place, attn_t, other_t, chunks, shards):
    buf, sem = shard_scratch(parts, chunks)
    return pl.pallas_call(
        functools.partial(weight_grad_kernel, parts),
        out_shape=(like(chunks, HEAD_DIM, BLOCK),) * 2,
        in_specs=[SM, VM, VM] + [HBM] * len(shards),
        out_specs=(VM, VM),
        scratch_shapes=buf + [pltpu.VMEM((2 * HEAD_DIM, chunks * BLOCK), F32)] + sem,
        compiler_params=pltpu.CompilerParams(vmem_limit_bytes=24 * MIB),
        name="weight_grad",
    )(place, attn_t, other_t, *(in_hbm(shard) for shard in shards))


def backward_kernel(
    blocks_ref, place_ref, qkv_ref, attn_t_ref, lse_ref, early_ref, theirs_early_ref, late_ref,
    theirs_late_ref, out_ref, kv_ref, kt_ref, acc_ref, mine_ref, theirs_ref,
):
    block_count, slot_count = blocks_ref.shape
    half = block_count // 2
    zero = jnp.zeros((BLOCK, HEAD_DIM), BF16)

    def prepare(c, carry):
        k_one, v_one = qkv_ref[c, 1], qkv_ref[c, 2]
        kv_ref[rows_of(c), :] = jnp.concatenate([k_one, v_one], axis=1)
        kt_ref[c] = k_one.T
        acc_ref[rows_of(c), :] = jnp.zeros((BLOCK, 2 * HEAD_DIM), F32)
        return carry

    lax.fori_loop(0, block_count, prepare, 0, unroll=2)
    first = early_ref.shape[0]
    mine_ref[:first] = early_ref[...]
    mine_ref[first:] = late_ref[...]
    theirs_ref[:first] = theirs_early_ref[...]
    theirs_ref[first:] = theirs_late_ref[...]

    def one(b, d_one):
        q_one = qkv_ref[b, 0]
        q_t, d_t = q_one.T, d_one.T
        owners = [blocks_ref[b, s] for s in range(slot_count)]
        right = jnp.concatenate(
            [jnp.concatenate([q_t, zero], axis=1), jnp.concatenate([zero, d_t], axis=1)], axis=0
        )
        kv = jnp.concatenate([kv_ref[rows_of(c), :] for c in owners], axis=0)
        both = jnp.dot(kv, right, preferred_element_type=F32)
        scores, prob_grad = both[:, :BLOCK], both[:, BLOCK:]
        prob = jnp.exp2(scores * (INV_ROOT * LOG2E) - lse_ref[b])
        row_dot = jnp.sum(attn_t_ref[b].astype(F32) * d_t.astype(F32), axis=0, keepdims=True)
        score_grad = (prob * (prob_grad - row_dot) * INV_ROOT).astype(BF16)
        k_t = jnp.concatenate([kt_ref[c] for c in owners], axis=1)
        dq_t = jnp.dot(k_t, score_grad, preferred_element_type=F32)
        out_ref[b, 0] = dq_t.astype(BF16).T
        back = jnp.concatenate(
            [jnp.concatenate([q_one, zero], axis=1), jnp.concatenate([zero, d_one], axis=1)], axis=0
        )
        return owners, jnp.dot(
            jnp.concatenate([score_grad, prob.astype(BF16)], axis=1),
            back,
            preferred_element_type=F32,
        )

    def step(i, carry):
        chip = lax.rem(place_ref[0] + place_ref[2 + i], half)
        results = [
            one(2 * chip + place_ref[1], mine_ref[i]),
            one(2 * chip + 1 - place_ref[1], theirs_ref[i]),
        ]
        for owners, found in results:
            for s, c in enumerate(owners):
                acc_ref[rows_of(c), :] += found[s * BLOCK : (s + 1) * BLOCK, :]
        return carry

    lax.fori_loop(0, half, step, 0)

    def finish(c, carry):
        out_ref[c, 1] = acc_ref[rows_of(c), :HEAD_DIM].astype(BF16)
        out_ref[c, 2] = acc_ref[rows_of(c), HEAD_DIM:].astype(BF16)
        return carry

    lax.fori_loop(0, block_count, finish, 0, unroll=2)


def backward(blocks, place, qkv, attn_t, lse, *attn_grads):
    count = qkv.shape[0]
    return pl.pallas_call(
        backward_kernel,
        out_shape=like(count, 3, BLOCK, HEAD_DIM),
        in_specs=[SM, SM] + [VM] * (3 + len(attn_grads)),
        out_specs=VM,
        scratch_shapes=[
            pltpu.VMEM((count * BLOCK, 2 * HEAD_DIM), BF16),
            pltpu.VMEM((count, HEAD_DIM, BLOCK), BF16),
            pltpu.VMEM((count * BLOCK, 2 * HEAD_DIM), F32),
            pltpu.VMEM((count // 2, BLOCK, HEAD_DIM), BF16),
            pltpu.VMEM((count // 2, BLOCK, HEAD_DIM), BF16),
        ],
        compiler_params=pltpu.CompilerParams(vmem_limit_bytes=24 * MIB),
        name="backward",
    )(blocks, place, qkv, attn_t, lse, *attn_grads)


def collect_kernel(spots, *refs):
    w_refs, out_ref, sem = refs[: len(spots)], refs[-2], refs[-1]
    copies = [
        pltpu.make_async_copy(w_ref.at[spot], out_ref.at[n], sem.at[n])
        for n, (w_ref, spot) in enumerate(zip(w_refs, spots))
    ]
    for copy in copies:
        copy.start()
    for copy in copies:
        copy.wait()


def collect(spots, arrays):
    return pl.pallas_call(
        functools.partial(collect_kernel, spots),
        out_shape=like(len(spots), BLOCK, BLOCK),
        in_specs=[HBM] * len(spots),
        out_specs=VM,
        scratch_shapes=[pltpu.SemaphoreType.DMA((len(spots),))],
        name="collect",
    )(*(in_hbm(array) for array in arrays))


def project_kernel(groups, heads_ref, cols_ref, *refs):
    row_refs, w_refs = refs[:groups], refs[groups : 3 * groups]
    part_refs, rows_buf = refs[3 * groups : 4 * groups], refs[-1]
    half = w_refs[0].shape[0]
    for i in range(groups):
        for e in range(2 * half):
            rows_buf[i * BLOCK : (i + 1) * BLOCK, e * HEAD_DIM : (e + 1) * HEAD_DIM] = row_refs[i][
                heads_ref[e]
            ]
    rows = rows_buf[...]
    for j in range(0, groups, 2):
        weights = jnp.concatenate(
            [
                jnp.concatenate(
                    [w_refs[side * groups + t][...].reshape(half * HEAD_DIM, BLOCK) for side in range(2)],
                    axis=0,
                )
                for t in (j, j + 1)
            ],
            axis=1,
        )
        found = jnp.dot(rows, weights, preferred_element_type=F32).astype(BF16)
        for n in range(2):
            at = pl.ds(pl.multiple_of(cols_ref[j + n] * BLOCK, BLOCK), BLOCK)
            for i in range(groups):
                part_refs[i][:, at] = found[
                    i * BLOCK : (i + 1) * BLOCK, n * BLOCK : (n + 1) * BLOCK
                ]


def project(heads, cols, rows, weights):
    groups = len(rows)
    width = rows[0].shape[0] * HEAD_DIM
    return pl.pallas_call(
        functools.partial(project_kernel, groups),
        out_shape=(like(BLOCK, groups * BLOCK),) * groups,
        in_specs=[SM, SM] + [VM] * (3 * groups),
        out_specs=(VM,) * groups,
        scratch_shapes=[pltpu.VMEM((groups * BLOCK, width), BF16)],
        compiler_params=pltpu.CompilerParams(vmem_limit_bytes=24 * MIB),
        name="project",
    )(heads, cols, *rows, *weights)


def unpack_kernel(groups, cols_ref, places_ref, grads_ref, *refs):
    layer_refs, pg_refs = refs[:groups], refs[groups : 2 * groups]
    layer_ref, dq_ref, dk_ref, dv_ref, pg_ref = refs[2 * groups :]
    for h in range(grads_ref.shape[0]):
        cols = slice(h * HEAD_DIM, (h + 1) * HEAD_DIM)
        dq_ref[:, cols] = grads_ref[h, 0]
        dk_ref[:, cols] = grads_ref[h, 1]
        dv_ref[:, cols] = grads_ref[h, 2]
    wide = layer_refs[0].shape[1]
    for i in range(groups):
        layer_ref[:, pl.ds(pl.multiple_of(places_ref[i] * wide, wide), wide)] = layer_refs[i][...]
        for j in range(groups):
            at = pl.multiple_of(cols_ref[i * groups + j] * BLOCK, BLOCK)
            pg_ref[:, pl.ds(at, BLOCK)] = pg_refs[i][j].astype(F32)


def unpack(cols, places, grads, layers, pg_pieces):
    wide = like(BLOCK, grads.shape[0] * HEAD_DIM)
    groups = len(pg_pieces)
    return pl.pallas_call(
        functools.partial(unpack_kernel, groups),
        out_shape=(
            like(BLOCK, groups * layers[0].shape[1]),
            wide,
            wide,
            wide,
            like(HEAD_DIM, groups * groups * BLOCK, dtype=F32),
        ),
        in_specs=[SM, SM, VM] + [VM] * (2 * groups),
        out_specs=(VM,) * 5,
        compiler_params=pltpu.CompilerParams(vmem_limit_bytes=24 * MIB),
        name="unpack",
    )(cols, places, grads, *layers, *pg_pieces)


def shifted(value, axis, by):
    size = lax.axis_size(axis)
    return lax.ppermute(value, axis, [(i, (i + by) % size) for i in range(size)])


def from_others(value, axis):
    return [value] + [shifted(value, axis, i) for i in range(1, lax.axis_size(axis))]


def spread(value, axis):
    size = lax.axis_size(axis)
    here = lax.axis_index(axis)
    total = lax.dynamic_index_in_dim(value, here, 0, keepdims=False).astype(F32)
    for i in range(1, size):
        piece = lax.dynamic_index_in_dim(value, (here + i) % size, 0, keepdims=False)
        total = total + shifted(piece, axis, i).astype(F32)
    return total


def swapped(value):
    return lax.ppermute(value, "c", [(0, 1), (1, 0)])


def body(query_in, key_in, value_in, out_grad, out_proj, key_blocks):
    seq, dp = ("z", "c"), ("x", "y")
    chips = lax.axis_size("z")
    core, z = lax.axis_index("c").astype(jnp.int32), lax.axis_index("z").astype(jnp.int32)
    x, y = lax.axis_index("x").astype(jnp.int32), lax.axis_index("y").astype(jnp.int32)
    tokens = lax.axis_size(seq) * lax.axis_size(dp) * query_in.shape[1]
    groups = lax.axis_size("x")
    chunks = out_proj.shape[1] // BLOCK
    blocks = key_blocks[0]
    index = jnp.arange(groups, dtype=jnp.int32)

    place = (x * groups + y)[None]
    qkv_out, gw = pack(place, query_in[0], key_in[0], value_in[0], out_grad[0], out_proj)
    qkv = lax.all_to_all(qkv_out, seq, split_axis=0, concat_axis=0, tiled=True)
    proj_theirs = swapped(out_proj)

    shifts, parts, shards = [0], [(0, 0, chunks)], [gw]
    up = down = gw
    for k in range(1, chips // 2):
        if k == chips // 2 - 1:
            qkv, up, down = lax.optimization_barrier((qkv, up, down))
        up, down = shifted(up, "z", 1), shifted(down, "z", -1)
        for shift, array in ((-k, up), (k, down)):
            parts.append((len(shifts), 0, chunks))
            shifts.append(shift)
            shards.append(array)
    cut = chunks // 2
    parts += [(len(shifts), 0, cut), (len(shifts), cut, chunks)]
    shifts.append(chips // 2)
    shards += [shifted(up[:cut], "z", 1), shifted(down[cut:], "z", -1)]
    parts = tuple(parts)
    steps = jnp.array([s % chips for s in shifts], jnp.int32)
    spot = jnp.concatenate([jnp.stack([z, core]), steps])

    attn, attn_t, lse = forward(blocks, qkv)
    other_t = swapped(
        lax.dynamic_index_in_dim(
            attn_t.reshape((chips, 2) + attn_t.shape[1:]), 1 - core, 1, keepdims=False
        )
    )
    early, theirs_early = attn_grad(parts[:-2], out_proj, proj_theirs, shards[:-2])
    theirs_early = swapped(theirs_early)
    attn, shards[-2], shards[-1] = lax.optimization_barrier((attn, shards[-2], shards[-1]))
    attn_rows = lax.all_to_all(attn, seq, split_axis=0, concat_axis=0, tiled=True)
    late, theirs_late = attn_grad(
        ((0, 0, cut), (0, cut, chunks)), out_proj, proj_theirs, shards[-2:]
    )
    theirs_late = swapped(theirs_late)
    spots = tuple([chunks] * (chips - 1) + [chunks - cut])
    own_weights = collect(spots, shards[: chips - 1] + shards[-1:])
    theirs_late, own_weights = lax.optimization_barrier((theirs_late, own_weights))
    weights = from_others(own_weights, "y")
    grads = backward(blocks, spot, qkv, attn_t, lse, early, theirs_early, late, theirs_late)
    grad_rows = lax.all_to_all(grads, seq, split_axis=0, concat_axis=0, tiled=True)

    weights += [swapped(piece) for piece in weights]
    rows = from_others(attn_rows, "x")
    owner = 2 * ((z + steps) % chips)
    heads = jnp.concatenate([owner + core, owner + 1 - core])
    found = project(heads, (y - index) % groups, rows, weights)
    layers = [part if i == 0 else shifted(part, "x", -i) for i, part in enumerate(found)]

    other_t, _ = lax.optimization_barrier((other_t, rows))
    pg_mine, pg_theirs = weight_grad(parts, spot, attn_t, other_t, chunks, shards)
    pg = (pg_mine.astype(F32) + swapped(pg_theirs).astype(F32)).astype(BF16)
    pg = spread(pg.reshape((groups, groups) + pg.shape[1:]), "x").astype(BF16)
    pg = (spread(pg, "y") * (1.0 / math.sqrt(tokens))).astype(BF16)
    pg_pieces = from_others(jnp.stack(from_others(pg, "y")), "x")
    cols = (((x - index) % groups)[:, None] * groups + ((y - index) % groups)[None]).reshape(-1)

    layer, dq, dk, dv, proj_grad = unpack(cols, (x + index) % groups, grad_rows, layers, pg_pieces)
    return layer[None], dq[None], dk[None], dv[None], proj_grad


def solution(mesh):
    split = Mesh(mesh.devices.reshape(8, 2, 4, 4), ("z", "c", "x", "y"))
    rows = P(("x", "y"), ("z", "c"), None)
    in_specs = (rows, rows, rows, rows, P(("z", "c"), None), P(("z", "c"), None, None))
    out_specs = (rows, rows, rows, rows, P(("z", "c"), None))
    return jax.shard_map(body, mesh=split, in_specs=in_specs, out_specs=out_specs, check_vma=False)
```

time: 366 us -> 220 us (0.60)
  waiting for transfers between devices: 160 us -> 94.2 us
  Pallas kernels: 103 us -> 47.1 us
  local copies, waits for them, and re-layouts: 27.1 us -> 6.65 us
    ppermute x32 -> x29, waiting for transfers between devices: 160 us -> 82.5 us  [shifted(): lax.ppermute(value, axis, [(i, (i + by) % size) for i in range(size)])]
    pallas_call x4 -> x8, Pallas kernels: 90.8 us -> 34.6 us  [the longest x1 13.6 us: backward(): pl.pallas_call(backward_kernel, out_shape=like(count, 3, BLOCK, HEAD_DIM)...]
    unnamed x50 -> x36, local copies, waits for them, and re-layouts: 20.9 us -> 3.45 us
    all_to_all x1, waiting for transfers between devices: 0.01 us -> 8.42 us  [body(): lax.all_to_all(attn, seq, split_axis=0, concat_axis=0, tiled=True)]
    ppermute x32 -> x29, starting transfers between devices: 38.2 us -> 36.1 us  [shifted(): lax.ppermute(value, axis, [(i, (i + by) % size) for i in range(size)])]
  transfers between devices with their start and end apart: 44 -> 41, of which waited for: 12 -> 12; matrix products, arithmetic and copies ran while one was open for 6% -> 3% of each run, Pallas kernels for 9% -> 19%
where the time goes in v2:
time: 220 us; the launch traced here: 216 us
  waiting for transfers between devices  94.2 us (43%)
  starting transfers between devices  64 us (29%)
  Pallas kernels  47.1 us (21%)
  local copies, waits for them, and re-layouts  6.65 us (3%)
  other arithmetic  3.63 us (2%)
    ppermute x29, waiting for transfers between devices, shifted(): lax.ppermute(value, axis, [(i, (i + by) % size) for i in range(size)])  82.5 us
    ppermute x29, starting transfers between devices, shifted(): lax.ppermute(value, axis, [(i, (i + by) % size) for i in range(size)])  36.1 us
    pallas_call x1, Pallas kernels, backward(): pl.pallas_call(backward_kernel, out_shape=like(count, 3, BLOCK, HEAD_DIM)...  13.6 us
    pallas_call x1, Pallas kernels, forward(): pl.pallas_call(forward_kernel, out_shape=(like(count, BLOCK, HEAD_DIM), l...  12.5 us
    all_to_all x1, starting transfers between devices, body(): qkv = lax.all_to_all(qkv_out, seq, split_axis=0, concat_axis=0, tiled=True)  10.1 us
    all_to_all x1, starting transfers between devices, body(): lax.all_to_all(attn, seq, split_axis=0, concat_axis=0, tiled=True)  9.12 us
    all_to_all x1, waiting for transfers between devices, body(): lax.all_to_all(attn, seq, split_axis=0, concat_axis=0, tiled=True)  8.42 us
    pallas_call x2, Pallas kernels, attn_grad(): pl.pallas_call(functools.partial(attn_grad_kernel, parts), out_shape=(lik...  6.11 us
  transfers between devices with their start and end apart: 41, of which 12 were waited for; matrix products, arithmetic and copies ran while one was open for 3% of the time, Pallas kernels for 19%

profile of v2, /device:TPU:1, one launch (start us, length us, event | category | flops | bytes accessed | tf_op | source)
XLA Modules:
  0.0 216.5 jit_solution(5954737188884851888)
XLA Ops:
  0.6 3.0 %pack.1 = (bf16[16,3,128,128]{3,2,1,0:T(8,128)(2,1)}, bf16[17,128,128]{2,1,0:T(8,128)(2,1)}) custom-call(s32[1]{0:T(128)} %bitcast.3.place_ref, bf16[128,2048]{1,0:T(8,128)(2,1)} %bitcast.43, bf16[128,2048]{1,0:T(8,128)(2,1)} %bitcast.44, bf16[128,2048]{1,0:T(8,128)(2,1)} %bitcast.45, bf16[128,2048]{1,0:T(8,128)(2,1)} %bitcast.46, bf16[128,2048]{1,0:T(8,128)(2,1)} %mine_ref.3), custom_call_target="tpu_custom_call" | custom-call | tf_op jit(solution)/shard_map/pack/pallas_call | solution.py:62
  3.7 10.1 %all-to-all-start = ((bf16[16,3,128,128]{3,2,1,0:T(8,128)(2,1)}), bf16[16,3,128,128]{3,2,1,0:T(8,128)(2,1)S(1)}, u32[]{:S(2)}, u32[]{:S(2)}) async-start(bf16[16,3,128,128]{3,2,1,0:T(8,128)(2,1)} %get-tuple-element.34), calls=%async_computation | async-start | bytes 3145728 | tf_op jit(solution)/shard_map/all_to_all | solution.py:452
  13.8 1.5 collective-permute-start
  15.3 1.3 collective-permute-start.2
  16.6 46.4 %collective-permute-done.refs_1_ = bf16[17,128,128]{2,1,0:T(8,128)(2,1)S(1)} collective-permute-done((bf16[17,128,128]{2,1,0:T(8,128)(2,1)S(1)}, bf16[17,128,128]{2,1,0:T(8,128)(2,1)S(1)}, u32[]{:S(2)}, u32[]{:S(2)}) %collective-permute-start) | collective-permute-done | bytes 557088 | tf_op jit(solution)/shard_map/ppermute | solution.py:418
  63.0 2.7 %collective-permute-start.3 = (bf16[17,128,128]{2,1,0:T(8,128)(2,1)S(1)}, bf16[17,128,128]{2,1,0:T(8,128)(2,1)S(1)}, u32[]{:S(2)}, u32[]{:S(2)}) collective-permute-start(bf16[17,128,128]{2,1,0:T(8,128)(2,1)S(1)} %collective-permute-done.2.refs_2_), channel_id=1, source_target_pairs={{0,224},{32,0},{64,32},{96,64},{128,96},{160,128},{192,160},{224,1... | collective-permute-start | bytes 1671176 | tf_op jit(solution)/shard_map/ppermute | solution.py:418
  65.7 11.8 %collective-permute-done.1.refs_3_ = bf16[17,128,128]{2,1,0:T(8,128)(2,1)S(1)} collective-permute-done((bf16[17,128,128]{2,1,0:T(8,128)(2,1)S(1)}, bf16[17,128,128]{2,1,0:T(8,128)(2,1)S(1)}, u32[]{:S(2)}, u32[]{:S(2)}) %collective-permute-start.1) | collective-permute-done | bytes 557088 | tf_op jit(solution)/shard_map/ppermute | solution.py:418
  77.5 2.4 %collective-permute-start.6 = (bf16[17,128,128]{2,1,0:T(8,128)(2,1)S(1)}, bf16[17,128,128]{2,1,0:T(8,128)(2,1)S(1)}, u32[]{:S(2)}, u32[]{:S(2)}) collective-permute-start(bf16[17,128,128]{2,1,0:T(8,128)(2,1)S(1)} %collective-permute-done.3.refs_4_), channel_id=1, source_target_pairs={{0,224},{32,0},{64,32},{96,64},{128,96},{160,128},{192,160},{224,1... | collective-permute-start | bytes 1671176 | tf_op jit(solution)/shard_map/ppermute | solution.py:418
  79.9 10.1 %collective-permute-done.6.refs_6_ = bf16[17,128,128]{2,1,0:T(8,128)(2,1)S(1)} collective-permute-done((bf16[17,128,128]{2,1,0:T(8,128)(2,1)S(1)}, bf16[17,128,128]{2,1,0:T(8,128)(2,1)S(1)}, u32[]{:S(2)}, u32[]{:S(2)}) %collective-permute-start.6) | collective-permute-done | bytes 557088 | tf_op jit(solution)/shard_map/ppermute | solution.py:418
  90.8 3.2 %collective-permute-start.9 = (bf16[9,128,128]{2,1,0:T(8,128)(2,1)}, bf16[9,128,128]{2,1,0:T(8,128)(2,1)S(1)}, u32[]{:S(2)}, u32[]{:S(2)}) collective-permute-start(bf16[9,128,128]{2,1,0:T(8,128)(2,1)} %slice.9), channel_id=1, source_target_pairs={{0,224},{32,0},{64,32},{96,64},{128,96},{160,128},{192,160},{224,1... | collective-permute-start | bytes 884744 | tf_op jit(solution)/shard_map/ppermute | solution.py:418
  95.0 12.5 %forward.1 = (bf16[16,128,128]{2,1,0:T(8,128)(2,1)}, bf16[16,128,128]{2,1,0:T(8,128)(2,1)S(1)}, f32[16,1,128]{2,1,0:T(1,128)S(1)}) custom-call(s32[16,8]{1,0:T(8,128)S(1)} %copy.13.blocks_ref, bf16[16,3,128,128]{3,2,1,0:T(8,128)(2,1)S(1)} %all-to-all-done.qkv_ref), custom_call_target="tpu_custom_call" | custom-call | tf_op jit(solution)/shard_map/forward/pallas_call | solution.py:118
  108.3 9.1 %all-to-all-start.2 = ((bf16[16,128,128]{2,1,0:T(8,128)(2,1)}), bf16[16,128,128]{2,1,0:T(8,128)(2,1)}, u32[]{:S(2)}, u32[]{:S(2)}) async-start(bf16[16,128,128]{2,1,0:T(8,128)(2,1)} %get-tuple-element.49), calls=%async_computation.2 | async-start | bytes 1048576 | tf_op jit(solution)/shard_map/all_to_all | solution.py:482
  117.6 1.8 collective-permute-done.4.theirs_ref
  119.4 4.6 %attn_grad.2 = (bf16[7,128,128]{2,1,0:T(8,128)(2,1)S(1)}, bf16[7,128,128]{2,1,0:T(8,128)(2,1)}) custom-call(bf16[128,2048]{1,0:T(8,128)(2,1)S(1)} %copy-done, bf16[128,2048]{1,0:T(8,128)(2,1)S(1)} %collective-permute-done.4.theirs_ref, bf16[17,128,128]{2,1,0:T(8,128)(2,1)} %get-tuple-element.35.refs_0_, bf16[17,128,128]{2,1,0:T(8,128)(2,1)} %copy-done.8, ...), custom_call_target="tpu_custom_call" | custom-call | tf_op jit(solution)/shard_map/attn_grad/pallas_call | solution.py:172
  124.3 1.5 attn_grad.3
  126.4 8.4 %all-to-all-done.2.refs_0_ = bf16[16,128,128]{2,1,0:T(8,128)(2,1)} async-done(((bf16[16,128,128]{2,1,0:T(8,128)(2,1)}), bf16[16,128,128]{2,1,0:T(8,128)(2,1)}, u32[]{:S(2)}, u32[]{:S(2)}) %all-to-all-start.2) | async-done | bytes 524320 | tf_op jit(solution)/shard_map/all_to_all | solution.py:482
  134.8 1.2 collective-permute-start.11
  136.0 2.4 %collective-permute-start.12 = (bf16[16,128,128]{2,1,0:T(8,128)(2,1)}, bf16[16,128,128]{2,1,0:T(8,128)(2,1)}, u32[]{:S(2)}, u32[]{:S(2)}) collective-permute-start(bf16[16,128,128]{2,1,0:T(8,128)(2,1)} %all-to-all-done.2.refs_0_), channel_id=1, source_target_pairs={{0,8},{4,12},{8,0},{12,4},{1,9},{5,13},{9,1},{13,5},{2,10},{6,14},... | collective-permute-start | bytes 1572872 | tf_op jit(solution)/shard_map/ppermute | solution.py:418
  138.5 1.2 collective-permute-start.13
  139.7 1.6 collect.1.refs_4_
  141.4 13.6 %backward.1 = bf16[16,3,128,128]{3,2,1,0:T(8,128)(2,1)} custom-call(s32[16,8]{1,0:T(8,128)S(1)} %copy.13.blocks_ref, s32[10]{0:T(128)S(1)} %pad_add_fusion.place_ref, bf16[16,3,128,128]{3,2,1,0:T(8,128)(2,1)S(1)} %all-to-all-done.qkv_ref, bf16[16,128,128]{2,1,0:T(8,128)(2,1)S(1)} %get-tuple-element.37.attn_t_ref.attn_ref, ...), custom_call_target="tpu_custom_call" | custom-call | tf_op jit(solution)/shard_map/backward/pallas_call | solution.py:297
  155.0 3.7 %all-to-all-start.1 = ((bf16[16,3,128,128]{3,2,1,0:T(8,128)(2,1)}), bf16[16,3,128,128]{3,2,1,0:T(8,128)(2,1)S(1)}, u32[]{:S(2)}, u32[]{:S(2)}) async-start(bf16[16,3,128,128]{3,2,1,0:T(8,128)(2,1)} %backward.1), calls=%async_computation.1 | async-start | bytes 3145728 | tf_op jit(solution)/shard_map/all_to_all | solution.py:492
  158.9 1.4 collective-permute-done.24.other_ref
  160.4 1.1 collective-permute-done.12.refs_2_
  161.5 4.0 %weight_grad.1 = (bf16[16,128,128]{2,1,0:T(8,128)(2,1)S(1)}, bf16[16,128,128]{2,1,0:T(8,128)(2,1)}) custom-call(s32[10]{0:T(128)S(1)} %pad_add_fusion.place_ref, bf16[16,128,128]{2,1,0:T(8,128)(2,1)S(1)} %get-tuple-element.37.attn_t_ref.attn_ref, bf16[8,128,128]{2,1,0:T(8,128)(2,1)S(1)} %collective-permute-done.24.other_ref, ...), custom_call_target="tpu_custom_call" | custom-call | tf_op jit(solution)/shard_map/weight_grad/pallas_call | solution.py:216
  166.6 1.4 collective-permute-start.14
  167.9 2.6 %collective-permute-start.15 = (bf16[8,128,128]{2,1,0:T(8,128)(2,1)S(1)}, bf16[8,128,128]{2,1,0:T(8,128)(2,1)S(1)}, u32[]{:S(2)}, u32[]{:S(2)}) collective-permute-start(bf16[8,128,128]{2,1,0:T(8,128)(2,1)S(1)} %copy-done.1), channel_id=1, source_target_pairs={{0,2},{1,3},{2,0},{3,1},{4,6},{5,7},{6,4},{7,5},{8,10},{9,11},{10,... | collective-permute-start | bytes 786440 | tf_op jit(solution)/shard_map/ppermute | solution.py:418
  170.5 1.1 collective-permute-start.16
  171.6 1.3 add_convert_fusion
  173.8 2.7 %collective-permute-start.28 = (bf16[4,128,128]{2,1,0:T(8,128)(2,1)}, bf16[4,128,128]{2,1,0:T(8,128)(2,1)}, u32[]{:S(2)}, u32[]{:S(2)}) collective-permute-start(bf16[4,128,128]{2,1,0:T(8,128)(2,1)} %get-tuple-element.66), channel_id=1, source_target_pairs={{0,12},{4,0},{8,4},{12,8},{1,13},{5,1},{9,5},{13,9},{2,14},{6,2},{... | collective-permute-start | bytes 393224 | tf_op jit(solution)/shard_map/ppermute | solution.py:418
  176.5 0.9 collective-permute-start.27
  177.7 4.6 %collective-permute-done.15.refs_6_ = bf16[8,128,128]{2,1,0:T(8,128)(2,1)S(1)} collective-permute-done((bf16[8,128,128]{2,1,0:T(8,128)(2,1)S(1)}, bf16[8,128,128]{2,1,0:T(8,128)(2,1)S(1)}, u32[]{:S(2)}, u32[]{:S(2)}) %collective-permute-start.15) | collective-permute-done | bytes 262176 | tf_op jit(solution)/shard_map/ppermute | solution.py:418
  182.3 1.1 collective-permute-start.17
  183.9 1.8 collective-permute-start.20
  185.9 1.2 fusion.2
  188.1 1.9 collective-permute-start.30
  190.8 0.9 copy-done.4
  191.7 3.5 %project.1 = (bf16[128,512]{1,0:T(8,128)(2,1)S(1)}, bf16[128,512]{1,0:T(8,128)(2,1)S(1)}, bf16[128,512]{1,0:T(8,128)(2,1)}, bf16[128,512]{1,0:T(8,128)(2,1)}) custom-call(s32[16]{0:T(128)S(1)} %pad_add_fusion.1.heads_ref, s32[4]{0:T(128)S(1)} %and_select_fusion.2.cols_ref, bf16[16,128,128]{2,1,0:T(8,128)(2,1)} %all-to-all-done.2.refs_0_, ...), custom_call_target="tpu_custom_call" | custom-call | tf_op jit(solution)/shard_map/project/pallas_call | solution.py:370
  195.2 1.7 collective-permute-start.21
  196.9 0.8 fusion.6
  197.8 2.3 %collective-permute-start.34 = (bf16[128,128]{1,0:T(8,128)(2,1)S(1)}, bf16[128,128]{1,0:T(8,128)(2,1)S(1)}, u32[]{:S(2)}, u32[]{:S(2)}) collective-permute-start(bf16[128,128]{1,0:T(8,128)(2,1)S(1)} %fusion.6), channel_id=1, source_target_pairs={{0,3},{1,0},{2,1},{3,2},{4,7},{5,4},{6,5},{7,6},{8,11},{9,8},{10,9... | collective-permute-start | bytes 98312 | tf_op jit(solution)/shard_map/ppermute | solution.py:418
  200.1 0.9 collective-permute-start.33
  201.0 1.1 collective-permute-start.22
  202.1 2.3 %collective-permute-done.33 = bf16[128,128]{1,0:T(8,128)(2,1)S(1)} collective-permute-done((bf16[128,128]{1,0:T(8,128)(2,1)S(1)}, bf16[128,128]{1,0:T(8,128)(2,1)S(1)}, u32[]{:S(2)}, u32[]{:S(2)}) %collective-permute-start.33) | collective-permute-done | bytes 32800 | tf_op jit(solution)/shard_map/ppermute | solution.py:418
  205.1 1.8 collective-permute-start.36
  206.9 1.3 collective-permute-start.37
  208.3 5.4 %collective-permute-done.35.refs_5_ = bf16[4,128,128]{2,1,0:T(8,128)(2,1)S(1)} collective-permute-done((bf16[4,128,128]{2,1,0:T(8,128)(2,1)S(1)}, bf16[4,128,128]{2,1,0:T(8,128)(2,1)S(1)}, u32[]{:S(2)}, u32[]{:S(2)}) %collective-permute-start.35) | collective-permute-done | bytes 131104 | tf_op jit(solution)/shard_map/ppermute | solution.py:418
  213.7 2.8 %unpack.1 = (bf16[128,2048]{1,0:T(8,128)(2,1)}, bf16[128,2048]{1,0:T(8,128)(2,1)}, bf16[128,2048]{1,0:T(8,128)(2,1)}, bf16[128,2048]{1,0:T(8,128)(2,1)}, f32[128,2048]{1,0:T(8,128)}) custom-call(s32[16]{0:T(128)S(1)} %add.163.cols_ref, s32[4]{0:T(128)S(1)} %and_select_fusion.1.places_ref, bf16[16,3,128,128]{3,2,1,0:T(8,128)(2,1)S(1)} %all-to-all-done.1.grads_ref, ...), custom_call_target="tpu_custom_call" | custom-call | tf_op jit(solution)/shard_map/unpack/pallas_call | solution.py:400
  (98 shorter events, 9.6 us)
Async XLA Ops:
  3.7 91.2 %copy-start.16 = (s32[1,16,8]{1,2,0:T(8,128)S(1)}, s32[1,16,8]{1,2,0:T(8,128)}, u32[]{:S(2)}) copy-start(s32[1,16,8]{1,2,0:T(8,128)} %param.12) | copy-start | bytes 1540
  3.7 73.8 %all-to-all-start = ((bf16[16,3,128,128]{3,2,1,0:T(8,128)(2,1)}), bf16[16,3,128,128]{3,2,1,0:T(8,128)(2,1)S(1)}, u32[]{:S(2)}, u32[]{:S(2)}) async-start(bf16[16,3,128,128]{3,2,1,0:T(8,128)(2,1)} %get-tuple-element.34), calls=%async_computation | async-start | bytes 3145728 | tf_op jit(solution)/shard_map/all_to_all | solution.py:452
  13.8 49.2 %collective-permute-start = (bf16[17,128,128]{2,1,0:T(8,128)(2,1)S(1)}, bf16[17,128,128]{2,1,0:T(8,128)(2,1)S(1)}, u32[]{:S(2)}, u32[]{:S(2)}) collective-permute-start(bf16[17,128,128]{2,1,0:T(8,128)(2,1)S(1)} %copy-done.7), channel_id=1, source_target_pairs={{0,32},{32,64},{64,96},{96,128},{128,160},{160,192},{192,224},{224... | collective-permute-start | bytes 1671176 | tf_op jit(solution)/shard_map/ppermute | solution.py:418
  15.3 47.8 %collective-permute-start.2 = (bf16[17,128,128]{2,1,0:T(8,128)(2,1)S(1)}, bf16[17,128,128]{2,1,0:T(8,128)(2,1)S(1)}, u32[]{:S(2)}, u32[]{:S(2)}) collective-permute-start(bf16[17,128,128]{2,1,0:T(8,128)(2,1)S(1)} %copy-done.7), channel_id=1, source_target_pairs={{0,224},{32,0},{64,32},{96,64},{128,96},{160,128},{192,160},{224,1... | collective-permute-start | bytes 1671176 | tf_op jit(solution)/shard_map/ppermute | solution.py:418
  63.0 14.5 %copy-start.8 = (bf16[17,128,128]{2,1,0:T(8,128)(2,1)}, bf16[17,128,128]{2,1,0:T(8,128)(2,1)S(1)}, u32[]{:S(2)}) copy-start(bf16[17,128,128]{2,1,0:T(8,128)(2,1)S(1)} %collective-permute-done.refs_1_) | copy-start | bytes 1671172
  63.0 14.5 %collective-permute-start.1 = (bf16[17,128,128]{2,1,0:T(8,128)(2,1)S(1)}, bf16[17,128,128]{2,1,0:T(8,128)(2,1)S(1)}, u32[]{:S(2)}, u32[]{:S(2)}) collective-permute-start(bf16[17,128,128]{2,1,0:T(8,128)(2,1)S(1)} %collective-permute-done.refs_1_), channel_id=1, source_target_pairs={{0,32},{32,64},{64,96},{96,128},{128,160},{160,192},{192,224},{224... | collective-permute-start | bytes 1671176 | tf_op jit(solution)/shard_map/ppermute | solution.py:418
  63.0 14.5 %copy-start.9 = (bf16[17,128,128]{2,1,0:T(8,128)(2,1)}, bf16[17,128,128]{2,1,0:T(8,128)(2,1)S(1)}, u32[]{:S(2)}) copy-start(bf16[17,128,128]{2,1,0:T(8,128)(2,1)S(1)} %collective-permute-done.2.refs_2_) | copy-start | bytes 1671172
  63.0 14.5 %collective-permute-start.3 = (bf16[17,128,128]{2,1,0:T(8,128)(2,1)S(1)}, bf16[17,128,128]{2,1,0:T(8,128)(2,1)S(1)}, u32[]{:S(2)}, u32[]{:S(2)}) collective-permute-start(bf16[17,128,128]{2,1,0:T(8,128)(2,1)S(1)} %collective-permute-done.2.refs_2_), channel_id=1, source_target_pairs={{0,224},{32,0},{64,32},{96,64},{128,96},{160,128},{192,160},{224,1... | collective-permute-start | bytes 1671176 | tf_op jit(solution)/shard_map/ppermute | solution.py:418
  77.5 17.4 %copy-start.10 = (bf16[17,128,128]{2,1,0:T(8,128)(2,1)}, bf16[17,128,128]{2,1,0:T(8,128)(2,1)S(1)}, u32[]{:S(2)}) copy-start(bf16[17,128,128]{2,1,0:T(8,128)(2,1)S(1)} %collective-permute-done.1.refs_3_) | copy-start | bytes 1671172
  77.5 12.4 %copy-start.11 = (bf16[17,128,128]{2,1,0:T(8,128)(2,1)}, bf16[17,128,128]{2,1,0:T(8,128)(2,1)S(1)}, u32[]{:S(2)}) copy-start(bf16[17,128,128]{2,1,0:T(8,128)(2,1)S(1)} %collective-permute-done.3.refs_4_) | copy-start | bytes 1671172
  77.5 12.4 %collective-permute-start.6 = (bf16[17,128,128]{2,1,0:T(8,128)(2,1)S(1)}, bf16[17,128,128]{2,1,0:T(8,128)(2,1)S(1)}, u32[]{:S(2)}, u32[]{:S(2)}) collective-permute-start(bf16[17,128,128]{2,1,0:T(8,128)(2,1)S(1)} %collective-permute-done.3.refs_4_), channel_id=1, source_target_pairs={{0,224},{32,0},{64,32},{96,64},{128,96},{160,128},{192,160},{224,1... | collective-permute-start | bytes 1671176 | tf_op jit(solution)/shard_map/ppermute | solution.py:418
  79.9 14.0 %collective-permute-start.5 = (bf16[17,128,128]{2,1,0:T(8,128)(2,1)S(1)}, bf16[17,128,128]{2,1,0:T(8,128)(2,1)S(1)}, u32[]{:S(2)}, u32[]{:S(2)}) collective-permute-start(bf16[17,128,128]{2,1,0:T(8,128)(2,1)S(1)} %collective-permute-done.1.refs_3_), channel_id=1, source_target_pairs={{0,32},{32,64},{64,96},{96,128},{128,160},{160,192},{192,224},{224... | collective-permute-start | bytes 1671176 | tf_op jit(solution)/shard_map/ppermute | solution.py:418
  90.8 26.6 %copy-start = (bf16[128,2048]{1,0:T(8,128)(2,1)S(1)}, bf16[128,2048]{1,0:T(8,128)(2,1)}, u32[]{:S(2)}) copy-start(bf16[128,2048]{1,0:T(8,128)(2,1)} %mine_ref.3) | copy-start | bytes 1572868
  90.8 16.7 %collective-permute-start.9 = (bf16[9,128,128]{2,1,0:T(8,128)(2,1)}, bf16[9,128,128]{2,1,0:T(8,128)(2,1)S(1)}, u32[]{:S(2)}, u32[]{:S(2)}) collective-permute-start(bf16[9,128,128]{2,1,0:T(8,128)(2,1)} %slice.9), channel_id=1, source_target_pairs={{0,224},{32,0},{64,32},{96,64},{128,96},{160,128},{192,160},{224,1... | collective-permute-start | bytes 884744 | tf_op jit(solution)/shard_map/ppermute | solution.py:418
  94.7 12.7 %collective-permute-start.8 = (bf16[8,128,128]{2,1,0:T(8,128)(2,1)}, bf16[8,128,128]{2,1,0:T(8,128)(2,1)S(1)}, u32[]{:S(2)}, u32[]{:S(2)}) collective-permute-start(bf16[8,128,128]{2,1,0:T(8,128)(2,1)} %slice.8), channel_id=1, source_target_pairs={{0,32},{32,64},{64,96},{96,128},{128,160},{160,192},{192,224},{224... | collective-permute-start | bytes 786440 | tf_op jit(solution)/shard_map/ppermute | solution.py:418
  108.3 26.5 %all-to-all-start.2 = ((bf16[16,128,128]{2,1,0:T(8,128)(2,1)}), bf16[16,128,128]{2,1,0:T(8,128)(2,1)}, u32[]{:S(2)}, u32[]{:S(2)}) async-start(bf16[16,128,128]{2,1,0:T(8,128)(2,1)} %get-tuple-element.49), calls=%async_computation.2 | async-start | bytes 1048576 | tf_op jit(solution)/shard_map/all_to_all | solution.py:482
  117.4 2.0 collective-permute-start.4
  124.0 15.6 %copy-start.17 = (s32[8]{0:T(128)S(1)}, s32[8]{0:T(128)}, u32[]{:S(2)}) copy-start(s32[8]{0:T(128)} %constant.126.clone) | copy-start | bytes 100
  124.0 17.3 %collective-permute-start.7 = (bf16[7,128,128]{2,1,0:T(8,128)(2,1)}, bf16[7,128,128]{2,1,0:T(8,128)(2,1)}, u32[]{:S(2)}, u32[]{:S(2)}) collective-permute-start(bf16[7,128,128]{2,1,0:T(8,128)(2,1)} %get-tuple-element.42), channel_id=1, source_target_pairs={{0,16},{16,0},{1,17},{17,1},{2,18},{18,2},{3,19},{19,3},{4,20},{20... | collective-permute-start | bytes 688136 | tf_op jit(solution)/shard_map/ppermute | solution.py:436
  125.8 15.6 %collective-permute-start.10 = (bf16[1,128,128]{2,1,0:T(8,128)(2,1)S(1)}, bf16[1,128,128]{2,1,0:T(8,128)(2,1)S(1)}, u32[]{:S(2)}, u32[]{:S(2)}) collective-permute-start(bf16[1,128,128]{2,1,0:T(8,128)(2,1)S(1)} %get-tuple-element.47), channel_id=1, source_target_pairs={{0,16},{16,0},{1,17},{17,1},{2,18},{18,2},{3,19},{19,3},{4,20},{20... | collective-permute-start | bytes 98312 | tf_op jit(solution)/shard_map/ppermute | solution.py:436
  134.8 25.6 %collective-permute-start.11 = (bf16[16,128,128]{2,1,0:T(8,128)(2,1)}, bf16[16,128,128]{2,1,0:T(8,128)(2,1)S(1)}, u32[]{:S(2)}, u32[]{:S(2)}) collective-permute-start(bf16[16,128,128]{2,1,0:T(8,128)(2,1)} %all-to-all-done.2.refs_0_), channel_id=1, source_target_pairs={{0,4},{4,8},{8,12},{12,0},{1,5},{5,9},{9,13},{13,1},{2,6},{6,10},{... | collective-permute-start | bytes 1572872 | tf_op jit(solution)/shard_map/ppermute | solution.py:418
  136.0 25.4 %collective-permute-start.12 = (bf16[16,128,128]{2,1,0:T(8,128)(2,1)}, bf16[16,128,128]{2,1,0:T(8,128)(2,1)}, u32[]{:S(2)}, u32[]{:S(2)}) collective-permute-start(bf16[16,128,128]{2,1,0:T(8,128)(2,1)} %all-to-all-done.2.refs_0_), channel_id=1, source_target_pairs={{0,8},{4,12},{8,0},{12,4},{1,9},{5,13},{9,1},{13,5},{2,10},{6,14},... | collective-permute-start | bytes 1572872 | tf_op jit(solution)/shard_map/ppermute | solution.py:418
  138.5 23.0 %collective-permute-start.13 = (bf16[16,128,128]{2,1,0:T(8,128)(2,1)}, bf16[16,128,128]{2,1,0:T(8,128)(2,1)}, u32[]{:S(2)}, u32[]{:S(2)}) collective-permute-start(bf16[16,128,128]{2,1,0:T(8,128)(2,1)} %all-to-all-done.2.refs_0_), channel_id=1, source_target_pairs={{0,12},{4,0},{8,4},{12,8},{1,13},{5,1},{9,5},{13,9},{2,14},{6,2},{... | collective-permute-start | bytes 1572872 | tf_op jit(solution)/shard_map/ppermute | solution.py:418
  155.0 58.7 %all-to-all-start.1 = ((bf16[16,3,128,128]{3,2,1,0:T(8,128)(2,1)}), bf16[16,3,128,128]{3,2,1,0:T(8,128)(2,1)S(1)}, u32[]{:S(2)}, u32[]{:S(2)}) async-start(bf16[16,3,128,128]{3,2,1,0:T(8,128)(2,1)} %backward.1), calls=%async_computation.1 | async-start | bytes 3145728 | tf_op jit(solution)/shard_map/all_to_all | solution.py:492
  158.7 1.6 collective-permute-start.24
  166.3 5.3 %collective-permute-start.25 = (bf16[16,128,128]{2,1,0:T(8,128)(2,1)}, bf16[16,128,128]{2,1,0:T(8,128)(2,1)}, u32[]{:S(2)}, u32[]{:S(2)}) collective-permute-start(bf16[16,128,128]{2,1,0:T(8,128)(2,1)} %get-tuple-element.57), channel_id=1, source_target_pairs={{0,16},{16,0},{1,17},{17,1},{2,18},{18,2},{3,19},{19,3},{4,20},{20... | collective-permute-start | bytes 1572872 | tf_op jit(solution)/shard_map/ppermute | solution.py:436
  166.6 10.9 %collective-permute-start.14 = (bf16[8,128,128]{2,1,0:T(8,128)(2,1)S(1)}, bf16[8,128,128]{2,1,0:T(8,128)(2,1)S(1)}, u32[]{:S(2)}, u32[]{:S(2)}) collective-permute-start(bf16[8,128,128]{2,1,0:T(8,128)(2,1)S(1)} %copy-done.1), channel_id=1, source_target_pairs={{0,1},{1,2},{2,3},{3,0},{4,5},{5,6},{6,7},{7,4},{8,9},{9,10},{10,1... | collective-permute-start | bytes 786440 | tf_op jit(solution)/shard_map/ppermute | solution.py:418
  167.9 14.4 %collective-permute-start.15 = (bf16[8,128,128]{2,1,0:T(8,128)(2,1)S(1)}, bf16[8,128,128]{2,1,0:T(8,128)(2,1)S(1)}, u32[]{:S(2)}, u32[]{:S(2)}) collective-permute-start(bf16[8,128,128]{2,1,0:T(8,128)(2,1)S(1)} %copy-done.1), channel_id=1, source_target_pairs={{0,2},{1,3},{2,0},{3,1},{4,6},{5,7},{6,4},{7,5},{8,10},{9,11},{10,... | collective-permute-start | bytes 786440 | tf_op jit(solution)/shard_map/ppermute | solution.py:418
  170.5 12.9 %collective-permute-start.16 = (bf16[8,128,128]{2,1,0:T(8,128)(2,1)S(1)}, bf16[8,128,128]{2,1,0:T(8,128)(2,1)S(1)}, u32[]{:S(2)}, u32[]{:S(2)}) collective-permute-start(bf16[8,128,128]{2,1,0:T(8,128)(2,1)S(1)} %copy-done.1), channel_id=1, source_target_pairs={{0,3},{1,0},{2,1},{3,2},{4,7},{5,4},{6,5},{7,6},{8,11},{9,8},{10,9... | collective-permute-start | bytes 786440 | tf_op jit(solution)/shard_map/ppermute | solution.py:418
  173.8 9.6 %collective-permute-start.28 = (bf16[4,128,128]{2,1,0:T(8,128)(2,1)}, bf16[4,128,128]{2,1,0:T(8,128)(2,1)}, u32[]{:S(2)}, u32[]{:S(2)}) collective-permute-start(bf16[4,128,128]{2,1,0:T(8,128)(2,1)} %get-tuple-element.66), channel_id=1, source_target_pairs={{0,12},{4,0},{8,4},{12,8},{1,13},{5,1},{9,5},{13,9},{2,14},{6,2},{... | collective-permute-start | bytes 393224 | tf_op jit(solution)/shard_map/ppermute | solution.py:418
  176.5 7.4 %collective-permute-start.27 = (bf16[4,128,128]{2,1,0:T(8,128)(2,1)}, bf16[4,128,128]{2,1,0:T(8,128)(2,1)}, u32[]{:S(2)}, u32[]{:S(2)}) collective-permute-start(bf16[4,128,128]{2,1,0:T(8,128)(2,1)} %get-tuple-element.67), channel_id=1, source_target_pairs={{0,8},{4,12},{8,0},{12,4},{1,9},{5,13},{9,1},{13,5},{2,10},{6,14},... | collective-permute-start | bytes 393224 | tf_op jit(solution)/shard_map/ppermute | solution.py:418
  177.5 8.4 %collective-permute-start.26 = (bf16[4,128,128]{2,1,0:T(8,128)(2,1)S(1)}, bf16[4,128,128]{2,1,0:T(8,128)(2,1)}, u32[]{:S(2)}, u32[]{:S(2)}) collective-permute-start(bf16[4,128,128]{2,1,0:T(8,128)(2,1)S(1)} %get-tuple-element.65), channel_id=1, source_target_pairs={{0,4},{4,8},{8,12},{12,0},{1,5},{5,9},{9,13},{13,1},{2,6},{6,10},{... | collective-permute-start | bytes 393224 | tf_op jit(solution)/shard_map/ppermute | solution.py:418
  182.3 5.8 %collective-permute-start.17 = (bf16[8,128,128]{2,1,0:T(8,128)(2,1)S(1)}, bf16[8,128,128]{2,1,0:T(8,128)(2,1)S(1)}, u32[]{:S(2)}, u32[]{:S(2)}) collective-permute-start(bf16[8,128,128]{2,1,0:T(8,128)(2,1)S(1)} %copy-done.1), channel_id=1, source_target_pairs={{0,16},{16,0},{1,17},{17,1},{2,18},{18,2},{3,19},{19,3},{4,20},{20... | collective-permute-start | bytes 786440 | tf_op jit(solution)/shard_map/ppermute | solution.py:436
  183.4 6.5 %collective-permute-start.18 = (bf16[8,128,128]{2,1,0:T(8,128)(2,1)S(1)}, bf16[8,128,128]{2,1,0:T(8,128)(2,1)S(1)}, u32[]{:S(2)}, u32[]{:S(2)}) collective-permute-start(bf16[8,128,128]{2,1,0:T(8,128)(2,1)S(1)} %collective-permute-done.14.refs_5_), channel_id=1, source_target_pairs={{0,16},{16,0},{1,17},{17,1},{2,18},{18,2},{3,19},{19,3},{4,20},{20... | collective-permute-start | bytes 786440 | tf_op jit(solution)/shard_map/ppermute | solution.py:436
  183.4 7.3 %collective-permute-start.19 = (bf16[8,128,128]{2,1,0:T(8,128)(2,1)S(1)}, bf16[8,128,128]{2,1,0:T(8,128)(2,1)}, u32[]{:S(2)}, u32[]{:S(2)}) collective-permute-start(bf16[8,128,128]{2,1,0:T(8,128)(2,1)S(1)} %collective-permute-done.15.refs_6_), channel_id=1, source_target_pairs={{0,16},{16,0},{1,17},{17,1},{2,18},{18,2},{3,19},{19,3},{4,20},{20... | collective-permute-start | bytes 786440 | tf_op jit(solution)/shard_map/ppermute | solution.py:436
  183.9 6.8 %collective-permute-start.20 = (bf16[8,128,128]{2,1,0:T(8,128)(2,1)S(1)}, bf16[8,128,128]{2,1,0:T(8,128)(2,1)}, u32[]{:S(2)}, u32[]{:S(2)}) collective-permute-start(bf16[8,128,128]{2,1,0:T(8,128)(2,1)S(1)} %collective-permute-done.16.refs_7_), channel_id=1, source_target_pairs={{0,16},{16,0},{1,17},{17,1},{2,18},{18,2},{3,19},{19,3},{4,20},{20... | collective-permute-start | bytes 786440 | tf_op jit(solution)/shard_map/ppermute | solution.py:436
  187.8 9.2 %collective-permute-start.31 = (bf16[128,128]{1,0:T(8,128)(2,1)}, bf16[128,128]{1,0:T(8,128)(2,1)}, u32[]{:S(2)}, u32[]{:S(2)}) collective-permute-start(bf16[128,128]{1,0:T(8,128)(2,1)} %get-tuple-element.69), channel_id=1, source_target_pairs={{0,3},{1,0},{2,1},{3,2},{4,7},{5,4},{6,5},{7,6},{8,11},{9,8},{10,9... | collective-permute-start | bytes 98312 | tf_op jit(solution)/shard_map/ppermute | solution.py:418
  188.1 8.9 %collective-permute-start.30 = (bf16[128,128]{1,0:T(8,128)(2,1)}, bf16[128,128]{1,0:T(8,128)(2,1)}, u32[]{:S(2)}, u32[]{:S(2)}) collective-permute-start(bf16[128,128]{1,0:T(8,128)(2,1)} %get-tuple-element.70), channel_id=1, source_target_pairs={{0,2},{1,3},{2,0},{3,1},{4,6},{5,7},{6,4},{7,5},{8,10},{9,11},{10,... | collective-permute-start | bytes 98312 | tf_op jit(solution)/shard_map/ppermute | solution.py:418
  190.7 6.3 %collective-permute-start.29 = (bf16[128,128]{1,0:T(8,128)(2,1)}, bf16[128,128]{1,0:T(8,128)(2,1)}, u32[]{:S(2)}, u32[]{:S(2)}) collective-permute-start(bf16[128,128]{1,0:T(8,128)(2,1)} %get-tuple-element.68), channel_id=1, source_target_pairs={{0,1},{1,2},{2,3},{3,0},{4,5},{5,6},{6,7},{7,4},{8,9},{9,10},{10,1... | collective-permute-start | bytes 98312 | tf_op jit(solution)/shard_map/ppermute | solution.py:418
  195.2 11.7 %collective-permute-start.21 = (bf16[128,512]{1,0:T(8,128)(2,1)S(1)}, bf16[128,512]{1,0:T(8,128)(2,1)S(1)}, u32[]{:S(2)}, u32[]{:S(2)}) collective-permute-start(bf16[128,512]{1,0:T(8,128)(2,1)S(1)} %get-tuple-element.52), channel_id=1, source_target_pairs={{0,12},{4,0},{8,4},{12,8},{1,13},{5,1},{9,5},{13,9},{2,14},{6,2},{... | collective-permute-start | bytes 393224 | tf_op jit(solution)/shard_map/ppermute | solution.py:418
  197.8 4.3 %collective-permute-start.34 = (bf16[128,128]{1,0:T(8,128)(2,1)S(1)}, bf16[128,128]{1,0:T(8,128)(2,1)S(1)}, u32[]{:S(2)}, u32[]{:S(2)}) collective-permute-start(bf16[128,128]{1,0:T(8,128)(2,1)S(1)} %fusion.6), channel_id=1, source_target_pairs={{0,3},{1,0},{2,1},{3,2},{4,7},{5,4},{6,5},{7,6},{8,11},{9,8},{10,9... | collective-permute-start | bytes 98312 | tf_op jit(solution)/shard_map/ppermute | solution.py:418
  200.1 4.3 %collective-permute-start.33 = (bf16[128,128]{1,0:T(8,128)(2,1)S(1)}, bf16[128,128]{1,0:T(8,128)(2,1)S(1)}, u32[]{:S(2)}, u32[]{:S(2)}) collective-permute-start(bf16[128,128]{1,0:T(8,128)(2,1)S(1)} %fusion.6), channel_id=1, source_target_pairs={{0,2},{1,3},{2,0},{3,1},{4,6},{5,7},{6,4},{7,5},{8,10},{9,11},{10,... | collective-permute-start | bytes 98312 | tf_op jit(solution)/shard_map/ppermute | solution.py:418
  201.0 4.0 %collective-permute-start.32 = (bf16[128,128]{1,0:T(8,128)(2,1)S(1)}, bf16[128,128]{1,0:T(8,128)(2,1)S(1)}, u32[]{:S(2)}, u32[]{:S(2)}) collective-permute-start(bf16[128,128]{1,0:T(8,128)(2,1)S(1)} %fusion.6), channel_id=1, source_target_pairs={{0,1},{1,2},{2,3},{3,0},{4,5},{5,6},{6,7},{7,4},{8,9},{9,10},{10,1... | collective-permute-start | bytes 98312 | tf_op jit(solution)/shard_map/ppermute | solution.py:418
  201.0 7.3 %collective-permute-start.22 = (bf16[128,512]{1,0:T(8,128)(2,1)}, bf16[128,512]{1,0:T(8,128)(2,1)S(1)}, u32[]{:S(2)}, u32[]{:S(2)}) collective-permute-start(bf16[128,512]{1,0:T(8,128)(2,1)} %get-tuple-element.53), channel_id=1, source_target_pairs={{0,8},{4,12},{8,0},{12,4},{1,9},{5,13},{9,1},{13,5},{2,10},{6,14},... | collective-permute-start | bytes 393224 | tf_op jit(solution)/shard_map/ppermute | solution.py:418
  202.1 6.2 %collective-permute-start.23 = (bf16[128,512]{1,0:T(8,128)(2,1)}, bf16[128,512]{1,0:T(8,128)(2,1)S(1)}, u32[]{:S(2)}, u32[]{:S(2)}) collective-permute-start(bf16[128,512]{1,0:T(8,128)(2,1)} %get-tuple-element.54), channel_id=1, source_target_pairs={{0,4},{4,8},{8,12},{12,0},{1,5},{5,9},{9,13},{13,1},{2,6},{6,10},{... | collective-permute-start | bytes 393224 | tf_op jit(solution)/shard_map/ppermute | solution.py:418
  205.0 8.7 %collective-permute-start.35 = (bf16[4,128,128]{2,1,0:T(8,128)(2,1)S(1)}, bf16[4,128,128]{2,1,0:T(8,128)(2,1)S(1)}, u32[]{:S(2)}, u32[]{:S(2)}) collective-permute-start(bf16[4,128,128]{2,1,0:T(8,128)(2,1)S(1)} %pad_maximum_fusion.refs_4_), channel_id=1, source_target_pairs={{0,4},{4,8},{8,12},{12,0},{1,5},{5,9},{9,13},{13,1},{2,6},{6,10},{... | collective-permute-start | bytes 393224 | tf_op jit(solution)/shard_map/ppermute | solution.py:418
  205.1 8.6 %collective-permute-start.36 = (bf16[4,128,128]{2,1,0:T(8,128)(2,1)S(1)}, bf16[4,128,128]{2,1,0:T(8,128)(2,1)S(1)}, u32[]{:S(2)}, u32[]{:S(2)}) collective-permute-start(bf16[4,128,128]{2,1,0:T(8,128)(2,1)S(1)} %pad_maximum_fusion.refs_4_), channel_id=1, source_target_pairs={{0,8},{4,12},{8,0},{12,4},{1,9},{5,13},{9,1},{13,5},{2,10},{6,14},... | collective-permute-start | bytes 393224 | tf_op jit(solution)/shard_map/ppermute | solution.py:418
  206.9 6.8 %collective-permute-start.37 = (bf16[4,128,128]{2,1,0:T(8,128)(2,1)S(1)}, bf16[4,128,128]{2,1,0:T(8,128)(2,1)S(1)}, u32[]{:S(2)}, u32[]{:S(2)}) collective-permute-start(bf16[4,128,128]{2,1,0:T(8,128)(2,1)S(1)} %pad_maximum_fusion.refs_4_), channel_id=1, source_target_pairs={{0,12},{4,0},{8,4},{12,8},{1,13},{5,1},{9,5},{13,9},{2,14},{6,2},{... | collective-permute-start | bytes 393224 | tf_op jit(solution)/shard_map/ppermute | solution.py:418
  (11 other events, 35.8 us)

commit v3 on v2

--- a/solution.py
+++ b/solution.py
@@ -19,6 +19,15 @@
 SM = pl.BlockSpec(memory_space=pltpu.SMEM)
 HBM = pl.BlockSpec(memory_space=pltpu.HBM)
 MIB = 1024 * 1024
+QUERY = slice(0, BLOCK)
+KEY = slice(BLOCK, 2 * BLOCK)
+VALUE = slice(2 * BLOCK, 3 * BLOCK)
+SENT = 3 * BLOCK + BLOCK // 2
+MICROSECOND = 1_150_000_000
+
+
+def cost(flops):
+    return pl.CostEstimate(flops=flops, bytes_accessed=0, transcendentals=0)
 
 
 def in_hbm(value):
@@ -30,30 +39,36 @@
 
 
 def pack_kernel(
-    place_ref, q_ref, k_ref, v_ref, g_ref, w_ref, qkv_ref, gw_ref, held, qkv_held, gw_held, sem
+    place_ref, q_ref, k_ref, v_ref, g_ref, w_ref, qkv_ref, g_out_ref, held, w_held, qkv_held,
+    g_held, sem,
 ):
     count = qkv_ref.shape[0]
     cut = pl.ds(pl.multiple_of(place_ref[0] * BLOCK, BLOCK), BLOCK)
+    half = BLOCK // 2
     loads = [
         pltpu.make_async_copy(source, held.at[n], sem.at[n])
         for n, source in enumerate((g_ref, q_ref, k_ref, v_ref))
     ]
-    loads.append(pltpu.make_async_copy(w_ref.at[:, cut], gw_held.at[count], sem.at[4]))
+    loads.append(pltpu.make_async_copy(w_ref.at[:, cut], w_held, sem.at[4]))
     for copy in loads:
         copy.start()
     loads[0].wait()
+    for j in range(count):
+        g_held[j] = held[0, :, j * BLOCK : (j + 1) * BLOCK]
+    g_out = pltpu.make_async_copy(g_held, g_out_ref, sem.at[5])
+    g_out.start()
     loads[4].wait()
     for j in range(count):
-        gw_held[j] = held[0, :, j * BLOCK : (j + 1) * BLOCK]
-    gw_out = pltpu.make_async_copy(gw_held, gw_ref, sem.at[5])
-    gw_out.start()
+        qkv_held[j, 3 * BLOCK :] = w_held[(j % 2) * half : (j % 2 + 1) * half, :]
     for n in range(3):
         loads[n + 1].wait()
         for j in range(count):
-            qkv_held[j, n] = held[n + 1, :, j * BLOCK : (j + 1) * BLOCK]
+            qkv_held[j, n * BLOCK : (n + 1) * BLOCK] = held[
+                n + 1, :, j * BLOCK : (j + 1) * BLOCK
+            ]
     qkv_out = pltpu.make_async_copy(qkv_held, qkv_ref, sem.at[6])
     qkv_out.start()
-    gw_out.wait()
+    g_out.wait()
     qkv_out.wait()
 
 
@@ -62,18 +77,20 @@
     return pl.pallas_call(
         pack_kernel,
         out_shape=(
-            pltpu.HBM((count, 3, BLOCK, BLOCK), BF16),
-            pltpu.HBM((count + 1, BLOCK, BLOCK), BF16),
+            pltpu.HBM((count, SENT, BLOCK), BF16),
+            pltpu.HBM((count, BLOCK, BLOCK), BF16),
         ),
         in_specs=[SM] + [HBM] * 5,
         out_specs=(HBM, HBM),
         scratch_shapes=[
             pltpu.VMEM((4,) + q.shape, BF16),
-            pltpu.VMEM((count, 3, BLOCK, BLOCK), BF16),
-            pltpu.VMEM((count + 1, BLOCK, BLOCK), BF16),
+            pltpu.VMEM((BLOCK, BLOCK), BF16),
+            pltpu.VMEM((count, SENT, BLOCK), BF16),
+            pltpu.VMEM((count, BLOCK, BLOCK), BF16),
             pltpu.SemaphoreType.DMA((7,)),
         ],
         compiler_params=pltpu.CompilerParams(vmem_limit_bytes=24 * MIB),
+        cost_estimate=cost(3 * MICROSECOND),
         name="pack",
     )(place, *(in_hbm(value) for value in (q, k, v, g, w)))
 
@@ -86,15 +103,15 @@
     block_count, slot_count = blocks_ref.shape
 
     def prepare(c, carry):
-        vt_ref[c] = qkv_ref[c, 2].T
+        vt_ref[c] = qkv_ref[c, VALUE].T
         return carry
 
     lax.fori_loop(0, block_count, prepare, 0, unroll=4)
 
     def one(b):
         owners = [blocks_ref[b, s] for s in range(slot_count)]
-        keys = jnp.concatenate([qkv_ref[c, 1] for c in owners], axis=0)
-        scores = jnp.dot(keys, qkv_ref[b, 0].T, preferred_element_type=F32)
+        keys = jnp.concatenate([qkv_ref[c, KEY] for c in owners], axis=0)
+        scores = jnp.dot(keys, qkv_ref[b, QUERY].T, preferred_element_type=F32)
         top = jnp.max(scores, axis=0, keepdims=True)
         raised = jnp.exp2((scores - top) * (INV_ROOT * LOG2E))
         total = jnp.sum(raised, axis=0, keepdims=True)
@@ -126,6 +143,7 @@
         out_specs=(VM, VM, VM),
         scratch_shapes=[pltpu.VMEM((count, HEAD_DIM, BLOCK), BF16)],
         compiler_params=pltpu.CompilerParams(vmem_limit_bytes=24 * MIB),
+        cost_estimate=cost(12 * MICROSECOND),
         name="forward",
     )(blocks, qkv)
 
@@ -176,6 +194,7 @@
         out_specs=(VM, VM),
         scratch_shapes=buf + [pltpu.VMEM((mine.shape[1], 2 * HEAD_DIM), BF16)] + sem,
         compiler_params=pltpu.CompilerParams(vmem_limit_bytes=24 * MIB),
+        cost_estimate=cost(4 * MICROSECOND),
         name="attn_grad",
     )(mine, theirs, *(in_hbm(shard) for shard in shards))
 
@@ -220,6 +239,7 @@
         out_specs=(VM, VM),
         scratch_shapes=buf + [pltpu.VMEM((2 * HEAD_DIM, chunks * BLOCK), F32)] + sem,
         compiler_params=pltpu.CompilerParams(vmem_limit_bytes=24 * MIB),
+        cost_estimate=cost(4 * MICROSECOND),
         name="weight_grad",
     )(place, attn_t, other_t, *(in_hbm(shard) for shard in shards))
 
@@ -233,7 +253,7 @@
     zero = jnp.zeros((BLOCK, HEAD_DIM), BF16)
 
     def prepare(c, carry):
-        k_one, v_one = qkv_ref[c, 1], qkv_ref[c, 2]
+        k_one, v_one = qkv_ref[c, KEY], qkv_ref[c, VALUE]
         kv_ref[rows_of(c), :] = jnp.concatenate([k_one, v_one], axis=1)
         kt_ref[c] = k_one.T
         acc_ref[rows_of(c), :] = jnp.zeros((BLOCK, 2 * HEAD_DIM), F32)
@@ -247,7 +267,7 @@
     theirs_ref[first:] = theirs_late_ref[...]
 
     def one(b, d_one):
-        q_one = qkv_ref[b, 0]
+        q_one = qkv_ref[b, QUERY]
         q_t, d_t = q_one.T, d_one.T
         owners = [blocks_ref[b, s] for s in range(slot_count)]
         right = jnp.concatenate(
@@ -307,110 +327,79 @@
             pltpu.VMEM((count // 2, BLOCK, HEAD_DIM), BF16),
         ],
         compiler_params=pltpu.CompilerParams(vmem_limit_bytes=24 * MIB),
+        cost_estimate=cost(13 * MICROSECOND),
         name="backward",
     )(blocks, place, qkv, attn_t, lse, *attn_grads)
 
 
-def collect_kernel(spots, *refs):
-    w_refs, out_ref, sem = refs[: len(spots)], refs[-2], refs[-1]
-    copies = [
-        pltpu.make_async_copy(w_ref.at[spot], out_ref.at[n], sem.at[n])
-        for n, (w_ref, spot) in enumerate(zip(w_refs, spots))
-    ]
-    for copy in copies:
-        copy.start()
-    for copy in copies:
-        copy.wait()
-
-
-def collect(spots, arrays):
-    return pl.pallas_call(
-        functools.partial(collect_kernel, spots),
-        out_shape=like(len(spots), BLOCK, BLOCK),
-        in_specs=[HBM] * len(spots),
+def project_kernel(pieces, cols_ref, core_ref, mine_ref, *refs):
+    own_refs, other_refs = refs[: len(pieces)], refs[len(pieces) : 2 * len(pieces)]
+    layer_ref, rows_buf = refs[2 * len(pieces) :]
+    count = mine_ref.shape[0]
+    for h in range(count):
+        rows_buf[:, h * HEAD_DIM : (h + 1) * HEAD_DIM] = mine_ref[h]
+    rows = rows_buf[...]
+    lower = core_ref[0] == 0
+    groups = max(high for _, _, high in pieces)
+    for n, (shift, low, high) in enumerate(pieces):
+        for j in range(0, high - low, 2):
+            weights = []
+            for t in (j, j + 1):
+                own, other = own_refs[n][t], other_refs[n][t]
+                first = jnp.where(lower, own, other)
+                second = jnp.where(lower, other, own)
+                weights.append(
+                    jnp.concatenate([first, second], axis=1).reshape(count * HEAD_DIM, BLOCK)
+                )
+            found = jnp.dot(
+                rows, jnp.concatenate(weights, axis=1), preferred_element_type=F32
+            ).astype(BF16)
+            for t in range(2):
+                at = pl.multiple_of(cols_ref[shift * groups + low + j + t] * BLOCK, BLOCK)
+                layer_ref[:, pl.ds(at, BLOCK)] = found[:, t * BLOCK : (t + 1) * BLOCK]
+
+
+def project(pieces, cols, core, mine, own, other):
+    count = mine.shape[0]
+    return pl.pallas_call(
+        functools.partial(project_kernel, pieces),
+        out_shape=like(BLOCK, cols.shape[0] * BLOCK),
+        in_specs=[SM, SM] + [VM] * (1 + 2 * len(pieces)),
         out_specs=VM,
-        scratch_shapes=[pltpu.SemaphoreType.DMA((len(spots),))],
-        name="collect",
-    )(*(in_hbm(array) for array in arrays))
-
-
-def project_kernel(groups, heads_ref, cols_ref, *refs):
-    row_refs, w_refs = refs[:groups], refs[groups : 3 * groups]
-    part_refs, rows_buf = refs[3 * groups : 4 * groups], refs[-1]
-    half = w_refs[0].shape[0]
-    for i in range(groups):
-        for e in range(2 * half):
-            rows_buf[i * BLOCK : (i + 1) * BLOCK, e * HEAD_DIM : (e + 1) * HEAD_DIM] = row_refs[i][
-                heads_ref[e]
-            ]
-    rows = rows_buf[...]
-    for j in range(0, groups, 2):
-        weights = jnp.concatenate(
-            [
-                jnp.concatenate(
-                    [w_refs[side * groups + t][...].reshape(half * HEAD_DIM, BLOCK) for side in range(2)],
-                    axis=0,
-                )
-                for t in (j, j + 1)
-            ],
-            axis=1,
-        )
-        found = jnp.dot(rows, weights, preferred_element_type=F32).astype(BF16)
-        for n in range(2):
-            at = pl.ds(pl.multiple_of(cols_ref[j + n] * BLOCK, BLOCK), BLOCK)
-            for i in range(groups):
-                part_refs[i][:, at] = found[
-                    i * BLOCK : (i + 1) * BLOCK, n * BLOCK : (n + 1) * BLOCK
-                ]
-
-
-def project(heads, cols, rows, weights):
-    groups = len(rows)
-    width = rows[0].shape[0] * HEAD_DIM
-    return pl.pallas_call(
-        functools.partial(project_kernel, groups),
-        out_shape=(like(BLOCK, groups * BLOCK),) * groups,
-        in_specs=[SM, SM] + [VM] * (3 * groups),
-        out_specs=(VM,) * groups,
-        scratch_shapes=[pltpu.VMEM((groups * BLOCK, width), BF16)],
-        compiler_params=pltpu.CompilerParams(vmem_limit_bytes=24 * MIB),
+        scratch_shapes=[pltpu.VMEM((BLOCK, count * HEAD_DIM), BF16)],
+        compiler_params=pltpu.CompilerParams(vmem_limit_bytes=32 * MIB),
+        cost_estimate=cost(6 * MICROSECOND),
         name="project",
-    )(heads, cols, *rows, *weights)
-
-
-def unpack_kernel(groups, cols_ref, places_ref, grads_ref, *refs):
-    layer_refs, pg_refs = refs[:groups], refs[groups : 2 * groups]
-    layer_ref, dq_ref, dk_ref, dv_ref, pg_ref = refs[2 * groups :]
+    )(cols, core, mine, *own, *other)
+
+
+def unpack_kernel(groups, places_ref, grads_ref, *refs):
+    part_refs = refs[:groups]
+    dq_ref, dk_ref, dv_ref, pg_ref = refs[groups:]
     for h in range(grads_ref.shape[0]):
         cols = slice(h * HEAD_DIM, (h + 1) * HEAD_DIM)
         dq_ref[:, cols] = grads_ref[h, 0]
         dk_ref[:, cols] = grads_ref[h, 1]
         dv_ref[:, cols] = grads_ref[h, 2]
-    wide = layer_refs[0].shape[1]
+    wide = groups * BLOCK
     for i in range(groups):
-        layer_ref[:, pl.ds(pl.multiple_of(places_ref[i] * wide, wide), wide)] = layer_refs[i][...]
-        for j in range(groups):
-            at = pl.multiple_of(cols_ref[i * groups + j] * BLOCK, BLOCK)
-            pg_ref[:, pl.ds(at, BLOCK)] = pg_refs[i][j].astype(F32)
-
-
-def unpack(cols, places, grads, layers, pg_pieces):
+        for t in range(groups):
+            at = pl.ds(pl.multiple_of(places_ref[i] * wide + t * BLOCK, BLOCK), BLOCK)
+            pg_ref[:, at] = part_refs[i][t].astype(F32)
+
+
+def unpack(places, grads, parts):
     wide = like(BLOCK, grads.shape[0] * HEAD_DIM)
-    groups = len(pg_pieces)
+    groups = len(parts)
     return pl.pallas_call(
         functools.partial(unpack_kernel, groups),
-        out_shape=(
-            like(BLOCK, groups * layers[0].shape[1]),
-            wide,
-            wide,
-            wide,
-            like(HEAD_DIM, groups * groups * BLOCK, dtype=F32),
-        ),
-        in_specs=[SM, SM, VM] + [VM] * (2 * groups),
-        out_specs=(VM,) * 5,
+        out_shape=(wide, wide, wide, like(HEAD_DIM, groups * groups * BLOCK, dtype=F32)),
+        in_specs=[SM, VM] + [VM] * groups,
+        out_specs=(VM,) * 4,
         compiler_params=pltpu.CompilerParams(vmem_limit_bytes=24 * MIB),
+        cost_estimate=cost(3 * MICROSECOND),
         name="unpack",
-    )(cols, places, grads, *layers, *pg_pieces)
+    )(places, grads, *parts)
 
 
 def shifted(value, axis, by):
@@ -455,22 +444,28 @@
     shifts, parts, shards = [0], [(0, 0, chunks)], [gw]
     up = down = gw
     for k in range(1, chips // 2):
-        if k == chips // 2 - 1:
+        if k == 2:
             qkv, up, down = lax.optimization_barrier((qkv, up, down))
+            w_near = from_others(qkv[:, 3 * BLOCK :], "y")
+        if k == 3:
+            up, down, w_near = lax.optimization_barrier((up, down, w_near))
+            w_here = jnp.stack(w_near)
+            w_up, w_down = shifted(w_here, "x", 1), shifted(w_here, "x", -1)
         up, down = shifted(up, "z", 1), shifted(down, "z", -1)
         for shift, array in ((-k, up), (k, down)):
             parts.append((len(shifts), 0, chunks))
             shifts.append(shift)
             shards.append(array)
     cut = chunks // 2
+    attn, attn_t, lse = forward(blocks, qkv)
+    attn, up, down = lax.optimization_barrier((attn, up, down))
+    shards += [shifted(up[:cut], "z", 1), shifted(down[cut:], "z", -1)]
     parts += [(len(shifts), 0, cut), (len(shifts), cut, chunks)]
     shifts.append(chips // 2)
-    shards += [shifted(up[:cut], "z", 1), shifted(down[cut:], "z", -1)]
     parts = tuple(parts)
     steps = jnp.array([s % chips for s in shifts], jnp.int32)
     spot = jnp.concatenate([jnp.stack([z, core]), steps])
 
-    attn, attn_t, lse = forward(blocks, qkv)
     other_t = swapped(
         lax.dynamic_index_in_dim(
             attn_t.reshape((chips, 2) + attn_t.shape[1:]), 1 - core, 1, keepdims=False
@@ -478,35 +473,33 @@
     )
     early, theirs_early = attn_grad(parts[:-2], out_proj, proj_theirs, shards[:-2])
     theirs_early = swapped(theirs_early)
-    attn, shards[-2], shards[-1] = lax.optimization_barrier((attn, shards[-2], shards[-1]))
+    attn, early, shards[-2], shards[-1], w_up, w_down = lax.optimization_barrier(
+        (attn, early, shards[-2], shards[-1], w_up, w_down)
+    )
     attn_rows = lax.all_to_all(attn, seq, split_axis=0, concat_axis=0, tiled=True)
     late, theirs_late = attn_grad(
         ((0, 0, cut), (0, cut, chunks)), out_proj, proj_theirs, shards[-2:]
     )
     theirs_late = swapped(theirs_late)
-    spots = tuple([chunks] * (chips - 1) + [chunks - cut])
-    own_weights = collect(spots, shards[: chips - 1] + shards[-1:])
-    theirs_late, own_weights = lax.optimization_barrier((theirs_late, own_weights))
-    weights = from_others(own_weights, "y")
+    middle = groups // 2
+    w_far = [shifted(w_up[:middle], "x", 1), shifted(w_down[middle:], "x", -1)]
     grads = backward(blocks, spot, qkv, attn_t, lse, early, theirs_early, late, theirs_late)
+    grads, attn_rows, w_far, other_t = lax.optimization_barrier((grads, attn_rows, w_far, other_t))
     grad_rows = lax.all_to_all(grads, seq, split_axis=0, concat_axis=0, tiled=True)
 
-    weights += [swapped(piece) for piece in weights]
-    rows = from_others(attn_rows, "x")
-    owner = 2 * ((z + steps) % chips)
-    heads = jnp.concatenate([owner + core, owner + 1 - core])
-    found = project(heads, (y - index) % groups, rows, weights)
-    layers = [part if i == 0 else shifted(part, "x", -i) for i, part in enumerate(found)]
-
-    other_t, _ = lax.optimization_barrier((other_t, rows))
     pg_mine, pg_theirs = weight_grad(parts, spot, attn_t, other_t, chunks, shards)
     pg = (pg_mine.astype(F32) + swapped(pg_theirs).astype(F32)).astype(BF16)
     pg = spread(pg.reshape((groups, groups) + pg.shape[1:]), "x").astype(BF16)
-    pg = (spread(pg, "y") * (1.0 / math.sqrt(tokens))).astype(BF16)
-    pg_pieces = from_others(jnp.stack(from_others(pg, "y")), "x")
+    pieces = ((0, 0, groups), (1, 0, groups), (groups - 1, 0, groups))
+    pieces += ((middle, 0, middle), (middle, middle, groups))
+    weights = [w_here, w_up, w_down] + w_far
     cols = (((x - index) % groups)[:, None] * groups + ((y - index) % groups)[None]).reshape(-1)
-
-    layer, dq, dk, dv, proj_grad = unpack(cols, (x + index) % groups, grad_rows, layers, pg_pieces)
+    layer = project(pieces, cols, core[None], attn_rows, weights, [swapped(w) for w in weights])
+    pg, layer = lax.optimization_barrier((pg, layer))
+    pg = sum(piece.astype(F32) for piece in from_others(pg, "y"))
+    pg = (pg * (1.0 / math.sqrt(tokens))).astype(BF16)
+    pg_pieces = from_others(pg, "x")
+    dq, dk, dv, proj_grad = unpack((x - index) % groups, grad_rows, pg_pieces)
     return layer[None], dq[None], dk[None], dv[None], proj_grad
 
 

time: 220 us -> 199 us (0.905); the launches traced: 216 us -> 198 us
  waiting for transfers between devices: 94.2 us -> 79.1 us
  starting transfers between devices: 64 us -> 60.4 us
    all_to_all x1, waiting for transfers between devices: 8.42 us -> 0.01 us  [body(): lax.all_to_all(attn, seq, split_axis=0, concat_axis=0, tiled=True)]
    ppermute x29 -> x24, waiting for transfers between devices: 82.5 us -> 74.2 us  [shifted(): lax.ppermute(value, axis, [(i, (i + by) % size) for i in range(size)])]
    ppermute x29 -> x24, starting transfers between devices: 36.1 us -> 28.3 us  [shifted(): lax.ppermute(value, axis, [(i, (i + by) % size) for i in range(size)])]
    ppermute x9 -> x10, starting transfers between devices: 4.92 us -> 9.1 us  [swapped(): return lax.ppermute(value, 'c', [(0, 1), (1, 0)])]
    all_to_all x1, starting transfers between devices: 9.12 us -> 5.09 us  [body(): lax.all_to_all(attn, seq, split_axis=0, concat_axis=0, tiled=True)]
    all_to_all x1, starting transfers between devices: 3.74 us -> 7.76 us  [body(): lax.all_to_all(grads, seq, split_axis=0, concat_axis=0, tiled=True)]
    slice x0 -> x3, local copies, waits for them, and re-layouts: none -> 2.24 us  [the longest x2 2.22 us: body(): w_far = [shifted(w_up[:middle], 'x', 1), shifted(w_down[middle:], 'x', -1)]]
    ppermute x9 -> x10, waiting for transfers between devices: 3.19 us -> 4.84 us  [swapped(): return lax.ppermute(value, 'c', [(0, 1), (1, 0)])]
  transfers between devices with their start and end apart: 41 -> 37, of which waited for: 12 -> 13; matrix products, arithmetic and copies ran while one was open for 3% -> 3% of each run, Pallas kernels for 19% -> 21%
where the time goes in v3:
time: 199 us; the launch traced here: 198 us
  waiting for transfers between devices  79.1 us (40%)
  starting transfers between devices  60.4 us (30%)
  Pallas kernels  46.9 us (24%)
  local copies, waits for them, and re-layouts  8.15 us (4%)
  other arithmetic  2.92 us (1%)
    ppermute x24, waiting for transfers between devices, shifted(): lax.ppermute(value, axis, [(i, (i + by) % size) for i in range(size)])  74.2 us
    ppermute x24, starting transfers between devices, shifted(): lax.ppermute(value, axis, [(i, (i + by) % size) for i in range(size)])  28.3 us
    pallas_call x1, Pallas kernels, backward(): pl.pallas_call(backward_kernel, out_shape=like(count, 3, BLOCK, HEAD_DIM)...  13.6 us
    pallas_call x1, Pallas kernels, forward(): pl.pallas_call(forward_kernel, out_shape=(like(count, BLOCK, HEAD_DIM), l...  11.7 us
    all_to_all x1, starting transfers between devices, body(): qkv = lax.all_to_all(qkv_out, seq, split_axis=0, concat_axis=0, tiled=True)  10.1 us
    ppermute x10, starting transfers between devices, swapped(): return lax.ppermute(value, 'c', [(0, 1), (1, 0)])  9.1 us
    all_to_all x1, starting transfers between devices, body(): lax.all_to_all(grads, seq, split_axis=0, concat_axis=0, tiled=True)  7.76 us
    pallas_call x2, Pallas kernels, attn_grad(): pl.pallas_call(functools.partial(attn_grad_kernel, parts), out_shape=(lik...  6.11 us
  transfers between devices with their start and end apart: 37, of which 13 were waited for; matrix products, arithmetic and copies ran while one was open for 3% of the time, Pallas kernels for 21%

profile of v3, /device:TPU:1, one launch (start us, length us, event | category | flops | bytes accessed | tf_op | source)
XLA Modules:
  0.0 198.4 jit_solution(15789180445682181874)
XLA Ops:
  0.6 3.0 %pack.1 = (bf16[16,448,128]{2,1,0:T(8,128)(2,1)}, bf16[16,128,128]{2,1,0:T(8,128)(2,1)}) custom-call(s32[1]{0:T(128)} %bitcast.3.place_ref, bf16[128,2048]{1,0:T(8,128)(2,1)} %bitcast.39, bf16[128,2048]{1,0:T(8,128)(2,1)} %bitcast.40, bf16[128,2048]{1,0:T(8,128)(2,1)} %bitcast.41, bf16[128,2048]{1,0:T(8,128)(2,1)} %bitcast.42, bf16[128,2048]{1,0:T(8,128)(2,1)} %mine_ref.3), custom_call_target="tpu_custom_call" | custom-call | flops 3449999872 | tf_op jit(solution)/shard_map/pack/pallas_call | solution.py:77
  3.7 10.1 %all-to-all-start = ((bf16[16,448,128]{2,1,0:T(8,128)(2,1)}), bf16[16,448,128]{2,1,0:T(8,128)(2,1)S(1)}, u32[]{:S(2)}, u32[]{:S(2)}) async-start(bf16[16,448,128]{2,1,0:T(8,128)(2,1)} %get-tuple-element.45), calls=%async_computation | async-start | bytes 3670016 | tf_op jit(solution)/shard_map/all_to_all | solution.py:441
  13.8 1.5 collective-permute-start
  15.3 1.3 collective-permute-start.1
  16.6 51.5 %collective-permute-done.refs_1_ = bf16[16,128,128]{2,1,0:T(8,128)(2,1)} collective-permute-done((bf16[16,128,128]{2,1,0:T(8,128)(2,1)S(1)}, bf16[16,128,128]{2,1,0:T(8,128)(2,1)}, u32[]{:S(2)}, u32[]{:S(2)}) %collective-permute-start) | collective-permute-done | bytes 524320 | tf_op jit(solution)/shard_map/ppermute | solution.py:407
  68.3 2.5 %collective-permute-start.3 = (bf16[16,128,128]{2,1,0:T(8,128)(2,1)}, bf16[16,128,128]{2,1,0:T(8,128)(2,1)}, u32[]{:S(2)}, u32[]{:S(2)}) collective-permute-start(bf16[16,128,128]{2,1,0:T(8,128)(2,1)} %collective-permute-done.1.refs_2_), channel_id=1, source_target_pairs={{0,224},{32,0},{64,32},{96,64},{128,96},{160,128},{192,160},{224,1... | collective-permute-start | bytes 1572872 | tf_op jit(solution)/shard_map/ppermute | solution.py:407
  70.8 1.4 collective-permute-start.4
  72.2 2.6 %collective-permute-start.5 = (bf16[16,64,128]{2,1,0:T(8,128)(2,1)S(1)}, bf16[16,64,128]{2,1,0:T(8,128)(2,1)S(1)}, u32[]{:S(2)}, u32[]{:S(2)}) collective-permute-start(bf16[16,64,128]{2,1,0:T(8,128)(2,1)S(1)} %slice.15), channel_id=1, source_target_pairs={{0,2},{1,3},{2,0},{3,1},{4,6},{5,7},{6,4},{7,5},{8,10},{9,11},{10,... | collective-permute-start | bytes 786440 | tf_op jit(solution)/shard_map/ppermute | solution.py:407
  74.8 1.1 collective-permute-start.6
  76.0 2.7 %collective-permute-done.4 = bf16[16,64,128]{2,1,0:T(8,128)(2,1)S(1)} collective-permute-done((bf16[16,64,128]{2,1,0:T(8,128)(2,1)S(1)}, bf16[16,64,128]{2,1,0:T(8,128)(2,1)S(1)}, u32[]{:S(2)}, u32[]{:S(2)}) %collective-permute-start.4) | collective-permute-done | bytes 262176 | tf_op jit(solution)/shard_map/ppermute | solution.py:407
  78.7 3.0 %collective-permute-start.9 = (bf16[128,2048]{1,0:T(8,128)(2,1)S(1)}, bf16[128,2048]{1,0:T(8,128)(2,1)S(1)}, u32[]{:S(2)}, u32[]{:S(2)}) collective-permute-start(bf16[128,2048]{1,0:T(8,128)(2,1)S(1)} %copy-done.6), channel_id=1, source_target_pairs={{0,16},{16,0},{1,17},{17,1},{2,18},{18,2},{3,19},{19,3},{4,20},{20... | collective-permute-start | bytes 1572872 | tf_op jit(solution)/shard_map/ppermute | solution.py:425
  81.6 3.7 %collective-permute-done.5 = bf16[16,64,128]{2,1,0:T(8,128)(2,1)S(1)} collective-permute-done((bf16[16,64,128]{2,1,0:T(8,128)(2,1)S(1)}, bf16[16,64,128]{2,1,0:T(8,128)(2,1)S(1)}, u32[]{:S(2)}, u32[]{:S(2)}) %collective-permute-start.5) | collective-permute-done | bytes 262176 | tf_op jit(solution)/shard_map/ppermute | solution.py:407
  86.1 1.3 pad_maximum_fusion.refs_0_
  87.4 1.3 collective-permute-start.12
  88.7 1.5 collective-permute-start.13
  90.2 2.7 %collective-permute-start.8 = (bf16[16,128,128]{2,1,0:T(8,128)(2,1)}, bf16[16,128,128]{2,1,0:T(8,128)(2,1)S(1)}, u32[]{:S(2)}, u32[]{:S(2)}) collective-permute-start(bf16[16,128,128]{2,1,0:T(8,128)(2,1)} %collective-permute-done.3.refs_4_), channel_id=1, source_target_pairs={{0,224},{32,0},{64,32},{96,64},{128,96},{160,128},{192,160},{224,1... | collective-permute-start | bytes 1572872 | tf_op jit(solution)/shard_map/ppermute | solution.py:407
  92.8 11.7 %forward.1 = (bf16[16,128,128]{2,1,0:T(8,128)(2,1)S(1)}, bf16[16,128,128]{2,1,0:T(8,128)(2,1)S(1)}, f32[16,1,128]{2,1,0:T(1,128)S(1)}) custom-call(s32[16,8]{1,0:T(8,128)S(1)} %copy.12.blocks_ref, bf16[16,448,128]{2,1,0:T(8,128)(2,1)S(1)} %all-to-all-done.qkv_ref), custom_call_target="tpu_custom_call" | custom-call | flops 13799999488 | tf_op jit(solution)/shard_map/forward/pallas_call | solution.py:135
  104.6 0.8 copy-done.2
  105.5 2.9 %collective-permute-start.11 = (bf16[8,128,128]{2,1,0:T(8,128)(2,1)S(1)}, bf16[8,128,128]{2,1,0:T(8,128)(2,1)S(1)}, u32[]{:S(2)}, u32[]{:S(2)}) collective-permute-start(bf16[8,128,128]{2,1,0:T(8,128)(2,1)S(1)} %slice.17), channel_id=1, source_target_pairs={{0,224},{32,0},{64,32},{96,64},{128,96},{160,128},{192,160},{224,1... | collective-permute-start | bytes 786440 | tf_op jit(solution)/shard_map/ppermute | solution.py:407
  108.4 4.6 %attn_grad.2 = (bf16[7,128,128]{2,1,0:T(8,128)(2,1)S(1)}, bf16[7,128,128]{2,1,0:T(8,128)(2,1)}) custom-call(bf16[128,2048]{1,0:T(8,128)(2,1)S(1)} %copy-done.6, bf16[128,2048]{1,0:T(8,128)(2,1)S(1)} %collective-permute-done.9.theirs_ref, bf16[16,128,128]{2,1,0:T(8,128)(2,1)} %get-tuple-element.46.refs_0_, ...), custom_call_target="tpu_custom_call" | custom-call | flops 4600000000 | tf_op jit(solution)/shard_map/attn_grad/pallas_call | solution.py:190
  113.1 4.1 %collective-permute-start.14 = (bf16[7,128,128]{2,1,0:T(8,128)(2,1)}, bf16[7,128,128]{2,1,0:T(8,128)(2,1)}, u32[]{:S(2)}, u32[]{:S(2)}) collective-permute-start(bf16[7,128,128]{2,1,0:T(8,128)(2,1)} %get-tuple-element.64), channel_id=1, source_target_pairs={{0,16},{16,0},{1,17},{17,1},{2,18},{18,2},{3,19},{19,3},{4,20},{20... | collective-permute-start | bytes 688136 | tf_op jit(solution)/shard_map/ppermute | solution.py:425
  118.0 1.5 attn_grad.3
  119.6 0.7 dynamic-slice_bitcast_fusion
  120.8 5.1 %all-to-all-start.1 = ((bf16[16,128,128]{2,1,0:T(8,128)(2,1)}), bf16[16,128,128]{2,1,0:T(8,128)(2,1)S(1)}, u32[]{:S(2)}, u32[]{:S(2)}) async-start(bf16[16,128,128]{2,1,0:T(8,128)(2,1)} %copy-done.2), calls=%async_computation.1 | async-start | bytes 1048576 | tf_op jit(solution)/shard_map/all_to_all | solution.py:479
  125.9 1.1 slice.18
  127.2 1.1 slice.19
  128.2 2.8 %collective-permute-start.17 = (bf16[2,16,64,128]{3,2,1,0:T(8,128)(2,1)S(1)}, bf16[2,16,64,128]{3,2,1,0:T(8,128)(2,1)}, u32[]{:S(2)}, u32[]{:S(2)}) collective-permute-start(bf16[2,16,64,128]{3,2,1,0:T(8,128)(2,1)S(1)} %slice.19), channel_id=1, source_target_pairs={{0,12},{4,0},{8,4},{12,8},{1,13},{5,1},{9,5},{13,9},{2,14},{6,2},{... | collective-permute-start | bytes 1572872 | tf_op jit(solution)/shard_map/ppermute | solution.py:407
  131.0 13.6 %backward.1 = bf16[16,3,128,128]{3,2,1,0:T(8,128)(2,1)} custom-call(s32[16,8]{1,0:T(8,128)S(1)} %copy.12.blocks_ref, s32[10]{0:T(128)S(1)} %pad_add_fusion.place_ref, bf16[16,448,128]{2,1,0:T(8,128)(2,1)S(1)} %all-to-all-done.qkv_ref, bf16[16,128,128]{2,1,0:T(8,128)(2,1)S(1)} %copy-done.4, f32[16,1,128]{2,1,0:T(1,128)S(1)} %get-tuple-element.49.lse_ref, ...), custom_call_target="tpu_custom_call" | custom-call | flops 14949999616 | tf_op jit(solution)/shard_map/backward/pallas_call | solution.py:317
  144.6 0.8 copy-done.7
  145.4 0.8 copy-done
  146.2 7.8 %all-to-all-start.2 = ((bf16[16,3,128,128]{3,2,1,0:T(8,128)(2,1)}), bf16[16,3,128,128]{3,2,1,0:T(8,128)(2,1)S(1)}, u32[]{:S(2)}, u32[]{:S(2)}) async-start(bf16[16,3,128,128]{3,2,1,0:T(8,128)(2,1)} %backward.1), calls=%async_computation.2 | async-start | bytes 3145728 | tf_op jit(solution)/shard_map/all_to_all | solution.py:488
  154.0 1.0 copy-done.5
  155.0 4.5 %weight_grad.1 = (bf16[16,128,128]{2,1,0:T(8,128)(2,1)S(1)}, bf16[16,128,128]{2,1,0:T(8,128)(2,1)}) custom-call(s32[10]{0:T(128)S(1)} %pad_add_fusion.place_ref, bf16[16,128,128]{2,1,0:T(8,128)(2,1)S(1)} %copy-done.5, bf16[8,128,128]{2,1,0:T(8,128)(2,1)} %collective-permute-done.18.other_ref, bf16[16,128,128]{2,1,0:T(8,128)(2,1)} %get-tuple-element.46.refs_0_, ...), custom_call_target="tpu_custom_call" | custom-call | flops 4600000000 | tf_op jit(solution)/shard_map/weight_grad/pallas_call | solution.py:235
  160.8 1.0 collective-permute-done.19
  162.1 1.3 add_convert_fusion
  163.4 1.2 collective-permute-done.23.refs_5_
  165.2 1.1 collective-permute-done.25.refs_7_
  166.3 0.7 collective-permute-done.26.refs_8_
  167.1 0.7 collective-permute-done.27.refs_9_
  167.8 5.5 %project.1 = bf16[128,2048]{1,0:T(8,128)(2,1)} custom-call(s32[16]{0:T(128)S(1)} %add.119.cols_ref, s32[1]{0:T(128)} %bitcast.1.core_ref, bf16[16,128,128]{2,1,0:T(8,128)(2,1)S(1)} %copy-done.1, bf16[4,16,64,128]{3,2,1,0:T(8,128)(2,1)S(1)} %pad_maximum_fusion.refs_0_, bf16[4,16,64,128]{3,2,1,0:T(8,128)(2,1)} %collective-permute-done.12.refs_1_, ...), custom_call_target="tpu_custom_call" | custom-call | flops 6899999744 | tf_op jit(solution)/shard_map/project/pallas_call | solution.py:364
  173.4 1.3 collective-permute-done.20
  174.8 2.3 %collective-permute-start.30 = (bf16[4,128,128]{2,1,0:T(8,128)(2,1)S(1)}, bf16[4,128,128]{2,1,0:T(8,128)(2,1)S(1)}, u32[]{:S(2)}, u32[]{:S(2)}) collective-permute-start(bf16[4,128,128]{2,1,0:T(8,128)(2,1)S(1)} %fusion.2), channel_id=1, source_target_pairs={{0,3},{1,0},{2,1},{3,2},{4,7},{5,4},{6,5},{7,6},{8,11},{9,8},{10,9... | collective-permute-start | bytes 393224 | tf_op jit(solution)/shard_map/ppermute | solution.py:407
  177.9 2.1 %collective-permute-done.30 = bf16[4,128,128]{2,1,0:T(8,128)(2,1)S(1)} collective-permute-done((bf16[4,128,128]{2,1,0:T(8,128)(2,1)S(1)}, bf16[4,128,128]{2,1,0:T(8,128)(2,1)S(1)}, u32[]{:S(2)}, u32[]{:S(2)}) %collective-permute-start.30) | collective-permute-done | bytes 131104 | tf_op jit(solution)/shard_map/ppermute | solution.py:407
  180.0 2.9 %collective-permute-done.29 = bf16[4,128,128]{2,1,0:T(8,128)(2,1)S(1)} collective-permute-done((bf16[4,128,128]{2,1,0:T(8,128)(2,1)S(1)}, bf16[4,128,128]{2,1,0:T(8,128)(2,1)S(1)}, u32[]{:S(2)}, u32[]{:S(2)}) %collective-permute-start.29) | collective-permute-done | bytes 131104 | tf_op jit(solution)/shard_map/ppermute | solution.py:407
  182.8 3.9 %collective-permute-done.28 = bf16[4,128,128]{2,1,0:T(8,128)(2,1)S(1)} collective-permute-done((bf16[4,128,128]{2,1,0:T(8,128)(2,1)S(1)}, bf16[4,128,128]{2,1,0:T(8,128)(2,1)S(1)}, u32[]{:S(2)}, u32[]{:S(2)}) %collective-permute-start.28) | collective-permute-done | bytes 131104 | tf_op jit(solution)/shard_map/ppermute | solution.py:407
  187.7 1.9 collective-permute-start.33
  189.6 6.2 %collective-permute-done.31.refs_1_ = bf16[4,128,128]{2,1,0:T(8,128)(2,1)S(1)} collective-permute-done((bf16[4,128,128]{2,1,0:T(8,128)(2,1)S(1)}, bf16[4,128,128]{2,1,0:T(8,128)(2,1)S(1)}, u32[]{:S(2)}, u32[]{:S(2)}) %collective-permute-start.31) | collective-permute-done | bytes 131104 | tf_op jit(solution)/shard_map/ppermute | solution.py:407
  195.9 2.5 %unpack.1 = (bf16[128,2048]{1,0:T(8,128)(2,1)}, bf16[128,2048]{1,0:T(8,128)(2,1)}, bf16[128,2048]{1,0:T(8,128)(2,1)}, f32[128,2048]{1,0:T(8,128)}) custom-call(s32[4]{0:T(128)S(1)} %and_select_fusion.1.places_ref, bf16[16,3,128,128]{3,2,1,0:T(8,128)(2,1)S(1)} %all-to-all-done.2.grads_ref, bf16[4,128,128]{2,1,0:T(8,128)(2,1)S(1)} %multiply_convert_fusion.refs_0_, ...), custom_call_target="tpu_custom_call" | custom-call | flops 3449999872 | tf_op jit(solution)/shard_map/unpack/pallas_call | solution.py:394
  (95 shorter events, 6.9 us)
Async XLA Ops:
  3.7 10.2 %copy-start.19 = (bf16[16,128,128]{2,1,0:T(8,128)(2,1)S(1)}, bf16[16,128,128]{2,1,0:T(8,128)(2,1)}, u32[]{:S(2)}) copy-start(bf16[16,128,128]{2,1,0:T(8,128)(2,1)} %get-tuple-element.46.refs_0_) | copy-start | bytes 1572868
  3.7 72.2 %copy-start.17 = (s32[1,16,8]{1,2,0:T(8,128)S(1)}, s32[1,16,8]{1,2,0:T(8,128)}, u32[]{:S(2)}) copy-start(s32[1,16,8]{1,2,0:T(8,128)} %param.12) | copy-start | bytes 1540
  3.7 72.2 %copy-start.18 = (s32[8]{0:T(128)S(1)}, s32[8]{0:T(128)}, u32[]{:S(2)}) copy-start(s32[8]{0:T(128)} %constant.83.clone) | copy-start | bytes 100
  3.7 75.0 %copy-start.6 = (bf16[128,2048]{1,0:T(8,128)(2,1)S(1)}, bf16[128,2048]{1,0:T(8,128)(2,1)}, u32[]{:S(2)}) copy-start(bf16[128,2048]{1,0:T(8,128)(2,1)} %mine_ref.3) | copy-start | bytes 1572868
  3.7 64.4 %all-to-all-start = ((bf16[16,448,128]{2,1,0:T(8,128)(2,1)}), bf16[16,448,128]{2,1,0:T(8,128)(2,1)S(1)}, u32[]{:S(2)}, u32[]{:S(2)}) async-start(bf16[16,448,128]{2,1,0:T(8,128)(2,1)} %get-tuple-element.45), calls=%async_computation | async-start | bytes 3670016 | tf_op jit(solution)/shard_map/all_to_all | solution.py:441
  13.8 54.2 %collective-permute-start = (bf16[16,128,128]{2,1,0:T(8,128)(2,1)S(1)}, bf16[16,128,128]{2,1,0:T(8,128)(2,1)}, u32[]{:S(2)}, u32[]{:S(2)}) collective-permute-start(bf16[16,128,128]{2,1,0:T(8,128)(2,1)S(1)} %copy-done.19), channel_id=1, source_target_pairs={{0,32},{32,64},{64,96},{96,128},{128,160},{160,192},{192,224},{224... | collective-permute-start | bytes 1572872 | tf_op jit(solution)/shard_map/ppermute | solution.py:407
  15.3 52.8 %collective-permute-start.1 = (bf16[16,128,128]{2,1,0:T(8,128)(2,1)S(1)}, bf16[16,128,128]{2,1,0:T(8,128)(2,1)}, u32[]{:S(2)}, u32[]{:S(2)}) collective-permute-start(bf16[16,128,128]{2,1,0:T(8,128)(2,1)S(1)} %copy-done.19), channel_id=1, source_target_pairs={{0,224},{32,0},{64,32},{96,64},{128,96},{160,128},{192,160},{224,1... | collective-permute-start | bytes 1572872 | tf_op jit(solution)/shard_map/ppermute | solution.py:407
  68.1 17.2 %collective-permute-start.2 = (bf16[16,128,128]{2,1,0:T(8,128)(2,1)}, bf16[16,128,128]{2,1,0:T(8,128)(2,1)}, u32[]{:S(2)}, u32[]{:S(2)}) collective-permute-start(bf16[16,128,128]{2,1,0:T(8,128)(2,1)} %collective-permute-done.refs_1_), channel_id=1, source_target_pairs={{0,32},{32,64},{64,96},{96,128},{128,160},{160,192},{192,224},{224... | collective-permute-start | bytes 1572872 | tf_op jit(solution)/shard_map/ppermute | solution.py:407
  68.3 17.0 %collective-permute-start.3 = (bf16[16,128,128]{2,1,0:T(8,128)(2,1)}, bf16[16,128,128]{2,1,0:T(8,128)(2,1)}, u32[]{:S(2)}, u32[]{:S(2)}) collective-permute-start(bf16[16,128,128]{2,1,0:T(8,128)(2,1)} %collective-permute-done.1.refs_2_), channel_id=1, source_target_pairs={{0,224},{32,0},{64,32},{96,64},{128,96},{160,128},{192,160},{224,1... | collective-permute-start | bytes 1572872 | tf_op jit(solution)/shard_map/ppermute | solution.py:407
  70.8 14.6 %copy-start.11 = (bf16[16,64,128]{2,1,0:T(8,128)(2,1)}, bf16[16,64,128]{2,1,0:T(8,128)(2,1)S(1)}, u32[]{:S(2)}) copy-start(bf16[16,64,128]{2,1,0:T(8,128)(2,1)S(1)} %slice.15) | copy-start | bytes 786436
  70.8 7.9 %collective-permute-start.4 = (bf16[16,64,128]{2,1,0:T(8,128)(2,1)S(1)}, bf16[16,64,128]{2,1,0:T(8,128)(2,1)S(1)}, u32[]{:S(2)}, u32[]{:S(2)}) collective-permute-start(bf16[16,64,128]{2,1,0:T(8,128)(2,1)S(1)} %slice.15), channel_id=1, source_target_pairs={{0,1},{1,2},{2,3},{3,0},{4,5},{5,6},{6,7},{7,4},{8,9},{9,10},{10,1... | collective-permute-start | bytes 786440 | tf_op jit(solution)/shard_map/ppermute | solution.py:407
  72.2 13.1 %collective-permute-start.5 = (bf16[16,64,128]{2,1,0:T(8,128)(2,1)S(1)}, bf16[16,64,128]{2,1,0:T(8,128)(2,1)S(1)}, u32[]{:S(2)}, u32[]{:S(2)}) collective-permute-start(bf16[16,64,128]{2,1,0:T(8,128)(2,1)S(1)} %slice.15), channel_id=1, source_target_pairs={{0,2},{1,3},{2,0},{3,1},{4,6},{5,7},{6,4},{7,5},{8,10},{9,11},{10,... | collective-permute-start | bytes 786440 | tf_op jit(solution)/shard_map/ppermute | solution.py:407
  74.8 10.5 %collective-permute-start.6 = (bf16[16,64,128]{2,1,0:T(8,128)(2,1)S(1)}, bf16[16,64,128]{2,1,0:T(8,128)(2,1)S(1)}, u32[]{:S(2)}, u32[]{:S(2)}) collective-permute-start(bf16[16,64,128]{2,1,0:T(8,128)(2,1)S(1)} %slice.15), channel_id=1, source_target_pairs={{0,3},{1,0},{2,1},{3,2},{4,7},{5,4},{6,5},{7,6},{8,11},{9,8},{10,9... | collective-permute-start | bytes 786440 | tf_op jit(solution)/shard_map/ppermute | solution.py:407
  78.7 6.7 %copy-start.12 = (bf16[16,64,128]{2,1,0:T(8,128)(2,1)}, bf16[16,64,128]{2,1,0:T(8,128)(2,1)S(1)}, u32[]{:S(2)}) copy-start(bf16[16,64,128]{2,1,0:T(8,128)(2,1)S(1)} %collective-permute-done.4) | copy-start | bytes 786436
  78.7 29.7 %collective-permute-start.9 = (bf16[128,2048]{1,0:T(8,128)(2,1)S(1)}, bf16[128,2048]{1,0:T(8,128)(2,1)S(1)}, u32[]{:S(2)}, u32[]{:S(2)}) collective-permute-start(bf16[128,2048]{1,0:T(8,128)(2,1)S(1)} %copy-done.6), channel_id=1, source_target_pairs={{0,16},{16,0},{1,17},{17,1},{2,18},{18,2},{3,19},{19,3},{4,20},{20... | collective-permute-start | bytes 1572872 | tf_op jit(solution)/shard_map/ppermute | solution.py:425
  87.4 29.8 %collective-permute-start.12 = (bf16[4,16,64,128]{3,2,1,0:T(8,128)(2,1)S(1)}, bf16[4,16,64,128]{3,2,1,0:T(8,128)(2,1)}, u32[]{:S(2)}, u32[]{:S(2)}) collective-permute-start(bf16[4,16,64,128]{3,2,1,0:T(8,128)(2,1)S(1)} %pad_maximum_fusion.refs_0_), channel_id=1, source_target_pairs={{0,4},{4,8},{8,12},{12,0},{1,5},{5,9},{9,13},{13,1},{2,6},{6,10},{... | collective-permute-start | bytes 3145736 | tf_op jit(solution)/shard_map/ppermute | solution.py:407
  88.7 28.5 %collective-permute-start.13 = (bf16[4,16,64,128]{3,2,1,0:T(8,128)(2,1)S(1)}, bf16[4,16,64,128]{3,2,1,0:T(8,128)(2,1)}, u32[]{:S(2)}, u32[]{:S(2)}) collective-permute-start(bf16[4,16,64,128]{3,2,1,0:T(8,128)(2,1)S(1)} %pad_maximum_fusion.refs_0_), channel_id=1, source_target_pairs={{0,12},{4,0},{8,4},{12,8},{1,13},{5,1},{9,5},{13,9},{2,14},{6,2},{... | collective-permute-start | bytes 3145736 | tf_op jit(solution)/shard_map/ppermute | solution.py:407
  90.2 15.2 %collective-permute-start.7 = (bf16[16,128,128]{2,1,0:T(8,128)(2,1)}, bf16[16,128,128]{2,1,0:T(8,128)(2,1)S(1)}, u32[]{:S(2)}, u32[]{:S(2)}) collective-permute-start(bf16[16,128,128]{2,1,0:T(8,128)(2,1)} %collective-permute-done.2.refs_3_), channel_id=1, source_target_pairs={{0,32},{32,64},{64,96},{96,128},{128,160},{160,192},{192,224},{224... | collective-permute-start | bytes 1572872 | tf_op jit(solution)/shard_map/ppermute | solution.py:407
  90.2 15.2 %collective-permute-start.8 = (bf16[16,128,128]{2,1,0:T(8,128)(2,1)}, bf16[16,128,128]{2,1,0:T(8,128)(2,1)S(1)}, u32[]{:S(2)}, u32[]{:S(2)}) collective-permute-start(bf16[16,128,128]{2,1,0:T(8,128)(2,1)} %collective-permute-done.3.refs_4_), channel_id=1, source_target_pairs={{0,224},{32,0},{64,32},{96,64},{128,96},{160,128},{192,160},{224,1... | collective-permute-start | bytes 1572872 | tf_op jit(solution)/shard_map/ppermute | solution.py:407
  105.3 14.3 %copy-start.3 = (bf16[16,128,128]{2,1,0:T(8,128)(2,1)}, bf16[16,128,128]{2,1,0:T(8,128)(2,1)S(1)}, u32[]{:S(2)}) copy-start(bf16[16,128,128]{2,1,0:T(8,128)(2,1)S(1)} %get-tuple-element.48.attn_t_ref.attn_ref) | copy-start | bytes 1572868
  105.4 11.8 %collective-permute-start.10 = (bf16[8,128,128]{2,1,0:T(8,128)(2,1)S(1)}, bf16[8,128,128]{2,1,0:T(8,128)(2,1)S(1)}, u32[]{:S(2)}, u32[]{:S(2)}) collective-permute-start(bf16[8,128,128]{2,1,0:T(8,128)(2,1)S(1)} %slice.16), channel_id=1, source_target_pairs={{0,32},{32,64},{64,96},{96,128},{128,160},{160,192},{192,224},{224... | collective-permute-start | bytes 786440 | tf_op jit(solution)/shard_map/ppermute | solution.py:407
  105.5 11.7 %collective-permute-start.11 = (bf16[8,128,128]{2,1,0:T(8,128)(2,1)S(1)}, bf16[8,128,128]{2,1,0:T(8,128)(2,1)S(1)}, u32[]{:S(2)}, u32[]{:S(2)}) collective-permute-start(bf16[8,128,128]{2,1,0:T(8,128)(2,1)S(1)} %slice.17), channel_id=1, source_target_pairs={{0,224},{32,0},{64,32},{96,64},{128,96},{160,128},{192,160},{224,1... | collective-permute-start | bytes 786440 | tf_op jit(solution)/shard_map/ppermute | solution.py:407
  113.1 6.4 %copy-start.9 = (bf16[7,128,128]{2,1,0:T(8,128)(2,1)}, bf16[7,128,128]{2,1,0:T(8,128)(2,1)S(1)}, u32[]{:S(2)}) copy-start(bf16[7,128,128]{2,1,0:T(8,128)(2,1)S(1)} %get-tuple-element.63.early_ref) | copy-start | bytes 688132
  113.1 17.9 %collective-permute-start.14 = (bf16[7,128,128]{2,1,0:T(8,128)(2,1)}, bf16[7,128,128]{2,1,0:T(8,128)(2,1)}, u32[]{:S(2)}, u32[]{:S(2)}) collective-permute-start(bf16[7,128,128]{2,1,0:T(8,128)(2,1)} %get-tuple-element.64), channel_id=1, source_target_pairs={{0,16},{16,0},{1,17},{17,1},{2,18},{18,2},{3,19},{19,3},{4,20},{20... | collective-permute-start | bytes 688136 | tf_op jit(solution)/shard_map/ppermute | solution.py:425
  119.5 11.5 %collective-permute-start.15 = (bf16[1,128,128]{2,1,0:T(8,128)(2,1)S(1)}, bf16[1,128,128]{2,1,0:T(8,128)(2,1)S(1)}, u32[]{:S(2)}, u32[]{:S(2)}) collective-permute-start(bf16[1,128,128]{2,1,0:T(8,128)(2,1)S(1)} %get-tuple-element.68), channel_id=1, source_target_pairs={{0,16},{16,0},{1,17},{17,1},{2,18},{18,2},{3,19},{19,3},{4,20},{20... | collective-permute-start | bytes 98312 | tf_op jit(solution)/shard_map/ppermute | solution.py:425
  120.3 24.3 %collective-permute-start.18 = (bf16[8,128,128]{2,1,0:T(8,128)(2,1)}, bf16[8,128,128]{2,1,0:T(8,128)(2,1)}, u32[]{:S(2)}, u32[]{:S(2)}) collective-permute-start(bf16[8,128,128]{2,1,0:T(8,128)(2,1)} %dynamic-slice_bitcast_fusion), channel_id=1, source_target_pairs={{0,16},{16,0},{1,17},{17,1},{2,18},{18,2},{3,19},{19,3},{4,20},{20... | collective-permute-start | bytes 786440 | tf_op jit(solution)/shard_map/ppermute | solution.py:425
  120.8 24.6 %all-to-all-start.1 = ((bf16[16,128,128]{2,1,0:T(8,128)(2,1)}), bf16[16,128,128]{2,1,0:T(8,128)(2,1)S(1)}, u32[]{:S(2)}, u32[]{:S(2)}) async-start(bf16[16,128,128]{2,1,0:T(8,128)(2,1)} %copy-done.2), calls=%async_computation.1 | async-start | bytes 1048576 | tf_op jit(solution)/shard_map/all_to_all | solution.py:479
  125.9 5.1 %copy-start.4 = (bf16[16,128,128]{2,1,0:T(8,128)(2,1)S(1)}, bf16[16,128,128]{2,1,0:T(8,128)(2,1)}, u32[]{:S(2)}) copy-start(bf16[16,128,128]{2,1,0:T(8,128)(2,1)} %copy-done.3) | copy-start | bytes 1572868
  127.1 17.5 %collective-permute-start.16 = (bf16[2,16,64,128]{3,2,1,0:T(8,128)(2,1)S(1)}, bf16[2,16,64,128]{3,2,1,0:T(8,128)(2,1)S(1)}, u32[]{:S(2)}, u32[]{:S(2)}) collective-permute-start(bf16[2,16,64,128]{3,2,1,0:T(8,128)(2,1)S(1)} %slice.18), channel_id=1, source_target_pairs={{0,4},{4,8},{8,12},{12,0},{1,5},{5,9},{9,13},{13,1},{2,6},{6,10},{... | collective-permute-start | bytes 1572872 | tf_op jit(solution)/shard_map/ppermute | solution.py:407
  128.2 17.2 %collective-permute-start.17 = (bf16[2,16,64,128]{3,2,1,0:T(8,128)(2,1)S(1)}, bf16[2,16,64,128]{3,2,1,0:T(8,128)(2,1)}, u32[]{:S(2)}, u32[]{:S(2)}) collective-permute-start(bf16[2,16,64,128]{3,2,1,0:T(8,128)(2,1)S(1)} %slice.19), channel_id=1, source_target_pairs={{0,12},{4,0},{8,4},{12,8},{1,13},{5,1},{9,5},{13,9},{2,14},{6,2},{... | collective-permute-start | bytes 1572872 | tf_op jit(solution)/shard_map/ppermute | solution.py:407
  146.2 49.7 %all-to-all-start.2 = ((bf16[16,3,128,128]{3,2,1,0:T(8,128)(2,1)}), bf16[16,3,128,128]{3,2,1,0:T(8,128)(2,1)S(1)}, u32[]{:S(2)}, u32[]{:S(2)}) async-start(bf16[16,3,128,128]{3,2,1,0:T(8,128)(2,1)} %backward.1), calls=%async_computation.2 | async-start | bytes 3145728 | tf_op jit(solution)/shard_map/all_to_all | solution.py:488
  159.5 2.3 %collective-permute-start.19 = (bf16[16,128,128]{2,1,0:T(8,128)(2,1)}, bf16[16,128,128]{2,1,0:T(8,128)(2,1)}, u32[]{:S(2)}, u32[]{:S(2)}) collective-permute-start(bf16[16,128,128]{2,1,0:T(8,128)(2,1)} %get-tuple-element.74), channel_id=1, source_target_pairs={{0,16},{16,0},{1,17},{17,1},{2,18},{18,2},{3,19},{19,3},{4,20},{20... | collective-permute-start | bytes 1572872 | tf_op jit(solution)/shard_map/ppermute | solution.py:425
  159.7 4.9 %collective-permute-start.23 = (bf16[4,16,64,128]{3,2,1,0:T(8,128)(2,1)S(1)}, bf16[4,16,64,128]{3,2,1,0:T(8,128)(2,1)}, u32[]{:S(2)}, u32[]{:S(2)}) collective-permute-start(bf16[4,16,64,128]{3,2,1,0:T(8,128)(2,1)S(1)} %pad_maximum_fusion.refs_0_), channel_id=1, source_target_pairs={{0,16},{16,0},{1,17},{17,1},{2,18},{18,2},{3,19},{19,3},{4,20},{20... | collective-permute-start | bytes 3145736 | tf_op jit(solution)/shard_map/ppermute | solution.py:425
  160.1 4.9 %collective-permute-start.24 = (bf16[4,16,64,128]{3,2,1,0:T(8,128)(2,1)}, bf16[4,16,64,128]{3,2,1,0:T(8,128)(2,1)}, u32[]{:S(2)}, u32[]{:S(2)}) collective-permute-start(bf16[4,16,64,128]{3,2,1,0:T(8,128)(2,1)} %collective-permute-done.12.refs_1_), channel_id=1, source_target_pairs={{0,16},{16,0},{1,17},{17,1},{2,18},{18,2},{3,19},{19,3},{4,20},{20... | collective-permute-start | bytes 3145736 | tf_op jit(solution)/shard_map/ppermute | solution.py:425
  160.2 6.1 %collective-permute-start.25 = (bf16[4,16,64,128]{3,2,1,0:T(8,128)(2,1)}, bf16[4,16,64,128]{3,2,1,0:T(8,128)(2,1)}, u32[]{:S(2)}, u32[]{:S(2)}) collective-permute-start(bf16[4,16,64,128]{3,2,1,0:T(8,128)(2,1)} %collective-permute-done.13.refs_2_), channel_id=1, source_target_pairs={{0,16},{16,0},{1,17},{17,1},{2,18},{18,2},{3,19},{19,3},{4,20},{20... | collective-permute-start | bytes 3145736 | tf_op jit(solution)/shard_map/ppermute | solution.py:425
  160.6 6.5 %collective-permute-start.26 = (bf16[2,16,64,128]{3,2,1,0:T(8,128)(2,1)}, bf16[2,16,64,128]{3,2,1,0:T(8,128)(2,1)}, u32[]{:S(2)}, u32[]{:S(2)}) collective-permute-start(bf16[2,16,64,128]{3,2,1,0:T(8,128)(2,1)} %copy-done.7), channel_id=1, source_target_pairs={{0,16},{16,0},{1,17},{17,1},{2,18},{18,2},{3,19},{19,3},{4,20},{20... | collective-permute-start | bytes 1572872 | tf_op jit(solution)/shard_map/ppermute | solution.py:425
  161.8 6.0 %collective-permute-start.27 = (bf16[2,16,64,128]{3,2,1,0:T(8,128)(2,1)}, bf16[2,16,64,128]{3,2,1,0:T(8,128)(2,1)}, u32[]{:S(2)}, u32[]{:S(2)}) collective-permute-start(bf16[2,16,64,128]{3,2,1,0:T(8,128)(2,1)} %collective-permute-done.17.refs_4_), channel_id=1, source_target_pairs={{0,16},{16,0},{1,17},{17,1},{2,18},{18,2},{3,19},{19,3},{4,20},{20... | collective-permute-start | bytes 1572872 | tf_op jit(solution)/shard_map/ppermute | solution.py:425
  162.1 5.7 %copy-start.1 = (bf16[16,128,128]{2,1,0:T(8,128)(2,1)S(1)}, bf16[16,128,128]{2,1,0:T(8,128)(2,1)}, u32[]{:S(2)}) copy-start(bf16[16,128,128]{2,1,0:T(8,128)(2,1)} %copy-done) | copy-start | bytes 1572868
  162.1 5.7 %copy-start.8 = (bf16[2,16,64,128]{3,2,1,0:T(8,128)(2,1)S(1)}, bf16[2,16,64,128]{3,2,1,0:T(8,128)(2,1)}, u32[]{:S(2)}) copy-start(bf16[2,16,64,128]{3,2,1,0:T(8,128)(2,1)} %copy-done.7) | copy-start | bytes 1572868
  164.6 8.8 %collective-permute-start.22 = (bf16[4,128,128]{2,1,0:T(8,128)(2,1)S(1)}, bf16[4,128,128]{2,1,0:T(8,128)(2,1)S(1)}, u32[]{:S(2)}, u32[]{:S(2)}) collective-permute-start(bf16[4,128,128]{2,1,0:T(8,128)(2,1)S(1)} %get-tuple-element.86), channel_id=1, source_target_pairs={{0,12},{4,0},{8,4},{12,8},{1,13},{5,1},{9,5},{13,9},{2,14},{6,2},{... | collective-permute-start | bytes 393224 | tf_op jit(solution)/shard_map/ppermute | solution.py:407
  164.9 8.4 %collective-permute-start.21 = (bf16[4,128,128]{2,1,0:T(8,128)(2,1)S(1)}, bf16[4,128,128]{2,1,0:T(8,128)(2,1)S(1)}, u32[]{:S(2)}, u32[]{:S(2)}) collective-permute-start(bf16[4,128,128]{2,1,0:T(8,128)(2,1)S(1)} %get-tuple-element.87), channel_id=1, source_target_pairs={{0,8},{4,12},{8,0},{12,4},{1,9},{5,13},{9,1},{13,5},{2,10},{6,14},... | collective-permute-start | bytes 393224 | tf_op jit(solution)/shard_map/ppermute | solution.py:407
  166.3 8.4 %collective-permute-start.20 = (bf16[4,128,128]{2,1,0:T(8,128)(2,1)S(1)}, bf16[4,128,128]{2,1,0:T(8,128)(2,1)S(1)}, u32[]{:S(2)}, u32[]{:S(2)}) collective-permute-start(bf16[4,128,128]{2,1,0:T(8,128)(2,1)S(1)} %get-tuple-element.85), channel_id=1, source_target_pairs={{0,4},{4,8},{8,12},{12,0},{1,5},{5,9},{9,13},{13,1},{2,6},{6,10},{... | collective-permute-start | bytes 393224 | tf_op jit(solution)/shard_map/ppermute | solution.py:407
  174.8 5.2 %collective-permute-start.30 = (bf16[4,128,128]{2,1,0:T(8,128)(2,1)S(1)}, bf16[4,128,128]{2,1,0:T(8,128)(2,1)S(1)}, u32[]{:S(2)}, u32[]{:S(2)}) collective-permute-start(bf16[4,128,128]{2,1,0:T(8,128)(2,1)S(1)} %fusion.2), channel_id=1, source_target_pairs={{0,3},{1,0},{2,1},{3,2},{4,7},{5,4},{6,5},{7,6},{8,11},{9,8},{10,9... | collective-permute-start | bytes 393224 | tf_op jit(solution)/shard_map/ppermute | solution.py:407
  177.0 5.8 %collective-permute-start.29 = (bf16[4,128,128]{2,1,0:T(8,128)(2,1)S(1)}, bf16[4,128,128]{2,1,0:T(8,128)(2,1)S(1)}, u32[]{:S(2)}, u32[]{:S(2)}) collective-permute-start(bf16[4,128,128]{2,1,0:T(8,128)(2,1)S(1)} %fusion.2), channel_id=1, source_target_pairs={{0,2},{1,3},{2,0},{3,1},{4,6},{5,7},{6,4},{7,5},{8,10},{9,11},{10,... | collective-permute-start | bytes 393224 | tf_op jit(solution)/shard_map/ppermute | solution.py:407
  177.5 9.3 %collective-permute-start.28 = (bf16[4,128,128]{2,1,0:T(8,128)(2,1)S(1)}, bf16[4,128,128]{2,1,0:T(8,128)(2,1)S(1)}, u32[]{:S(2)}, u32[]{:S(2)}) collective-permute-start(bf16[4,128,128]{2,1,0:T(8,128)(2,1)S(1)} %fusion.2), channel_id=1, source_target_pairs={{0,1},{1,2},{2,3},{3,0},{4,5},{5,6},{6,7},{7,4},{8,9},{9,10},{10,1... | collective-permute-start | bytes 393224 | tf_op jit(solution)/shard_map/ppermute | solution.py:407
  186.9 9.0 %collective-permute-start.31 = (bf16[4,128,128]{2,1,0:T(8,128)(2,1)S(1)}, bf16[4,128,128]{2,1,0:T(8,128)(2,1)S(1)}, u32[]{:S(2)}, u32[]{:S(2)}) collective-permute-start(bf16[4,128,128]{2,1,0:T(8,128)(2,1)S(1)} %multiply_convert_fusion.refs_0_), channel_id=1, source_target_pairs={{0,4},{4,8},{8,12},{12,0},{1,5},{5,9},{9,13},{13,1},{2,6},{6,10},{... | collective-permute-start | bytes 393224 | tf_op jit(solution)/shard_map/ppermute | solution.py:407
  187.0 8.9 %collective-permute-start.32 = (bf16[4,128,128]{2,1,0:T(8,128)(2,1)S(1)}, bf16[4,128,128]{2,1,0:T(8,128)(2,1)S(1)}, u32[]{:S(2)}, u32[]{:S(2)}) collective-permute-start(bf16[4,128,128]{2,1,0:T(8,128)(2,1)S(1)} %multiply_convert_fusion.refs_0_), channel_id=1, source_target_pairs={{0,8},{4,12},{8,0},{12,4},{1,9},{5,13},{9,1},{13,5},{2,10},{6,14},... | collective-permute-start | bytes 393224 | tf_op jit(solution)/shard_map/ppermute | solution.py:407
  187.7 8.2 %collective-permute-start.33 = (bf16[4,128,128]{2,1,0:T(8,128)(2,1)S(1)}, bf16[4,128,128]{2,1,0:T(8,128)(2,1)S(1)}, u32[]{:S(2)}, u32[]{:S(2)}) collective-permute-start(bf16[4,128,128]{2,1,0:T(8,128)(2,1)S(1)} %multiply_convert_fusion.refs_0_), channel_id=1, source_target_pairs={{0,12},{4,0},{8,4},{12,8},{1,13},{5,1},{9,5},{13,9},{2,14},{6,2},{... | collective-permute-start | bytes 393224 | tf_op jit(solution)/shard_map/ppermute | solution.py:407
  (11 other events, 17.6 us)

commit v4 on v3

--- a/solution.py
+++ b/solution.py
@@ -273,33 +273,30 @@
         right = jnp.concatenate(
             [jnp.concatenate([q_t, zero], axis=1), jnp.concatenate([zero, d_t], axis=1)], axis=0
         )
-        kv = jnp.concatenate([kv_ref[rows_of(c), :] for c in owners], axis=0)
-        both = jnp.dot(kv, right, preferred_element_type=F32)
-        scores, prob_grad = both[:, :BLOCK], both[:, BLOCK:]
-        prob = jnp.exp2(scores * (INV_ROOT * LOG2E) - lse_ref[b])
+        lse = lse_ref[b]
         row_dot = jnp.sum(attn_t_ref[b].astype(F32) * d_t.astype(F32), axis=0, keepdims=True)
-        score_grad = (prob * (prob_grad - row_dot) * INV_ROOT).astype(BF16)
-        k_t = jnp.concatenate([kt_ref[c] for c in owners], axis=1)
-        dq_t = jnp.dot(k_t, score_grad, preferred_element_type=F32)
-        out_ref[b, 0] = dq_t.astype(BF16).T
+        pairs = []
+        for c in owners:
+            both = jnp.dot(kv_ref[rows_of(c), :], right, preferred_element_type=F32)
+            prob = jnp.exp2(both[:, :BLOCK] * (INV_ROOT * LOG2E) - lse)
+            score_grad = (prob * (both[:, BLOCK:] - row_dot) * INV_ROOT).astype(BF16)
+            pairs.append((score_grad, prob.astype(BF16)))
         back = jnp.concatenate(
             [jnp.concatenate([q_one, zero], axis=1), jnp.concatenate([zero, d_one], axis=1)], axis=0
         )
-        return owners, jnp.dot(
-            jnp.concatenate([score_grad, prob.astype(BF16)], axis=1),
-            back,
-            preferred_element_type=F32,
-        )
+        for c, pair in zip(owners, pairs):
+            acc_ref[rows_of(c), :] += jnp.dot(
+                jnp.concatenate(pair, axis=1), back, preferred_element_type=F32
+            )
+        k_t = jnp.concatenate([kt_ref[c] for c in owners], axis=1)
+        score_grads = jnp.concatenate([score_grad for score_grad, _ in pairs], axis=0)
+        dq_t = jnp.dot(k_t, score_grads, preferred_element_type=F32)
+        out_ref[b, 0] = dq_t.astype(BF16).T
 
     def step(i, carry):
         chip = lax.rem(place_ref[0] + place_ref[2 + i], half)
-        results = [
-            one(2 * chip + place_ref[1], mine_ref[i]),
-            one(2 * chip + 1 - place_ref[1], theirs_ref[i]),
-        ]
-        for owners, found in results:
-            for s, c in enumerate(owners):
-                acc_ref[rows_of(c), :] += found[s * BLOCK : (s + 1) * BLOCK, :]
+        one(2 * chip + place_ref[1], mine_ref[i])
+        one(2 * chip + 1 - place_ref[1], theirs_ref[i])
         return carry
 
     lax.fori_loop(0, half, step, 0)
@@ -370,7 +367,7 @@
         compiler_params=pltpu.CompilerParams(vmem_limit_bytes=32 * MIB),
         cost_estimate=cost(6 * MICROSECOND),
         name="project",
-    )(cols, core, mine, *own, *other)
+    )(cols, core, mine, *(in_hbm(w) for w in own + other))
 
 
 def unpack_kernel(groups, places_ref, grads_ref, *refs):
@@ -411,14 +408,17 @@
     return [value] + [shifted(value, axis, i) for i in range(1, lax.axis_size(axis))]
 
 
-def spread(value, axis):
+def exchanged(value, axis):
     size = lax.axis_size(axis)
     here = lax.axis_index(axis)
-    total = lax.dynamic_index_in_dim(value, here, 0, keepdims=False).astype(F32)
-    for i in range(1, size):
-        piece = lax.dynamic_index_in_dim(value, (here + i) % size, 0, keepdims=False)
-        total = total + shifted(piece, axis, i).astype(F32)
-    return total
+    pieces = [
+        lax.dynamic_index_in_dim(value, (here + i) % size, 0, keepdims=False) for i in range(size)
+    ]
+    return pieces[:1] + [shifted(piece, axis, i) for i, piece in enumerate(pieces) if i]
+
+
+def total_of(pieces):
+    return sum(piece.astype(F32) for piece in pieces)
 
 
 def swapped(value):
@@ -489,14 +489,14 @@
 
     pg_mine, pg_theirs = weight_grad(parts, spot, attn_t, other_t, chunks, shards)
     pg = (pg_mine.astype(F32) + swapped(pg_theirs).astype(F32)).astype(BF16)
-    pg = spread(pg.reshape((groups, groups) + pg.shape[1:]), "x").astype(BF16)
+    pg_pieces = exchanged(pg.reshape((groups, groups) + pg.shape[1:]), "x")
     pieces = ((0, 0, groups), (1, 0, groups), (groups - 1, 0, groups))
     pieces += ((middle, 0, middle), (middle, middle, groups))
     weights = [w_here, w_up, w_down] + w_far
     cols = (((x - index) % groups)[:, None] * groups + ((y - index) % groups)[None]).reshape(-1)
     layer = project(pieces, cols, core[None], attn_rows, weights, [swapped(w) for w in weights])
-    pg, layer = lax.optimization_barrier((pg, layer))
-    pg = sum(piece.astype(F32) for piece in from_others(pg, "y"))
+    pg_pieces, layer = lax.optimization_barrier((pg_pieces, layer))
+    pg = total_of(from_others(total_of(pg_pieces).astype(BF16), "y"))
     pg = (pg * (1.0 / math.sqrt(tokens))).astype(BF16)
     pg_pieces = from_others(pg, "x")
     dq, dk, dv, proj_grad = unpack((x - index) % groups, grad_rows, pg_pieces)

time: 199 us -> 195 us (0.980)
  starting transfers between devices: 60.4 us -> 64.8 us
  local copies, waits for them, and re-layouts: 8.15 us -> 4.9 us
  waiting for transfers between devices: 79.1 us -> 76.4 us
    ppermute x24, starting transfers between devices: 28.3 us -> 33.3 us  [shifted(): lax.ppermute(value, axis, [(i, (i + by) % size) for i in range(size)])]
    unnamed x44 -> x20, local copies, waits for them, and re-layouts: 4.95 us -> 1.75 us
    pallas_call x1, Pallas kernels: 13.6 us -> 10.8 us  [backward(): pl.pallas_call(backward_kernel, out_shape=like(count, 3, BLOCK, HEAD_DIM)...]
  transfers between devices with their start and end apart: 37 -> 37, of which waited for: 13 -> 12; matrix products, arithmetic and copies ran while one was open for 3% -> 3% of each run, Pallas kernels for 21% -> 20%
where the time goes in v4:
time: 195 us
  waiting for transfers between devices  76.4 us (39%)
  starting transfers between devices  64.8 us (33%)
  Pallas kernels  45 us (23%)
  local copies, waits for them, and re-layouts  4.9 us (3%)
  other arithmetic  2.52 us (1%)
    ppermute x24, waiting for transfers between devices, shifted(): lax.ppermute(value, axis, [(i, (i + by) % size) for i in range(size)])  72.5 us
    ppermute x24, starting transfers between devices, shifted(): lax.ppermute(value, axis, [(i, (i + by) % size) for i in range(size)])  33.3 us
    pallas_call x1, Pallas kernels, forward(): pl.pallas_call(forward_kernel, out_shape=(like(count, BLOCK, HEAD_DIM), l...  12.5 us
    pallas_call x1, Pallas kernels, backward(): pl.pallas_call(backward_kernel, out_shape=like(count, 3, BLOCK, HEAD_DIM)...  10.8 us
    all_to_all x1, starting transfers between devices, body(): qkv = lax.all_to_all(qkv_out, seq, split_axis=0, concat_axis=0, tiled=True)  10.1 us
    ppermute x10, starting transfers between devices, swapped(): return lax.ppermute(value, 'c', [(0, 1), (1, 0)])  9.11 us
    all_to_all x1, starting transfers between devices, body(): lax.all_to_all(grads, seq, split_axis=0, concat_axis=0, tiled=True)  7.21 us
    pallas_call x2, Pallas kernels, attn_grad(): pl.pallas_call(functools.partial(attn_grad_kernel, parts), out_shape=(lik...  6.11 us
  transfers between devices with their start and end apart: 37, of which 12 were waited for; matrix products, arithmetic and copies ran while one was open for 3% of the time, Pallas kernels for 20%

profile of v4, /device:TPU:1, one launch (start us, length us, event | category | flops | bytes accessed | tf_op | source)
XLA Modules:
  0.0 194.5 jit_solution(13327368863438337638)
XLA Ops:
  0.6 3.0 %pack.1 = (bf16[16,448,128]{2,1,0:T(8,128)(2,1)}, bf16[16,128,128]{2,1,0:T(8,128)(2,1)}) custom-call(s32[1]{0:T(128)} %bitcast.3.place_ref, bf16[128,2048]{1,0:T(8,128)(2,1)} %bitcast.36, bf16[128,2048]{1,0:T(8,128)(2,1)} %bitcast.37, bf16[128,2048]{1,0:T(8,128)(2,1)} %bitcast.38, bf16[128,2048]{1,0:T(8,128)(2,1)} %bitcast.39, bf16[128,2048]{1,0:T(8,128)(2,1)} %mine_ref.3), custom_call_target="tpu_custom_call" | custom-call | flops 3449999872 | tf_op jit(solution)/shard_map/pack/pallas_call | solution.py:77
  3.7 10.1 %all-to-all-start = ((bf16[16,448,128]{2,1,0:T(8,128)(2,1)}), bf16[16,448,128]{2,1,0:T(8,128)(2,1)S(1)}, u32[]{:S(2)}, u32[]{:S(2)}) async-start(bf16[16,448,128]{2,1,0:T(8,128)(2,1)} %get-tuple-element.48), calls=%async_computation | async-start | bytes 3670016 | tf_op jit(solution)/shard_map/all_to_all | solution.py:441
  13.9 1.5 collective-permute-start
  15.3 1.3 collective-permute-start.1
  16.6 51.5 %collective-permute-done.refs_1_ = bf16[16,128,128]{2,1,0:T(8,128)(2,1)} collective-permute-done((bf16[16,128,128]{2,1,0:T(8,128)(2,1)S(1)}, bf16[16,128,128]{2,1,0:T(8,128)(2,1)}, u32[]{:S(2)}, u32[]{:S(2)}) %collective-permute-start) | collective-permute-done | bytes 524320 | tf_op jit(solution)/shard_map/ppermute | solution.py:404
  68.3 2.5 %collective-permute-start.3 = (bf16[16,128,128]{2,1,0:T(8,128)(2,1)}, bf16[16,128,128]{2,1,0:T(8,128)(2,1)}, u32[]{:S(2)}, u32[]{:S(2)}) collective-permute-start(bf16[16,128,128]{2,1,0:T(8,128)(2,1)} %collective-permute-done.1.refs_2_), channel_id=1, source_target_pairs={{0,224},{32,0},{64,32},{96,64},{128,96},{160,128},{192,160},{224,1... | collective-permute-start | bytes 1572872 | tf_op jit(solution)/shard_map/ppermute | solution.py:404
  70.8 1.4 collective-permute-start.4
  72.2 2.6 %collective-permute-start.5 = (bf16[16,64,128]{2,1,0:T(8,128)(2,1)S(1)}, bf16[16,64,128]{2,1,0:T(8,128)(2,1)S(1)}, u32[]{:S(2)}, u32[]{:S(2)}) collective-permute-start(bf16[16,64,128]{2,1,0:T(8,128)(2,1)S(1)} %slice.15), channel_id=1, source_target_pairs={{0,2},{1,3},{2,0},{3,1},{4,6},{5,7},{6,4},{7,5},{8,10},{9,11},{10,... | collective-permute-start | bytes 786440 | tf_op jit(solution)/shard_map/ppermute | solution.py:404
  74.8 1.1 collective-permute-start.6
  76.0 2.7 %collective-permute-done.4 = bf16[16,64,128]{2,1,0:T(8,128)(2,1)S(1)} collective-permute-done((bf16[16,64,128]{2,1,0:T(8,128)(2,1)S(1)}, bf16[16,64,128]{2,1,0:T(8,128)(2,1)S(1)}, u32[]{:S(2)}, u32[]{:S(2)}) %collective-permute-start.4) | collective-permute-done | bytes 262176 | tf_op jit(solution)/shard_map/ppermute | solution.py:404
  78.7 3.0 %collective-permute-start.9 = (bf16[128,2048]{1,0:T(8,128)(2,1)S(1)}, bf16[128,2048]{1,0:T(8,128)(2,1)S(1)}, u32[]{:S(2)}, u32[]{:S(2)}) collective-permute-start(bf16[128,2048]{1,0:T(8,128)(2,1)S(1)} %copy-done), channel_id=1, source_target_pairs={{0,16},{16,0},{1,17},{17,1},{2,18},{18,2},{3,19},{19,3},{4,20},{20... | collective-permute-start | bytes 1572872 | tf_op jit(solution)/shard_map/ppermute | solution.py:425
  81.7 3.7 %collective-permute-done.5 = bf16[16,64,128]{2,1,0:T(8,128)(2,1)S(1)} collective-permute-done((bf16[16,64,128]{2,1,0:T(8,128)(2,1)S(1)}, bf16[16,64,128]{2,1,0:T(8,128)(2,1)S(1)}, u32[]{:S(2)}, u32[]{:S(2)}) %collective-permute-start.5) | collective-permute-done | bytes 262176 | tf_op jit(solution)/shard_map/ppermute | solution.py:404
  85.3 2.1 %pad_maximum_fusion.refs_0_ = bf16[4,16,64,128]{3,2,1,0:T(8,128)(2,1)} fusion(bf16[1,16,64,128]{3,2,1,0:T(8,128)(2,1)} %bitcast.11, bf16[1,16,64,128]{3,2,1,0:T(8,128)(2,1)S(1)} %bitcast.34, bf16[1,16,64,128]{3,2,1,0:T(8,128)(2,1)S(1)} %bitcast.33, bf16[1,16,64,128]{3,2,1,0:T(8,128)(2,1)S(1)} %bitcast.32), kind=kLoop, calls=%fused_computation | loop fusion | flops 1572864 | bytes 2097152 | tf_op jit(solution)/shard_map/stack | solution.py:452
  87.4 1.2 collective-permute-start.12
  88.6 1.5 collective-permute-start.13
  90.1 2.7 %collective-permute-start.8 = (bf16[16,128,128]{2,1,0:T(8,128)(2,1)}, bf16[16,128,128]{2,1,0:T(8,128)(2,1)S(1)}, u32[]{:S(2)}, u32[]{:S(2)}) collective-permute-start(bf16[16,128,128]{2,1,0:T(8,128)(2,1)} %collective-permute-done.3.refs_4_), channel_id=1, source_target_pairs={{0,224},{32,0},{64,32},{96,64},{128,96},{160,128},{192,160},{224,1... | collective-permute-start | bytes 1572872 | tf_op jit(solution)/shard_map/ppermute | solution.py:404
  92.7 12.5 %forward.1 = (bf16[16,128,128]{2,1,0:T(8,128)(2,1)}, bf16[16,128,128]{2,1,0:T(8,128)(2,1)S(1)}, f32[16,1,128]{2,1,0:T(1,128)S(1)}) custom-call(s32[16,8]{1,0:T(8,128)S(1)} %copy.12.blocks_ref, bf16[16,448,128]{2,1,0:T(8,128)(2,1)S(1)} %all-to-all-done.qkv_ref), custom_call_target="tpu_custom_call" | custom-call | flops 13799999488 | tf_op jit(solution)/shard_map/forward/pallas_call | solution.py:135
  105.4 2.9 %collective-permute-start.11 = (bf16[8,128,128]{2,1,0:T(8,128)(2,1)S(1)}, bf16[8,128,128]{2,1,0:T(8,128)(2,1)S(1)}, u32[]{:S(2)}, u32[]{:S(2)}) collective-permute-start(bf16[8,128,128]{2,1,0:T(8,128)(2,1)S(1)} %slice.17), channel_id=1, source_target_pairs={{0,224},{32,0},{64,32},{96,64},{128,96},{160,128},{192,160},{224,1... | collective-permute-start | bytes 786440 | tf_op jit(solution)/shard_map/ppermute | solution.py:404
  108.3 4.6 %attn_grad.2 = (bf16[7,128,128]{2,1,0:T(8,128)(2,1)S(1)}, bf16[7,128,128]{2,1,0:T(8,128)(2,1)}) custom-call(bf16[128,2048]{1,0:T(8,128)(2,1)S(1)} %copy-done, bf16[128,2048]{1,0:T(8,128)(2,1)S(1)} %collective-permute-done.9.theirs_ref, bf16[16,128,128]{2,1,0:T(8,128)(2,1)} %get-tuple-element.49.refs_0_, bf16[16,128,128]{2,1,0:T(8,128)(2,1)} %collective-permute-done.refs_1_, ...), custom_call_target="tpu_custom_call" | custom-call | flops 4600000000 | tf_op jit(solution)/shard_map/attn_grad/pallas_call | solution.py:190
  113.0 4.1 %collective-permute-start.14 = (bf16[7,128,128]{2,1,0:T(8,128)(2,1)}, bf16[7,128,128]{2,1,0:T(8,128)(2,1)}, u32[]{:S(2)}, u32[]{:S(2)}) collective-permute-start(bf16[7,128,128]{2,1,0:T(8,128)(2,1)} %get-tuple-element.67), channel_id=1, source_target_pairs={{0,16},{16,0},{1,17},{17,1},{2,18},{18,2},{3,19},{19,3},{4,20},{20... | collective-permute-start | bytes 688136 | tf_op jit(solution)/shard_map/ppermute | solution.py:425
  117.1 0.7 copy-done.8
  117.9 1.5 attn_grad.3
  119.5 0.7 dynamic-slice_bitcast_fusion
  120.2 0.5 collective-permute-start.18
  120.7 5.1 %all-to-all-start.1 = ((bf16[16,128,128]{2,1,0:T(8,128)(2,1)}), bf16[16,128,128]{2,1,0:T(8,128)(2,1)S(1)}, u32[]{:S(2)}, u32[]{:S(2)}) async-start(bf16[16,128,128]{2,1,0:T(8,128)(2,1)} %get-tuple-element.72), calls=%async_computation.1 | async-start | bytes 1048576 | tf_op jit(solution)/shard_map/all_to_all | solution.py:479
  125.8 1.1 slice.18
  127.0 1.1 slice.19
  128.1 2.8 %collective-permute-start.17 = (bf16[2,16,64,128]{3,2,1,0:T(8,128)(2,1)S(1)}, bf16[2,16,64,128]{3,2,1,0:T(8,128)(2,1)}, u32[]{:S(2)}, u32[]{:S(2)}) collective-permute-start(bf16[2,16,64,128]{3,2,1,0:T(8,128)(2,1)S(1)} %slice.19), channel_id=1, source_target_pairs={{0,12},{4,0},{8,4},{12,8},{1,13},{5,1},{9,5},{13,9},{2,14},{6,2},{... | collective-permute-start | bytes 1572872 | tf_op jit(solution)/shard_map/ppermute | solution.py:404
  130.8 0.9 copy-done.2
  131.8 10.8 %backward.1 = bf16[16,3,128,128]{3,2,1,0:T(8,128)(2,1)} custom-call(s32[16,8]{1,0:T(8,128)S(1)} %copy.12.blocks_ref, s32[10]{0:T(128)S(1)} %pad_add_fusion.place_ref, bf16[16,448,128]{2,1,0:T(8,128)(2,1)S(1)} %all-to-all-done.qkv_ref, bf16[16,128,128]{2,1,0:T(8,128)(2,1)S(1)} %get-tuple-element.51.attn_t_ref.attn_ref, ...), custom_call_target="tpu_custom_call" | custom-call | flops 14949999616 | tf_op jit(solution)/shard_map/backward/pallas_call | solution.py:314
  142.6 0.6 all-to-all-done.1.mine_ref
  143.1 7.2 %all-to-all-start.2 = ((bf16[16,3,128,128]{3,2,1,0:T(8,128)(2,1)}), bf16[16,3,128,128]{3,2,1,0:T(8,128)(2,1)S(1)}, u32[]{:S(2)}, u32[]{:S(2)}) async-start(bf16[16,3,128,128]{3,2,1,0:T(8,128)(2,1)} %backward.1), calls=%async_computation.2 | async-start | bytes 3145728 | tf_op jit(solution)/shard_map/all_to_all | solution.py:488
  150.4 4.0 %weight_grad.1 = (bf16[16,128,128]{2,1,0:T(8,128)(2,1)S(1)}, bf16[16,128,128]{2,1,0:T(8,128)(2,1)}) custom-call(s32[10]{0:T(128)S(1)} %pad_add_fusion.place_ref, bf16[16,128,128]{2,1,0:T(8,128)(2,1)S(1)} %get-tuple-element.51.attn_t_ref.attn_ref, bf16[8,128,128]{2,1,0:T(8,128)(2,1)S(1)} %collective-permute-done.18.other_ref, ...), custom_call_target="tpu_custom_call" | custom-call | flops 4600000000 | tf_op jit(solution)/shard_map/weight_grad/pallas_call | solution.py:235
  155.7 0.9 collective-permute-done.19
  157.1 1.1 collective-permute-done.23.refs_5_
  158.5 1.2 collective-permute-done.24.refs_6_
  159.7 2.7 %collective-permute-start.21 = (bf16[4,128,128]{2,1,0:T(8,128)(2,1)S(1)}, bf16[4,128,128]{2,1,0:T(8,128)(2,1)S(1)}, u32[]{:S(2)}, u32[]{:S(2)}) collective-permute-start(bf16[4,128,128]{2,1,0:T(8,128)(2,1)S(1)} %get-tuple-element.92), channel_id=1, source_target_pairs={{0,8},{4,12},{8,0},{12,4},{1,9},{5,13},{9,1},{13,5},{2,10},{6,14},... | collective-permute-start | bytes 393224 | tf_op jit(solution)/shard_map/ppermute | solution.py:404
  162.4 1.8 collective-permute-start.22
  164.2 6.1 %project.1 = bf16[128,2048]{1,0:T(8,128)(2,1)} custom-call(s32[16]{0:T(128)S(1)} %add.120.cols_ref, s32[1]{0:T(128)} %bitcast.1.core_ref, bf16[16,128,128]{2,1,0:T(8,128)(2,1)S(1)} %all-to-all-done.1.mine_ref, bf16[4,16,64,128]{3,2,1,0:T(8,128)(2,1)} %pad_maximum_fusion.refs_0_, bf16[4,16,64,128]{3,2,1,0:T(8,128)(2,1)} %collective-permute-done.12.refs_1_, ...), custom_call_target="tpu_custom_call" | custom-call | flops 6899999744 | tf_op jit(solution)/shard_map/project/pallas_call | solution.py:361
  170.4 2.4 %collective-permute-start.30 = (bf16[4,128,128]{2,1,0:T(8,128)(2,1)S(1)}, bf16[4,128,128]{2,1,0:T(8,128)(2,1)S(1)}, u32[]{:S(2)}, u32[]{:S(2)}) collective-permute-start(bf16[4,128,128]{2,1,0:T(8,128)(2,1)S(1)} %add_convert_fusion.1), channel_id=1, source_target_pairs={{0,3},{1,0},{2,1},{3,2},{4,7},{5,4},{6,5},{7,6},{8,11},{9,8},{10,9... | collective-permute-start | bytes 393224 | tf_op jit(solution)/shard_map/ppermute | solution.py:404
  172.8 0.5 collective-permute-start.29
  173.7 2.3 %collective-permute-done.30 = bf16[4,128,128]{2,1,0:T(8,128)(2,1)S(1)} collective-permute-done((bf16[4,128,128]{2,1,0:T(8,128)(2,1)S(1)}, bf16[4,128,128]{2,1,0:T(8,128)(2,1)S(1)}, u32[]{:S(2)}, u32[]{:S(2)}) %collective-permute-start.30) | collective-permute-done | bytes 131104 | tf_op jit(solution)/shard_map/ppermute | solution.py:404
  176.0 2.6 %collective-permute-done.29 = bf16[4,128,128]{2,1,0:T(8,128)(2,1)S(1)} collective-permute-done((bf16[4,128,128]{2,1,0:T(8,128)(2,1)S(1)}, bf16[4,128,128]{2,1,0:T(8,128)(2,1)S(1)}, u32[]{:S(2)}, u32[]{:S(2)}) %collective-permute-start.29) | collective-permute-done | bytes 131104 | tf_op jit(solution)/shard_map/ppermute | solution.py:404
  178.6 3.9 %collective-permute-done.28 = bf16[4,128,128]{2,1,0:T(8,128)(2,1)S(1)} collective-permute-done((bf16[4,128,128]{2,1,0:T(8,128)(2,1)S(1)}, bf16[4,128,128]{2,1,0:T(8,128)(2,1)S(1)}, u32[]{:S(2)}, u32[]{:S(2)}) %collective-permute-start.28) | collective-permute-done | bytes 131104 | tf_op jit(solution)/shard_map/ppermute | solution.py:404
  182.7 3.4 %collective-permute-start.32 = (bf16[4,128,128]{2,1,0:T(8,128)(2,1)S(1)}, bf16[4,128,128]{2,1,0:T(8,128)(2,1)S(1)}, u32[]{:S(2)}, u32[]{:S(2)}) collective-permute-start(bf16[4,128,128]{2,1,0:T(8,128)(2,1)S(1)} %multiply_convert_fusion.refs_0_), channel_id=1, source_target_pairs={{0,8},{4,12},{8,0},{12,4},{1,9},{5,13},{9,1},{13,5},{2,10},{6,14},... | collective-permute-start | bytes 393224 | tf_op jit(solution)/shard_map/ppermute | solution.py:404
  186.1 2.4 %collective-permute-done.31.refs_1_ = bf16[4,128,128]{2,1,0:T(8,128)(2,1)S(1)} collective-permute-done((bf16[4,128,128]{2,1,0:T(8,128)(2,1)S(1)}, bf16[4,128,128]{2,1,0:T(8,128)(2,1)S(1)}, u32[]{:S(2)}, u32[]{:S(2)}) %collective-permute-start.31) | collective-permute-done | bytes 131104 | tf_op jit(solution)/shard_map/ppermute | solution.py:404
  188.5 3.5 %collective-permute-done.32.refs_2_ = bf16[4,128,128]{2,1,0:T(8,128)(2,1)S(1)} collective-permute-done((bf16[4,128,128]{2,1,0:T(8,128)(2,1)S(1)}, bf16[4,128,128]{2,1,0:T(8,128)(2,1)S(1)}, u32[]{:S(2)}, u32[]{:S(2)}) %collective-permute-start.32) | collective-permute-done | bytes 131104 | tf_op jit(solution)/shard_map/ppermute | solution.py:404
  192.0 2.5 %unpack.1 = (bf16[128,2048]{1,0:T(8,128)(2,1)}, bf16[128,2048]{1,0:T(8,128)(2,1)}, bf16[128,2048]{1,0:T(8,128)(2,1)}, f32[128,2048]{1,0:T(8,128)}) custom-call(s32[4]{0:T(128)S(1)} %and_select_fusion.1.places_ref, bf16[16,3,128,128]{3,2,1,0:T(8,128)(2,1)S(1)} %all-to-all-done.2.grads_ref, bf16[4,128,128]{2,1,0:T(8,128)(2,1)S(1)} %multiply_convert_fusion.refs_0_, ...), custom_call_target="tpu_custom_call" | custom-call | flops 3449999872 | tf_op jit(solution)/shard_map/unpack/pallas_call | solution.py:391
  (71 shorter events, 3.7 us)
Async XLA Ops:
  3.7 10.2 %copy-start.7 = (bf16[16,128,128]{2,1,0:T(8,128)(2,1)S(1)}, bf16[16,128,128]{2,1,0:T(8,128)(2,1)}, u32[]{:S(2)}) copy-start(bf16[16,128,128]{2,1,0:T(8,128)(2,1)} %get-tuple-element.49.refs_0_) | copy-start | bytes 1572868
  3.7 72.2 %copy-start.5 = (s32[1,16,8]{1,2,0:T(8,128)S(1)}, s32[1,16,8]{1,2,0:T(8,128)}, u32[]{:S(2)}) copy-start(s32[1,16,8]{1,2,0:T(8,128)} %param.12) | copy-start | bytes 1540
  3.7 72.2 %copy-start.6 = (s32[8]{0:T(128)S(1)}, s32[8]{0:T(128)}, u32[]{:S(2)}) copy-start(s32[8]{0:T(128)} %constant.87.clone) | copy-start | bytes 100
  3.7 75.0 %copy-start = (bf16[128,2048]{1,0:T(8,128)(2,1)S(1)}, bf16[128,2048]{1,0:T(8,128)(2,1)}, u32[]{:S(2)}) copy-start(bf16[128,2048]{1,0:T(8,128)(2,1)} %mine_ref.3) | copy-start | bytes 1572868
  3.7 64.4 %all-to-all-start = ((bf16[16,448,128]{2,1,0:T(8,128)(2,1)}), bf16[16,448,128]{2,1,0:T(8,128)(2,1)S(1)}, u32[]{:S(2)}, u32[]{:S(2)}) async-start(bf16[16,448,128]{2,1,0:T(8,128)(2,1)} %get-tuple-element.48), calls=%async_computation | async-start | bytes 3670016 | tf_op jit(solution)/shard_map/all_to_all | solution.py:441
  13.9 54.2 %collective-permute-start = (bf16[16,128,128]{2,1,0:T(8,128)(2,1)S(1)}, bf16[16,128,128]{2,1,0:T(8,128)(2,1)}, u32[]{:S(2)}, u32[]{:S(2)}) collective-permute-start(bf16[16,128,128]{2,1,0:T(8,128)(2,1)S(1)} %copy-done.7), channel_id=1, source_target_pairs={{0,32},{32,64},{64,96},{96,128},{128,160},{160,192},{192,224},{224... | collective-permute-start | bytes 1572872 | tf_op jit(solution)/shard_map/ppermute | solution.py:404
  15.3 52.8 %collective-permute-start.1 = (bf16[16,128,128]{2,1,0:T(8,128)(2,1)S(1)}, bf16[16,128,128]{2,1,0:T(8,128)(2,1)}, u32[]{:S(2)}, u32[]{:S(2)}) collective-permute-start(bf16[16,128,128]{2,1,0:T(8,128)(2,1)S(1)} %copy-done.7), channel_id=1, source_target_pairs={{0,224},{32,0},{64,32},{96,64},{128,96},{160,128},{192,160},{224,1... | collective-permute-start | bytes 1572872 | tf_op jit(solution)/shard_map/ppermute | solution.py:404
  68.1 17.2 %collective-permute-start.2 = (bf16[16,128,128]{2,1,0:T(8,128)(2,1)}, bf16[16,128,128]{2,1,0:T(8,128)(2,1)}, u32[]{:S(2)}, u32[]{:S(2)}) collective-permute-start(bf16[16,128,128]{2,1,0:T(8,128)(2,1)} %collective-permute-done.refs_1_), channel_id=1, source_target_pairs={{0,32},{32,64},{64,96},{96,128},{128,160},{160,192},{192,224},{224... | collective-permute-start | bytes 1572872 | tf_op jit(solution)/shard_map/ppermute | solution.py:404
  68.3 17.0 %collective-permute-start.3 = (bf16[16,128,128]{2,1,0:T(8,128)(2,1)}, bf16[16,128,128]{2,1,0:T(8,128)(2,1)}, u32[]{:S(2)}, u32[]{:S(2)}) collective-permute-start(bf16[16,128,128]{2,1,0:T(8,128)(2,1)} %collective-permute-done.1.refs_2_), channel_id=1, source_target_pairs={{0,224},{32,0},{64,32},{96,64},{128,96},{160,128},{192,160},{224,1... | collective-permute-start | bytes 1572872 | tf_op jit(solution)/shard_map/ppermute | solution.py:404
  70.8 7.9 %collective-permute-start.4 = (bf16[16,64,128]{2,1,0:T(8,128)(2,1)S(1)}, bf16[16,64,128]{2,1,0:T(8,128)(2,1)S(1)}, u32[]{:S(2)}, u32[]{:S(2)}) collective-permute-start(bf16[16,64,128]{2,1,0:T(8,128)(2,1)S(1)} %slice.15), channel_id=1, source_target_pairs={{0,1},{1,2},{2,3},{3,0},{4,5},{5,6},{6,7},{7,4},{8,9},{9,10},{10,1... | collective-permute-start | bytes 786440 | tf_op jit(solution)/shard_map/ppermute | solution.py:404
  72.2 13.1 %collective-permute-start.5 = (bf16[16,64,128]{2,1,0:T(8,128)(2,1)S(1)}, bf16[16,64,128]{2,1,0:T(8,128)(2,1)S(1)}, u32[]{:S(2)}, u32[]{:S(2)}) collective-permute-start(bf16[16,64,128]{2,1,0:T(8,128)(2,1)S(1)} %slice.15), channel_id=1, source_target_pairs={{0,2},{1,3},{2,0},{3,1},{4,6},{5,7},{6,4},{7,5},{8,10},{9,11},{10,... | collective-permute-start | bytes 786440 | tf_op jit(solution)/shard_map/ppermute | solution.py:404
  74.8 10.5 %collective-permute-start.6 = (bf16[16,64,128]{2,1,0:T(8,128)(2,1)S(1)}, bf16[16,64,128]{2,1,0:T(8,128)(2,1)}, u32[]{:S(2)}, u32[]{:S(2)}) collective-permute-start(bf16[16,64,128]{2,1,0:T(8,128)(2,1)S(1)} %slice.15), channel_id=1, source_target_pairs={{0,3},{1,0},{2,1},{3,2},{4,7},{5,4},{6,5},{7,6},{8,11},{9,8},{10,9... | collective-permute-start | bytes 786440 | tf_op jit(solution)/shard_map/ppermute | solution.py:404
  78.7 29.6 %collective-permute-start.9 = (bf16[128,2048]{1,0:T(8,128)(2,1)S(1)}, bf16[128,2048]{1,0:T(8,128)(2,1)S(1)}, u32[]{:S(2)}, u32[]{:S(2)}) collective-permute-start(bf16[128,2048]{1,0:T(8,128)(2,1)S(1)} %copy-done), channel_id=1, source_target_pairs={{0,16},{16,0},{1,17},{17,1},{2,18},{18,2},{3,19},{19,3},{4,20},{20... | collective-permute-start | bytes 1572872 | tf_op jit(solution)/shard_map/ppermute | solution.py:425
  87.4 29.7 %collective-permute-start.12 = (bf16[4,16,64,128]{3,2,1,0:T(8,128)(2,1)}, bf16[4,16,64,128]{3,2,1,0:T(8,128)(2,1)}, u32[]{:S(2)}, u32[]{:S(2)}) collective-permute-start(bf16[4,16,64,128]{3,2,1,0:T(8,128)(2,1)} %pad_maximum_fusion.refs_0_), channel_id=1, source_target_pairs={{0,4},{4,8},{8,12},{12,0},{1,5},{5,9},{9,13},{13,1},{2,6},{6,10},{... | collective-permute-start | bytes 3145736 | tf_op jit(solution)/shard_map/ppermute | solution.py:404
  88.6 28.5 %collective-permute-start.13 = (bf16[4,16,64,128]{3,2,1,0:T(8,128)(2,1)}, bf16[4,16,64,128]{3,2,1,0:T(8,128)(2,1)}, u32[]{:S(2)}, u32[]{:S(2)}) collective-permute-start(bf16[4,16,64,128]{3,2,1,0:T(8,128)(2,1)} %pad_maximum_fusion.refs_0_), channel_id=1, source_target_pairs={{0,12},{4,0},{8,4},{12,8},{1,13},{5,1},{9,5},{13,9},{2,14},{6,2},{... | collective-permute-start | bytes 3145736 | tf_op jit(solution)/shard_map/ppermute | solution.py:404
  90.1 15.2 %collective-permute-start.7 = (bf16[16,128,128]{2,1,0:T(8,128)(2,1)}, bf16[16,128,128]{2,1,0:T(8,128)(2,1)S(1)}, u32[]{:S(2)}, u32[]{:S(2)}) collective-permute-start(bf16[16,128,128]{2,1,0:T(8,128)(2,1)} %collective-permute-done.2.refs_3_), channel_id=1, source_target_pairs={{0,32},{32,64},{64,96},{96,128},{128,160},{160,192},{192,224},{224... | collective-permute-start | bytes 1572872 | tf_op jit(solution)/shard_map/ppermute | solution.py:404
  90.1 15.2 %collective-permute-start.8 = (bf16[16,128,128]{2,1,0:T(8,128)(2,1)}, bf16[16,128,128]{2,1,0:T(8,128)(2,1)S(1)}, u32[]{:S(2)}, u32[]{:S(2)}) collective-permute-start(bf16[16,128,128]{2,1,0:T(8,128)(2,1)} %collective-permute-done.3.refs_4_), channel_id=1, source_target_pairs={{0,224},{32,0},{64,32},{96,64},{128,96},{160,128},{192,160},{224,1... | collective-permute-start | bytes 1572872 | tf_op jit(solution)/shard_map/ppermute | solution.py:404
  105.2 3.1 %copy-start.3 = (bf16[16,128,128]{2,1,0:T(8,128)(2,1)}, bf16[16,128,128]{2,1,0:T(8,128)(2,1)S(1)}, u32[]{:S(2)}) copy-start(bf16[16,128,128]{2,1,0:T(8,128)(2,1)S(1)} %collective-permute-done.7.refs_5_) | copy-start | bytes 1572868
  105.2 3.1 %copy-start.4 = (bf16[16,128,128]{2,1,0:T(8,128)(2,1)}, bf16[16,128,128]{2,1,0:T(8,128)(2,1)S(1)}, u32[]{:S(2)}) copy-start(bf16[16,128,128]{2,1,0:T(8,128)(2,1)S(1)} %collective-permute-done.8.refs_6_) | copy-start | bytes 1572868
  105.3 11.8 %collective-permute-start.10 = (bf16[8,128,128]{2,1,0:T(8,128)(2,1)S(1)}, bf16[8,128,128]{2,1,0:T(8,128)(2,1)S(1)}, u32[]{:S(2)}, u32[]{:S(2)}) collective-permute-start(bf16[8,128,128]{2,1,0:T(8,128)(2,1)S(1)} %slice.16), channel_id=1, source_target_pairs={{0,32},{32,64},{64,96},{96,128},{128,160},{160,192},{192,224},{224... | collective-permute-start | bytes 786440 | tf_op jit(solution)/shard_map/ppermute | solution.py:404
  105.4 11.7 %collective-permute-start.11 = (bf16[8,128,128]{2,1,0:T(8,128)(2,1)S(1)}, bf16[8,128,128]{2,1,0:T(8,128)(2,1)S(1)}, u32[]{:S(2)}, u32[]{:S(2)}) collective-permute-start(bf16[8,128,128]{2,1,0:T(8,128)(2,1)S(1)} %slice.17), channel_id=1, source_target_pairs={{0,224},{32,0},{64,32},{96,64},{128,96},{160,128},{192,160},{224,1... | collective-permute-start | bytes 786440 | tf_op jit(solution)/shard_map/ppermute | solution.py:404
  113.0 6.4 %copy-start.1 = (bf16[7,128,128]{2,1,0:T(8,128)(2,1)}, bf16[7,128,128]{2,1,0:T(8,128)(2,1)S(1)}, u32[]{:S(2)}) copy-start(bf16[7,128,128]{2,1,0:T(8,128)(2,1)S(1)} %get-tuple-element.66.early_ref) | copy-start | bytes 688132
  113.0 17.9 %collective-permute-start.14 = (bf16[7,128,128]{2,1,0:T(8,128)(2,1)}, bf16[7,128,128]{2,1,0:T(8,128)(2,1)}, u32[]{:S(2)}, u32[]{:S(2)}) collective-permute-start(bf16[7,128,128]{2,1,0:T(8,128)(2,1)} %get-tuple-element.67), channel_id=1, source_target_pairs={{0,16},{16,0},{1,17},{17,1},{2,18},{18,2},{3,19},{19,3},{4,20},{20... | collective-permute-start | bytes 688136 | tf_op jit(solution)/shard_map/ppermute | solution.py:425
  117.1 0.7 copy-start.8
  117.1 0.8 copy-start.9
  119.4 11.4 %collective-permute-start.15 = (bf16[1,128,128]{2,1,0:T(8,128)(2,1)S(1)}, bf16[1,128,128]{2,1,0:T(8,128)(2,1)S(1)}, u32[]{:S(2)}, u32[]{:S(2)}) collective-permute-start(bf16[1,128,128]{2,1,0:T(8,128)(2,1)S(1)} %get-tuple-element.71), channel_id=1, source_target_pairs={{0,16},{16,0},{1,17},{17,1},{2,18},{18,2},{3,19},{19,3},{4,20},{20... | collective-permute-start | bytes 98312 | tf_op jit(solution)/shard_map/ppermute | solution.py:425
  120.2 22.3 %collective-permute-start.18 = (bf16[8,128,128]{2,1,0:T(8,128)(2,1)}, bf16[8,128,128]{2,1,0:T(8,128)(2,1)S(1)}, u32[]{:S(2)}, u32[]{:S(2)}) collective-permute-start(bf16[8,128,128]{2,1,0:T(8,128)(2,1)} %dynamic-slice_bitcast_fusion), channel_id=1, source_target_pairs={{0,16},{16,0},{1,17},{17,1},{2,18},{18,2},{3,19},{19,3},{4,20},{20... | collective-permute-start | bytes 786440 | tf_op jit(solution)/shard_map/ppermute | solution.py:425
  120.7 22.4 %all-to-all-start.1 = ((bf16[16,128,128]{2,1,0:T(8,128)(2,1)}), bf16[16,128,128]{2,1,0:T(8,128)(2,1)S(1)}, u32[]{:S(2)}, u32[]{:S(2)}) async-start(bf16[16,128,128]{2,1,0:T(8,128)(2,1)} %get-tuple-element.72), calls=%async_computation.1 | async-start | bytes 1048576 | tf_op jit(solution)/shard_map/all_to_all | solution.py:479
  126.9 15.7 %collective-permute-start.16 = (bf16[2,16,64,128]{3,2,1,0:T(8,128)(2,1)S(1)}, bf16[2,16,64,128]{3,2,1,0:T(8,128)(2,1)}, u32[]{:S(2)}, u32[]{:S(2)}) collective-permute-start(bf16[2,16,64,128]{3,2,1,0:T(8,128)(2,1)S(1)} %slice.18), channel_id=1, source_target_pairs={{0,4},{4,8},{8,12},{12,0},{1,5},{5,9},{9,13},{13,1},{2,6},{6,10},{... | collective-permute-start | bytes 1572872 | tf_op jit(solution)/shard_map/ppermute | solution.py:404
  128.1 14.5 %collective-permute-start.17 = (bf16[2,16,64,128]{3,2,1,0:T(8,128)(2,1)S(1)}, bf16[2,16,64,128]{3,2,1,0:T(8,128)(2,1)}, u32[]{:S(2)}, u32[]{:S(2)}) collective-permute-start(bf16[2,16,64,128]{3,2,1,0:T(8,128)(2,1)S(1)} %slice.19), channel_id=1, source_target_pairs={{0,12},{4,0},{8,4},{12,8},{1,13},{5,1},{9,5},{13,9},{2,14},{6,2},{... | collective-permute-start | bytes 1572872 | tf_op jit(solution)/shard_map/ppermute | solution.py:404
  130.8 0.9 copy-start.2
  143.1 48.9 %all-to-all-start.2 = ((bf16[16,3,128,128]{3,2,1,0:T(8,128)(2,1)}), bf16[16,3,128,128]{3,2,1,0:T(8,128)(2,1)S(1)}, u32[]{:S(2)}, u32[]{:S(2)}) async-start(bf16[16,3,128,128]{3,2,1,0:T(8,128)(2,1)} %backward.1), calls=%async_computation.2 | async-start | bytes 3145728 | tf_op jit(solution)/shard_map/all_to_all | solution.py:488
  154.4 2.2 %collective-permute-start.19 = (bf16[16,128,128]{2,1,0:T(8,128)(2,1)}, bf16[16,128,128]{2,1,0:T(8,128)(2,1)S(1)}, u32[]{:S(2)}, u32[]{:S(2)}) collective-permute-start(bf16[16,128,128]{2,1,0:T(8,128)(2,1)} %get-tuple-element.77), channel_id=1, source_target_pairs={{0,16},{16,0},{1,17},{17,1},{2,18},{18,2},{3,19},{19,3},{4,20},{20... | collective-permute-start | bytes 1572872 | tf_op jit(solution)/shard_map/ppermute | solution.py:425
  154.6 3.6 %collective-permute-start.23 = (bf16[4,16,64,128]{3,2,1,0:T(8,128)(2,1)}, bf16[4,16,64,128]{3,2,1,0:T(8,128)(2,1)}, u32[]{:S(2)}, u32[]{:S(2)}) collective-permute-start(bf16[4,16,64,128]{3,2,1,0:T(8,128)(2,1)} %pad_maximum_fusion.refs_0_), channel_id=1, source_target_pairs={{0,16},{16,0},{1,17},{17,1},{2,18},{18,2},{3,19},{19,3},{4,20},{20... | collective-permute-start | bytes 3145736 | tf_op jit(solution)/shard_map/ppermute | solution.py:425
  155.0 4.7 %collective-permute-start.24 = (bf16[4,16,64,128]{3,2,1,0:T(8,128)(2,1)}, bf16[4,16,64,128]{3,2,1,0:T(8,128)(2,1)}, u32[]{:S(2)}, u32[]{:S(2)}) collective-permute-start(bf16[4,16,64,128]{3,2,1,0:T(8,128)(2,1)} %collective-permute-done.12.refs_1_), channel_id=1, source_target_pairs={{0,16},{16,0},{1,17},{17,1},{2,18},{18,2},{3,19},{19,3},{4,20},{20... | collective-permute-start | bytes 3145736 | tf_op jit(solution)/shard_map/ppermute | solution.py:425
  155.1 7.3 %collective-permute-start.25 = (bf16[4,16,64,128]{3,2,1,0:T(8,128)(2,1)}, bf16[4,16,64,128]{3,2,1,0:T(8,128)(2,1)}, u32[]{:S(2)}, u32[]{:S(2)}) collective-permute-start(bf16[4,16,64,128]{3,2,1,0:T(8,128)(2,1)} %collective-permute-done.13.refs_2_), channel_id=1, source_target_pairs={{0,16},{16,0},{1,17},{17,1},{2,18},{18,2},{3,19},{19,3},{4,20},{20... | collective-permute-start | bytes 3145736 | tf_op jit(solution)/shard_map/ppermute | solution.py:425
  155.5 8.7 %collective-permute-start.26 = (bf16[2,16,64,128]{3,2,1,0:T(8,128)(2,1)}, bf16[2,16,64,128]{3,2,1,0:T(8,128)(2,1)}, u32[]{:S(2)}, u32[]{:S(2)}) collective-permute-start(bf16[2,16,64,128]{3,2,1,0:T(8,128)(2,1)} %collective-permute-done.16.refs_3_), channel_id=1, source_target_pairs={{0,16},{16,0},{1,17},{17,1},{2,18},{18,2},{3,19},{19,3},{4,20},{20... | collective-permute-start | bytes 1572872 | tf_op jit(solution)/shard_map/ppermute | solution.py:425
  156.6 7.6 %collective-permute-start.27 = (bf16[2,16,64,128]{3,2,1,0:T(8,128)(2,1)}, bf16[2,16,64,128]{3,2,1,0:T(8,128)(2,1)}, u32[]{:S(2)}, u32[]{:S(2)}) collective-permute-start(bf16[2,16,64,128]{3,2,1,0:T(8,128)(2,1)} %collective-permute-done.17.refs_4_), channel_id=1, source_target_pairs={{0,16},{16,0},{1,17},{17,1},{2,18},{18,2},{3,19},{19,3},{4,20},{20... | collective-permute-start | bytes 1572872 | tf_op jit(solution)/shard_map/ppermute | solution.py:425
  158.2 12.0 %collective-permute-start.20 = (bf16[4,128,128]{2,1,0:T(8,128)(2,1)S(1)}, bf16[4,128,128]{2,1,0:T(8,128)(2,1)S(1)}, u32[]{:S(2)}, u32[]{:S(2)}) collective-permute-start(bf16[4,128,128]{2,1,0:T(8,128)(2,1)S(1)} %get-tuple-element.93), channel_id=1, source_target_pairs={{0,4},{4,8},{8,12},{12,0},{1,5},{5,9},{9,13},{13,1},{2,6},{6,10},{... | collective-permute-start | bytes 393224 | tf_op jit(solution)/shard_map/ppermute | solution.py:404
  159.7 10.6 %collective-permute-start.21 = (bf16[4,128,128]{2,1,0:T(8,128)(2,1)S(1)}, bf16[4,128,128]{2,1,0:T(8,128)(2,1)S(1)}, u32[]{:S(2)}, u32[]{:S(2)}) collective-permute-start(bf16[4,128,128]{2,1,0:T(8,128)(2,1)S(1)} %get-tuple-element.92), channel_id=1, source_target_pairs={{0,8},{4,12},{8,0},{12,4},{1,9},{5,13},{9,1},{13,5},{2,10},{6,14},... | collective-permute-start | bytes 393224 | tf_op jit(solution)/shard_map/ppermute | solution.py:404
  162.4 7.9 %collective-permute-start.22 = (bf16[4,128,128]{2,1,0:T(8,128)(2,1)S(1)}, bf16[4,128,128]{2,1,0:T(8,128)(2,1)S(1)}, u32[]{:S(2)}, u32[]{:S(2)}) collective-permute-start(bf16[4,128,128]{2,1,0:T(8,128)(2,1)S(1)} %get-tuple-element.91), channel_id=1, source_target_pairs={{0,12},{4,0},{8,4},{12,8},{1,13},{5,1},{9,5},{13,9},{2,14},{6,2},{... | collective-permute-start | bytes 393224 | tf_op jit(solution)/shard_map/ppermute | solution.py:404
  170.4 5.6 %collective-permute-start.30 = (bf16[4,128,128]{2,1,0:T(8,128)(2,1)S(1)}, bf16[4,128,128]{2,1,0:T(8,128)(2,1)S(1)}, u32[]{:S(2)}, u32[]{:S(2)}) collective-permute-start(bf16[4,128,128]{2,1,0:T(8,128)(2,1)S(1)} %add_convert_fusion.1), channel_id=1, source_target_pairs={{0,3},{1,0},{2,1},{3,2},{4,7},{5,4},{6,5},{7,6},{8,11},{9,8},{10,9... | collective-permute-start | bytes 393224 | tf_op jit(solution)/shard_map/ppermute | solution.py:404
  172.8 5.8 %collective-permute-start.29 = (bf16[4,128,128]{2,1,0:T(8,128)(2,1)S(1)}, bf16[4,128,128]{2,1,0:T(8,128)(2,1)S(1)}, u32[]{:S(2)}, u32[]{:S(2)}) collective-permute-start(bf16[4,128,128]{2,1,0:T(8,128)(2,1)S(1)} %add_convert_fusion.1), channel_id=1, source_target_pairs={{0,2},{1,3},{2,0},{3,1},{4,6},{5,7},{6,4},{7,5},{8,10},{9,11},{10,... | collective-permute-start | bytes 393224 | tf_op jit(solution)/shard_map/ppermute | solution.py:404
  173.3 9.2 %collective-permute-start.28 = (bf16[4,128,128]{2,1,0:T(8,128)(2,1)S(1)}, bf16[4,128,128]{2,1,0:T(8,128)(2,1)S(1)}, u32[]{:S(2)}, u32[]{:S(2)}) collective-permute-start(bf16[4,128,128]{2,1,0:T(8,128)(2,1)S(1)} %add_convert_fusion.1), channel_id=1, source_target_pairs={{0,1},{1,2},{2,3},{3,0},{4,5},{5,6},{6,7},{7,4},{8,9},{9,10},{10,1... | collective-permute-start | bytes 393224 | tf_op jit(solution)/shard_map/ppermute | solution.py:404
  182.6 5.9 %collective-permute-start.31 = (bf16[4,128,128]{2,1,0:T(8,128)(2,1)S(1)}, bf16[4,128,128]{2,1,0:T(8,128)(2,1)S(1)}, u32[]{:S(2)}, u32[]{:S(2)}) collective-permute-start(bf16[4,128,128]{2,1,0:T(8,128)(2,1)S(1)} %multiply_convert_fusion.refs_0_), channel_id=1, source_target_pairs={{0,4},{4,8},{8,12},{12,0},{1,5},{5,9},{9,13},{13,1},{2,6},{6,10},{... | collective-permute-start | bytes 393224 | tf_op jit(solution)/shard_map/ppermute | solution.py:404
  182.7 9.3 %collective-permute-start.32 = (bf16[4,128,128]{2,1,0:T(8,128)(2,1)S(1)}, bf16[4,128,128]{2,1,0:T(8,128)(2,1)S(1)}, u32[]{:S(2)}, u32[]{:S(2)}) collective-permute-start(bf16[4,128,128]{2,1,0:T(8,128)(2,1)S(1)} %multiply_convert_fusion.refs_0_), channel_id=1, source_target_pairs={{0,8},{4,12},{8,0},{12,4},{1,9},{5,13},{9,1},{13,5},{2,10},{6,14},... | collective-permute-start | bytes 393224 | tf_op jit(solution)/shard_map/ppermute | solution.py:404
  186.1 5.9 %collective-permute-start.33 = (bf16[4,128,128]{2,1,0:T(8,128)(2,1)S(1)}, bf16[4,128,128]{2,1,0:T(8,128)(2,1)S(1)}, u32[]{:S(2)}, u32[]{:S(2)}) collective-permute-start(bf16[4,128,128]{2,1,0:T(8,128)(2,1)S(1)} %multiply_convert_fusion.refs_0_), channel_id=1, source_target_pairs={{0,12},{4,0},{8,4},{12,8},{1,13},{5,1},{9,5},{13,9},{2,14},{6,2},{... | collective-permute-start | bytes 393224 | tf_op jit(solution)/shard_map/ppermute | solution.py:404

commit v5 on v4

--- a/solution.py
+++ b/solution.py
@@ -110,14 +110,15 @@
 
     def one(b):
         owners = [blocks_ref[b, s] for s in range(slot_count)]
-        keys = jnp.concatenate([qkv_ref[c, KEY] for c in owners], axis=0)
-        scores = jnp.dot(keys, qkv_ref[b, QUERY].T, preferred_element_type=F32)
-        top = jnp.max(scores, axis=0, keepdims=True)
-        raised = jnp.exp2((scores - top) * (INV_ROOT * LOG2E))
-        total = jnp.sum(raised, axis=0, keepdims=True)
-        prob = (raised * (1.0 / total)).astype(BF16)
+        q_t = qkv_ref[b, QUERY].T
+        scores = [jnp.dot(qkv_ref[c, KEY], q_t, preferred_element_type=F32) for c in owners]
+        top = jnp.max(functools.reduce(jnp.maximum, scores), axis=0, keepdims=True)
+        raised = [jnp.exp2((score - top) * (INV_ROOT * LOG2E)) for score in scores]
+        total = jnp.sum(functools.reduce(jnp.add, raised), axis=0, keepdims=True)
+        weights = jnp.concatenate([one_raised.astype(BF16) for one_raised in raised], axis=0)
         v_t = jnp.concatenate([vt_ref[c] for c in owners], axis=1)
-        attn_t = jnp.dot(v_t, prob, preferred_element_type=F32).astype(BF16)
+        summed = jnp.dot(v_t, weights, preferred_element_type=F32)
+        attn_t = (summed * (1.0 / total)).astype(BF16)
         attn_t_ref[b] = attn_t
         attn_ref[b] = attn_t.T
         lse_ref[b] = top * (INV_ROOT * LOG2E) + jnp.log2(total)
@@ -481,18 +482,17 @@
         ((0, 0, cut), (0, cut, chunks)), out_proj, proj_theirs, shards[-2:]
     )
     theirs_late = swapped(theirs_late)
-    middle = groups // 2
-    w_far = [shifted(w_up[:middle], "x", 1), shifted(w_down[middle:], "x", -1)]
+    w_far = shifted(w_up, "x", 1)
     grads = backward(blocks, spot, qkv, attn_t, lse, early, theirs_early, late, theirs_late)
-    grads, attn_rows, w_far, other_t = lax.optimization_barrier((grads, attn_rows, w_far, other_t))
+    grads, attn_rows, other_t = lax.optimization_barrier((grads, attn_rows, other_t))
     grad_rows = lax.all_to_all(grads, seq, split_axis=0, concat_axis=0, tiled=True)
 
     pg_mine, pg_theirs = weight_grad(parts, spot, attn_t, other_t, chunks, shards)
+    pg_theirs, w_far = lax.optimization_barrier((pg_theirs, w_far))
     pg = (pg_mine.astype(F32) + swapped(pg_theirs).astype(F32)).astype(BF16)
     pg_pieces = exchanged(pg.reshape((groups, groups) + pg.shape[1:]), "x")
-    pieces = ((0, 0, groups), (1, 0, groups), (groups - 1, 0, groups))
-    pieces += ((middle, 0, middle), (middle, middle, groups))
-    weights = [w_here, w_up, w_down] + w_far
+    pieces = tuple((i, 0, groups) for i in (0, 1, groups - 1, 2))
+    weights = [w_here, w_up, w_down, w_far]
     cols = (((x - index) % groups)[:, None] * groups + ((y - index) % groups)[None]).reshape(-1)
     layer = project(pieces, cols, core[None], attn_rows, weights, [swapped(w) for w in weights])
     pg_pieces, layer = lax.optimization_barrier((pg_pieces, layer))

time: 195 us -> 187 us (0.959)
  starting transfers between devices: 64.8 us -> 59.4 us
  local copies, waits for them, and re-layouts: 4.9 us -> 2.75 us
    all_to_all x1, waiting for transfers between devices: 0.57 us -> 5.6 us  [body(): lax.all_to_all(attn, seq, split_axis=0, concat_axis=0, tiled=True)]
    all_to_all x1, starting transfers between devices: 7.21 us -> 3.6 us  [body(): lax.all_to_all(grads, seq, split_axis=0, concat_axis=0, tiled=True)]
    ppermute x24 -> x23, waiting for transfers between devices: 72.5 us -> 69.1 us  [shifted(): lax.ppermute(value, axis, [(i, (i + by) % size) for i in range(size)])]
    slice x2 -> x0, local copies, waits for them, and re-layouts: 2.15 us -> none  [body(): w_far = [shifted(w_up[:middle], 'x', 1), shifted(w_down[middle:], 'x', -1)]]
    ppermute x24 -> x23, starting transfers between devices: 33.3 us -> 31.3 us  [shifted(): lax.ppermute(value, axis, [(i, (i + by) % size) for i in range(size)])]
    ppermute x10 -> x9, starting transfers between devices: 9.11 us -> 9.32 us  [swapped(): return lax.ppermute(value, 'c', [(0, 1), (1, 0)])]
  transfers between devices with their start and end apart: 37 -> 35, of which waited for: 12 -> 13; matrix products, arithmetic and copies ran while one was open for 3% -> 1% of each run, Pallas kernels for 20% -> 20%
where the time goes in v5:
time: 187 us; the launch traced here: 186 us
  waiting for transfers between devices  77.7 us (42%)
  starting transfers between devices  59.4 us (32%)
  Pallas kernels  43.2 us (23%)
  local copies, waits for them, and re-layouts  2.75 us (1%)
    ppermute x23, waiting for transfers between devices, shifted(): lax.ppermute(value, axis, [(i, (i + by) % size) for i in range(size)])  69.1 us
    ppermute x23, starting transfers between devices, shifted(): lax.ppermute(value, axis, [(i, (i + by) % size) for i in range(size)])  31.3 us
    pallas_call x1, Pallas kernels, backward(): pl.pallas_call(backward_kernel, out_shape=like(count, 3, BLOCK, HEAD_DIM)...  10.7 us
    pallas_call x1, Pallas kernels, forward(): pl.pallas_call(forward_kernel, out_shape=(like(count, BLOCK, HEAD_DIM), l...  10.6 us
    all_to_all x1, starting transfers between devices, body(): qkv = lax.all_to_all(qkv_out, seq, split_axis=0, concat_axis=0, tiled=True)  10.1 us
    ppermute x9, starting transfers between devices, swapped(): return lax.ppermute(value, 'c', [(0, 1), (1, 0)])  9.32 us
    pallas_call x2, Pallas kernels, attn_grad(): pl.pallas_call(functools.partial(attn_grad_kernel, parts), out_shape=(lik...  6.12 us
    pallas_call x1, Pallas kernels, project(): pl.pallas_call(functools.partial(project_kernel, pieces), out_shape=like(...  6.04 us
  transfers between devices with their start and end apart: 35, of which 13 were waited for; matrix products, arithmetic and copies ran while one was open for 1% of the time, Pallas kernels for 20%

profile of v5, /device:TPU:1, one launch (start us, length us, event | category | flops | bytes accessed | tf_op | source)
XLA Modules:
  0.0 185.6 jit_solution(15785597835628516001)
XLA Ops:
  0.6 3.1 %pack.1 = (bf16[16,448,128]{2,1,0:T(8,128)(2,1)}, bf16[16,128,128]{2,1,0:T(8,128)(2,1)}) custom-call(s32[1]{0:T(128)} %bitcast.3.place_ref, bf16[128,2048]{1,0:T(8,128)(2,1)} %bitcast.36, bf16[128,2048]{1,0:T(8,128)(2,1)} %bitcast.37, bf16[128,2048]{1,0:T(8,128)(2,1)} %bitcast.38, bf16[128,2048]{1,0:T(8,128)(2,1)} %bitcast.39, bf16[128,2048]{1,0:T(8,128)(2,1)} %mine_ref.3), custom_call_target="tpu_custom_call" | custom-call | flops 3449999872 | tf_op jit(solution)/shard_map/pack/pallas_call | solution.py:77
  3.8 10.1 %all-to-all-start = ((bf16[16,448,128]{2,1,0:T(8,128)(2,1)}), bf16[16,448,128]{2,1,0:T(8,128)(2,1)S(1)}, u32[]{:S(2)}, u32[]{:S(2)}) async-start(bf16[16,448,128]{2,1,0:T(8,128)(2,1)} %get-tuple-element.48), calls=%async_computation | async-start | bytes 3670016 | tf_op jit(solution)/shard_map/all_to_all | solution.py:442
  14.0 1.5 collective-permute-start
  15.4 1.3 collective-permute-start.1
  16.7 51.5 %collective-permute-done.refs_1_ = bf16[16,128,128]{2,1,0:T(8,128)(2,1)} collective-permute-done((bf16[16,128,128]{2,1,0:T(8,128)(2,1)S(1)}, bf16[16,128,128]{2,1,0:T(8,128)(2,1)}, u32[]{:S(2)}, u32[]{:S(2)}) %collective-permute-start) | collective-permute-done | bytes 524320 | tf_op jit(solution)/shard_map/ppermute | solution.py:405
  68.4 2.5 %collective-permute-start.3 = (bf16[16,128,128]{2,1,0:T(8,128)(2,1)}, bf16[16,128,128]{2,1,0:T(8,128)(2,1)}, u32[]{:S(2)}, u32[]{:S(2)}) collective-permute-start(bf16[16,128,128]{2,1,0:T(8,128)(2,1)} %collective-permute-done.1.refs_2_), channel_id=1, source_target_pairs={{0,224},{32,0},{64,32},{96,64},{128,96},{160,128},{192,160},{224,1... | collective-permute-start | bytes 1572872 | tf_op jit(solution)/shard_map/ppermute | solution.py:405
  70.9 1.4 collective-permute-start.4
  72.3 2.7 %collective-permute-start.5 = (bf16[16,64,128]{2,1,0:T(8,128)(2,1)S(1)}, bf16[16,64,128]{2,1,0:T(8,128)(2,1)S(1)}, u32[]{:S(2)}, u32[]{:S(2)}) collective-permute-start(bf16[16,64,128]{2,1,0:T(8,128)(2,1)S(1)} %slice.9), channel_id=1, source_target_pairs={{0,2},{1,3},{2,0},{3,1},{4,6},{5,7},{6,4},{7,5},{8,10},{9,11},{10,... | collective-permute-start | bytes 786440 | tf_op jit(solution)/shard_map/ppermute | solution.py:405
  74.9 1.0 collective-permute-start.6
  76.1 2.7 %collective-permute-done.4 = bf16[16,64,128]{2,1,0:T(8,128)(2,1)S(1)} collective-permute-done((bf16[16,64,128]{2,1,0:T(8,128)(2,1)S(1)}, bf16[16,64,128]{2,1,0:T(8,128)(2,1)S(1)}, u32[]{:S(2)}, u32[]{:S(2)}) %collective-permute-start.4) | collective-permute-done | bytes 262176 | tf_op jit(solution)/shard_map/ppermute | solution.py:405
  78.9 2.9 %collective-permute-start.9 = (bf16[128,2048]{1,0:T(8,128)(2,1)S(1)}, bf16[128,2048]{1,0:T(8,128)(2,1)S(1)}, u32[]{:S(2)}, u32[]{:S(2)}) collective-permute-start(bf16[128,2048]{1,0:T(8,128)(2,1)S(1)} %copy-done), channel_id=1, source_target_pairs={{0,16},{16,0},{1,17},{17,1},{2,18},{18,2},{3,19},{19,3},{4,20},{20... | collective-permute-start | bytes 1572872 | tf_op jit(solution)/shard_map/ppermute | solution.py:426
  81.8 3.7 %collective-permute-done.5 = bf16[16,64,128]{2,1,0:T(8,128)(2,1)S(1)} collective-permute-done((bf16[16,64,128]{2,1,0:T(8,128)(2,1)S(1)}, bf16[16,64,128]{2,1,0:T(8,128)(2,1)S(1)}, u32[]{:S(2)}, u32[]{:S(2)}) %collective-permute-start.5) | collective-permute-done | bytes 262176 | tf_op jit(solution)/shard_map/ppermute | solution.py:405
  85.5 1.1 pad_maximum_fusion.refs_0_
  86.6 1.3 collective-permute-start.12
  87.8 1.5 collective-permute-start.13
  89.3 2.7 %collective-permute-start.8 = (bf16[16,128,128]{2,1,0:T(8,128)(2,1)}, bf16[16,128,128]{2,1,0:T(8,128)(2,1)S(1)}, u32[]{:S(2)}, u32[]{:S(2)}) collective-permute-start(bf16[16,128,128]{2,1,0:T(8,128)(2,1)} %collective-permute-done.3.refs_4_), channel_id=1, source_target_pairs={{0,224},{32,0},{64,32},{96,64},{128,96},{160,128},{192,160},{224,1... | collective-permute-start | bytes 1572872 | tf_op jit(solution)/shard_map/ppermute | solution.py:405
  92.0 10.6 %forward.1 = (bf16[16,128,128]{2,1,0:T(8,128)(2,1)}, bf16[16,128,128]{2,1,0:T(8,128)(2,1)S(1)}, f32[16,1,128]{2,1,0:T(1,128)S(1)}) custom-call(s32[16,8]{1,0:T(8,128)S(1)} %copy.12.blocks_ref, bf16[16,448,128]{2,1,0:T(8,128)(2,1)S(1)} %all-to-all-done.qkv_ref), custom_call_target="tpu_custom_call" | custom-call | flops 13799999488 | tf_op jit(solution)/shard_map/forward/pallas_call | solution.py:136
  102.8 2.9 %collective-permute-start.11 = (bf16[8,128,128]{2,1,0:T(8,128)(2,1)S(1)}, bf16[8,128,128]{2,1,0:T(8,128)(2,1)S(1)}, u32[]{:S(2)}, u32[]{:S(2)}) collective-permute-start(bf16[8,128,128]{2,1,0:T(8,128)(2,1)S(1)} %slice.11), channel_id=1, source_target_pairs={{0,224},{32,0},{64,32},{96,64},{128,96},{160,128},{192,160},{224,1... | collective-permute-start | bytes 786440 | tf_op jit(solution)/shard_map/ppermute | solution.py:405
  105.7 4.6 %attn_grad.2 = (bf16[7,128,128]{2,1,0:T(8,128)(2,1)S(1)}, bf16[7,128,128]{2,1,0:T(8,128)(2,1)}) custom-call(bf16[128,2048]{1,0:T(8,128)(2,1)S(1)} %copy-done, bf16[128,2048]{1,0:T(8,128)(2,1)S(1)} %collective-permute-done.9.theirs_ref, bf16[16,128,128]{2,1,0:T(8,128)(2,1)} %get-tuple-element.49.refs_0_, bf16[16,128,128]{2,1,0:T(8,128)(2,1)} %collective-permute-done.refs_1_, ...), custom_call_target="tpu_custom_call" | custom-call | flops 4600000000 | tf_op jit(solution)/shard_map/attn_grad/pallas_call | solution.py:191
  110.4 4.1 %collective-permute-start.14 = (bf16[7,128,128]{2,1,0:T(8,128)(2,1)}, bf16[7,128,128]{2,1,0:T(8,128)(2,1)}, u32[]{:S(2)}, u32[]{:S(2)}) collective-permute-start(bf16[7,128,128]{2,1,0:T(8,128)(2,1)} %get-tuple-element.67), channel_id=1, source_target_pairs={{0,16},{16,0},{1,17},{17,1},{2,18},{18,2},{3,19},{19,3},{4,20},{20... | collective-permute-start | bytes 688136 | tf_op jit(solution)/shard_map/ppermute | solution.py:426
  114.6 0.6 copy-done.11
  115.3 1.5 attn_grad.3
  117.0 0.7 dynamic-slice_bitcast_fusion
  117.7 0.5 collective-permute-start.16
  118.2 5.1 %all-to-all-start.1 = ((bf16[16,128,128]{2,1,0:T(8,128)(2,1)}), bf16[16,128,128]{2,1,0:T(8,128)(2,1)S(1)}, u32[]{:S(2)}, u32[]{:S(2)}) async-start(bf16[16,128,128]{2,1,0:T(8,128)(2,1)} %get-tuple-element.72), calls=%async_computation.1 | async-start | bytes 1048576 | tf_op jit(solution)/shard_map/all_to_all | solution.py:480
  123.3 0.9 copy-done.2
  124.2 10.7 %backward.1 = bf16[16,3,128,128]{3,2,1,0:T(8,128)(2,1)} custom-call(s32[16,8]{1,0:T(8,128)S(1)} %copy.12.blocks_ref, s32[10]{0:T(128)S(1)} %pad_add_fusion.place_ref, bf16[16,448,128]{2,1,0:T(8,128)(2,1)S(1)} %all-to-all-done.qkv_ref, bf16[16,128,128]{2,1,0:T(8,128)(2,1)S(1)} %get-tuple-element.51.attn_t_ref.attn_ref, ...), custom_call_target="tpu_custom_call" | custom-call | flops 14949999616 | tf_op jit(solution)/shard_map/backward/pallas_call | solution.py:315
  135.0 5.6 %all-to-all-done.1.mine_ref = bf16[16,128,128]{2,1,0:T(8,128)(2,1)S(1)} async-done(((bf16[16,128,128]{2,1,0:T(8,128)(2,1)}), bf16[16,128,128]{2,1,0:T(8,128)(2,1)S(1)}, u32[]{:S(2)}, u32[]{:S(2)}) %all-to-all-start.1) | async-done | bytes 524320 | tf_op jit(solution)/shard_map/all_to_all | solution.py:480
  140.6 3.6 %all-to-all-start.2 = ((bf16[16,3,128,128]{3,2,1,0:T(8,128)(2,1)}), bf16[16,3,128,128]{3,2,1,0:T(8,128)(2,1)S(1)}, u32[]{:S(2)}, u32[]{:S(2)}) async-start(bf16[16,3,128,128]{3,2,1,0:T(8,128)(2,1)} %backward.1), calls=%async_computation.2 | async-start | bytes 3145728 | tf_op jit(solution)/shard_map/all_to_all | solution.py:488
  144.3 0.5 collective-permute-start.23
  144.9 4.0 %weight_grad.1 = (bf16[16,128,128]{2,1,0:T(8,128)(2,1)S(1)}, bf16[16,128,128]{2,1,0:T(8,128)(2,1)}) custom-call(s32[10]{0:T(128)S(1)} %pad_add_fusion.place_ref, bf16[16,128,128]{2,1,0:T(8,128)(2,1)S(1)} %get-tuple-element.51.attn_t_ref.attn_ref, bf16[8,128,128]{2,1,0:T(8,128)(2,1)S(1)} %collective-permute-done.16.other_ref, ...), custom_call_target="tpu_custom_call" | custom-call | flops 4600000000 | tf_op jit(solution)/shard_map/weight_grad/pallas_call | solution.py:236
  149.4 1.0 collective-permute-start.25
  150.5 2.9 %collective-permute-done.18 = bf16[16,128,128]{2,1,0:T(8,128)(2,1)S(1)} collective-permute-done((bf16[16,128,128]{2,1,0:T(8,128)(2,1)}, bf16[16,128,128]{2,1,0:T(8,128)(2,1)S(1)}, u32[]{:S(2)}, u32[]{:S(2)}) %collective-permute-start.18) | collective-permute-done | bytes 524320 | tf_op jit(solution)/shard_map/ppermute | solution.py:426
  153.8 1.6 collective-permute-start.20
  155.4 1.3 collective-permute-start.21
  156.8 6.0 %project.1 = bf16[128,2048]{1,0:T(8,128)(2,1)} custom-call(s32[16]{0:T(128)S(1)} %add.120.cols_ref, s32[1]{0:T(128)} %bitcast.1.core_ref, bf16[16,128,128]{2,1,0:T(8,128)(2,1)S(1)} %all-to-all-done.1.mine_ref, bf16[4,16,64,128]{3,2,1,0:T(8,128)(2,1)} %copy-done.3, bf16[4,16,64,128]{3,2,1,0:T(8,128)(2,1)} %copy-done.8, bf16[4,16,64,128]{3,2,1,0:T(8,128)(2,1)} %copy-done.9, ...), custom_call_target="tpu_custom_call" | custom-call | flops 6899999744 | tf_op jit(solution)/shard_map/project/pallas_call | solution.py:362
  163.1 1.2 collective-permute-start.26
  164.4 2.8 %collective-permute-start.27 = (bf16[4,128,128]{2,1,0:T(8,128)(2,1)S(1)}, bf16[4,128,128]{2,1,0:T(8,128)(2,1)S(1)}, u32[]{:S(2)}, u32[]{:S(2)}) collective-permute-start(bf16[4,128,128]{2,1,0:T(8,128)(2,1)S(1)} %add_convert_fusion.1), channel_id=1, source_target_pairs={{0,2},{1,3},{2,0},{3,1},{4,6},{5,7},{6,4},{7,5},{8,10},{9,11},{10,... | collective-permute-start | bytes 393224 | tf_op jit(solution)/shard_map/ppermute | solution.py:405
  167.2 0.4 collective-permute-start.28
  167.6 1.0 collective-permute-done.26
  168.7 3.6 %collective-permute-done.27 = bf16[4,128,128]{2,1,0:T(8,128)(2,1)S(1)} collective-permute-done((bf16[4,128,128]{2,1,0:T(8,128)(2,1)S(1)}, bf16[4,128,128]{2,1,0:T(8,128)(2,1)S(1)}, u32[]{:S(2)}, u32[]{:S(2)}) %collective-permute-start.27) | collective-permute-done | bytes 131104 | tf_op jit(solution)/shard_map/ppermute | solution.py:405
  172.3 0.5 collective-permute-done.28
  172.8 0.7 collective-permute-start.29
  173.5 4.1 %collective-permute-start.30 = (bf16[4,128,128]{2,1,0:T(8,128)(2,1)S(1)}, bf16[4,128,128]{2,1,0:T(8,128)(2,1)S(1)}, u32[]{:S(2)}, u32[]{:S(2)}) collective-permute-start(bf16[4,128,128]{2,1,0:T(8,128)(2,1)S(1)} %multiply_convert_fusion.refs_0_), channel_id=1, source_target_pairs={{0,8},{4,12},{8,0},{12,4},{1,9},{5,13},{9,1},{13,5},{2,10},{6,14},... | collective-permute-start | bytes 393224 | tf_op jit(solution)/shard_map/ppermute | solution.py:405
  177.6 1.5 collective-permute-done.29.refs_1_
  179.1 3.2 %collective-permute-done.30.refs_2_ = bf16[4,128,128]{2,1,0:T(8,128)(2,1)S(1)} collective-permute-done((bf16[4,128,128]{2,1,0:T(8,128)(2,1)S(1)}, bf16[4,128,128]{2,1,0:T(8,128)(2,1)S(1)}, u32[]{:S(2)}, u32[]{:S(2)}) %collective-permute-start.30) | collective-permute-done | bytes 131104 | tf_op jit(solution)/shard_map/ppermute | solution.py:405
  182.3 0.8 collective-permute-done.31.refs_3_
  183.1 2.5 %unpack.1 = (bf16[128,2048]{1,0:T(8,128)(2,1)}, bf16[128,2048]{1,0:T(8,128)(2,1)}, bf16[128,2048]{1,0:T(8,128)(2,1)}, f32[128,2048]{1,0:T(8,128)}) custom-call(s32[4]{0:T(128)S(1)} %and_select_fusion.1.places_ref, bf16[16,3,128,128]{3,2,1,0:T(8,128)(2,1)S(1)} %all-to-all-done.2.grads_ref, bf16[4,128,128]{2,1,0:T(8,128)(2,1)S(1)} %multiply_convert_fusion.refs_0_, ...), custom_call_target="tpu_custom_call" | custom-call | flops 3449999872 | tf_op jit(solution)/shard_map/unpack/pallas_call | solution.py:392
  (71 shorter events, 2.3 us)
Async XLA Ops:
  3.8 10.2 %copy-start.10 = (bf16[16,128,128]{2,1,0:T(8,128)(2,1)S(1)}, bf16[16,128,128]{2,1,0:T(8,128)(2,1)}, u32[]{:S(2)}) copy-start(bf16[16,128,128]{2,1,0:T(8,128)(2,1)} %get-tuple-element.49.refs_0_) | copy-start | bytes 1572868
  3.8 72.2 %copy-start.6 = (s32[1,16,8]{1,2,0:T(8,128)S(1)}, s32[1,16,8]{1,2,0:T(8,128)}, u32[]{:S(2)}) copy-start(s32[1,16,8]{1,2,0:T(8,128)} %param.12) | copy-start | bytes 1540
  3.8 72.2 %copy-start.7 = (s32[8]{0:T(128)S(1)}, s32[8]{0:T(128)}, u32[]{:S(2)}) copy-start(s32[8]{0:T(128)} %constant.87.clone) | copy-start | bytes 100
  3.8 75.0 %copy-start = (bf16[128,2048]{1,0:T(8,128)(2,1)S(1)}, bf16[128,2048]{1,0:T(8,128)(2,1)}, u32[]{:S(2)}) copy-start(bf16[128,2048]{1,0:T(8,128)(2,1)} %mine_ref.3) | copy-start | bytes 1572868
  3.8 64.4 %all-to-all-start = ((bf16[16,448,128]{2,1,0:T(8,128)(2,1)}), bf16[16,448,128]{2,1,0:T(8,128)(2,1)S(1)}, u32[]{:S(2)}, u32[]{:S(2)}) async-start(bf16[16,448,128]{2,1,0:T(8,128)(2,1)} %get-tuple-element.48), calls=%async_computation | async-start | bytes 3670016 | tf_op jit(solution)/shard_map/all_to_all | solution.py:442
  14.0 54.2 %collective-permute-start = (bf16[16,128,128]{2,1,0:T(8,128)(2,1)S(1)}, bf16[16,128,128]{2,1,0:T(8,128)(2,1)}, u32[]{:S(2)}, u32[]{:S(2)}) collective-permute-start(bf16[16,128,128]{2,1,0:T(8,128)(2,1)S(1)} %copy-done.10), channel_id=1, source_target_pairs={{0,32},{32,64},{64,96},{96,128},{128,160},{160,192},{192,224},{224... | collective-permute-start | bytes 1572872 | tf_op jit(solution)/shard_map/ppermute | solution.py:405
  15.4 52.8 %collective-permute-start.1 = (bf16[16,128,128]{2,1,0:T(8,128)(2,1)S(1)}, bf16[16,128,128]{2,1,0:T(8,128)(2,1)}, u32[]{:S(2)}, u32[]{:S(2)}) collective-permute-start(bf16[16,128,128]{2,1,0:T(8,128)(2,1)S(1)} %copy-done.10), channel_id=1, source_target_pairs={{0,224},{32,0},{64,32},{96,64},{128,96},{160,128},{192,160},{224,1... | collective-permute-start | bytes 1572872 | tf_op jit(solution)/shard_map/ppermute | solution.py:405
  68.2 17.3 %collective-permute-start.2 = (bf16[16,128,128]{2,1,0:T(8,128)(2,1)}, bf16[16,128,128]{2,1,0:T(8,128)(2,1)}, u32[]{:S(2)}, u32[]{:S(2)}) collective-permute-start(bf16[16,128,128]{2,1,0:T(8,128)(2,1)} %collective-permute-done.refs_1_), channel_id=1, source_target_pairs={{0,32},{32,64},{64,96},{96,128},{128,160},{160,192},{192,224},{224... | collective-permute-start | bytes 1572872 | tf_op jit(solution)/shard_map/ppermute | solution.py:405
  68.4 17.0 %collective-permute-start.3 = (bf16[16,128,128]{2,1,0:T(8,128)(2,1)}, bf16[16,128,128]{2,1,0:T(8,128)(2,1)}, u32[]{:S(2)}, u32[]{:S(2)}) collective-permute-start(bf16[16,128,128]{2,1,0:T(8,128)(2,1)} %collective-permute-done.1.refs_2_), channel_id=1, source_target_pairs={{0,224},{32,0},{64,32},{96,64},{128,96},{160,128},{192,160},{224,1... | collective-permute-start | bytes 1572872 | tf_op jit(solution)/shard_map/ppermute | solution.py:405
  70.9 8.0 %collective-permute-start.4 = (bf16[16,64,128]{2,1,0:T(8,128)(2,1)S(1)}, bf16[16,64,128]{2,1,0:T(8,128)(2,1)S(1)}, u32[]{:S(2)}, u32[]{:S(2)}) collective-permute-start(bf16[16,64,128]{2,1,0:T(8,128)(2,1)S(1)} %slice.9), channel_id=1, source_target_pairs={{0,1},{1,2},{2,3},{3,0},{4,5},{5,6},{6,7},{7,4},{8,9},{9,10},{10,1... | collective-permute-start | bytes 786440 | tf_op jit(solution)/shard_map/ppermute | solution.py:405
  72.3 13.2 %collective-permute-start.5 = (bf16[16,64,128]{2,1,0:T(8,128)(2,1)S(1)}, bf16[16,64,128]{2,1,0:T(8,128)(2,1)S(1)}, u32[]{:S(2)}, u32[]{:S(2)}) collective-permute-start(bf16[16,64,128]{2,1,0:T(8,128)(2,1)S(1)} %slice.9), channel_id=1, source_target_pairs={{0,2},{1,3},{2,0},{3,1},{4,6},{5,7},{6,4},{7,5},{8,10},{9,11},{10,... | collective-permute-start | bytes 786440 | tf_op jit(solution)/shard_map/ppermute | solution.py:405
  74.9 10.5 %collective-permute-start.6 = (bf16[16,64,128]{2,1,0:T(8,128)(2,1)S(1)}, bf16[16,64,128]{2,1,0:T(8,128)(2,1)}, u32[]{:S(2)}, u32[]{:S(2)}) collective-permute-start(bf16[16,64,128]{2,1,0:T(8,128)(2,1)S(1)} %slice.9), channel_id=1, source_target_pairs={{0,3},{1,0},{2,1},{3,2},{4,7},{5,4},{6,5},{7,6},{8,11},{9,8},{10,9... | collective-permute-start | bytes 786440 | tf_op jit(solution)/shard_map/ppermute | solution.py:405
  78.9 26.9 %collective-permute-start.9 = (bf16[128,2048]{1,0:T(8,128)(2,1)S(1)}, bf16[128,2048]{1,0:T(8,128)(2,1)S(1)}, u32[]{:S(2)}, u32[]{:S(2)}) collective-permute-start(bf16[128,2048]{1,0:T(8,128)(2,1)S(1)} %copy-done), channel_id=1, source_target_pairs={{0,16},{16,0},{1,17},{17,1},{2,18},{18,2},{3,19},{19,3},{4,20},{20... | collective-permute-start | bytes 1572872 | tf_op jit(solution)/shard_map/ppermute | solution.py:426
  86.5 16.1 %copy-start.3 = (bf16[4,16,64,128]{3,2,1,0:T(8,128)(2,1)}, bf16[4,16,64,128]{3,2,1,0:T(8,128)(2,1)S(1)}, u32[]{:S(2)}) copy-start(bf16[4,16,64,128]{3,2,1,0:T(8,128)(2,1)S(1)} %pad_maximum_fusion.refs_0_) | copy-start | bytes 3145732
  86.6 28.0 %collective-permute-start.12 = (bf16[4,16,64,128]{3,2,1,0:T(8,128)(2,1)S(1)}, bf16[4,16,64,128]{3,2,1,0:T(8,128)(2,1)S(1)}, u32[]{:S(2)}, u32[]{:S(2)}) collective-permute-start(bf16[4,16,64,128]{3,2,1,0:T(8,128)(2,1)S(1)} %pad_maximum_fusion.refs_0_), channel_id=1, source_target_pairs={{0,4},{4,8},{8,12},{12,0},{1,5},{5,9},{9,13},{13,1},{2,6},{6,10},{... | collective-permute-start | bytes 3145736 | tf_op jit(solution)/shard_map/ppermute | solution.py:405
  87.8 26.7 %collective-permute-start.13 = (bf16[4,16,64,128]{3,2,1,0:T(8,128)(2,1)S(1)}, bf16[4,16,64,128]{3,2,1,0:T(8,128)(2,1)S(1)}, u32[]{:S(2)}, u32[]{:S(2)}) collective-permute-start(bf16[4,16,64,128]{3,2,1,0:T(8,128)(2,1)S(1)} %pad_maximum_fusion.refs_0_), channel_id=1, source_target_pairs={{0,12},{4,0},{8,4},{12,8},{1,13},{5,1},{9,5},{13,9},{2,14},{6,2},{... | collective-permute-start | bytes 3145736 | tf_op jit(solution)/shard_map/ppermute | solution.py:405
  89.3 13.3 %collective-permute-start.7 = (bf16[16,128,128]{2,1,0:T(8,128)(2,1)}, bf16[16,128,128]{2,1,0:T(8,128)(2,1)S(1)}, u32[]{:S(2)}, u32[]{:S(2)}) collective-permute-start(bf16[16,128,128]{2,1,0:T(8,128)(2,1)} %collective-permute-done.2.refs_3_), channel_id=1, source_target_pairs={{0,32},{32,64},{64,96},{96,128},{128,160},{160,192},{192,224},{224... | collective-permute-start | bytes 1572872 | tf_op jit(solution)/shard_map/ppermute | solution.py:405
  89.3 13.3 %collective-permute-start.8 = (bf16[16,128,128]{2,1,0:T(8,128)(2,1)}, bf16[16,128,128]{2,1,0:T(8,128)(2,1)S(1)}, u32[]{:S(2)}, u32[]{:S(2)}) collective-permute-start(bf16[16,128,128]{2,1,0:T(8,128)(2,1)} %collective-permute-done.3.refs_4_), channel_id=1, source_target_pairs={{0,224},{32,0},{64,32},{96,64},{128,96},{160,128},{192,160},{224,1... | collective-permute-start | bytes 1572872 | tf_op jit(solution)/shard_map/ppermute | solution.py:405
  102.6 3.1 %copy-start.4 = (bf16[16,128,128]{2,1,0:T(8,128)(2,1)}, bf16[16,128,128]{2,1,0:T(8,128)(2,1)S(1)}, u32[]{:S(2)}) copy-start(bf16[16,128,128]{2,1,0:T(8,128)(2,1)S(1)} %collective-permute-done.7.refs_5_) | copy-start | bytes 1572868
  102.6 3.1 %copy-start.5 = (bf16[16,128,128]{2,1,0:T(8,128)(2,1)}, bf16[16,128,128]{2,1,0:T(8,128)(2,1)S(1)}, u32[]{:S(2)}) copy-start(bf16[16,128,128]{2,1,0:T(8,128)(2,1)S(1)} %collective-permute-done.8.refs_6_) | copy-start | bytes 1572868
  102.7 11.8 %collective-permute-start.10 = (bf16[8,128,128]{2,1,0:T(8,128)(2,1)S(1)}, bf16[8,128,128]{2,1,0:T(8,128)(2,1)S(1)}, u32[]{:S(2)}, u32[]{:S(2)}) collective-permute-start(bf16[8,128,128]{2,1,0:T(8,128)(2,1)S(1)} %slice.10), channel_id=1, source_target_pairs={{0,32},{32,64},{64,96},{96,128},{128,160},{160,192},{192,224},{224... | collective-permute-start | bytes 786440 | tf_op jit(solution)/shard_map/ppermute | solution.py:405
  102.8 11.7 %collective-permute-start.11 = (bf16[8,128,128]{2,1,0:T(8,128)(2,1)S(1)}, bf16[8,128,128]{2,1,0:T(8,128)(2,1)S(1)}, u32[]{:S(2)}, u32[]{:S(2)}) collective-permute-start(bf16[8,128,128]{2,1,0:T(8,128)(2,1)S(1)} %slice.11), channel_id=1, source_target_pairs={{0,224},{32,0},{64,32},{96,64},{128,96},{160,128},{192,160},{224,1... | collective-permute-start | bytes 786440 | tf_op jit(solution)/shard_map/ppermute | solution.py:405
  110.4 6.5 %copy-start.1 = (bf16[7,128,128]{2,1,0:T(8,128)(2,1)}, bf16[7,128,128]{2,1,0:T(8,128)(2,1)S(1)}, u32[]{:S(2)}) copy-start(bf16[7,128,128]{2,1,0:T(8,128)(2,1)S(1)} %get-tuple-element.66.early_ref) | copy-start | bytes 688132
  110.4 12.9 %collective-permute-start.14 = (bf16[7,128,128]{2,1,0:T(8,128)(2,1)}, bf16[7,128,128]{2,1,0:T(8,128)(2,1)}, u32[]{:S(2)}, u32[]{:S(2)}) collective-permute-start(bf16[7,128,128]{2,1,0:T(8,128)(2,1)} %get-tuple-element.67), channel_id=1, source_target_pairs={{0,16},{16,0},{1,17},{17,1},{2,18},{18,2},{3,19},{19,3},{4,20},{20... | collective-permute-start | bytes 688136 | tf_op jit(solution)/shard_map/ppermute | solution.py:426
  114.5 0.7 copy-start.11
  114.5 0.8 copy-start.12
  114.5 2.3 %copy-start.8 = (bf16[4,16,64,128]{3,2,1,0:T(8,128)(2,1)}, bf16[4,16,64,128]{3,2,1,0:T(8,128)(2,1)S(1)}, u32[]{:S(2)}) copy-start(bf16[4,16,64,128]{3,2,1,0:T(8,128)(2,1)S(1)} %collective-permute-done.12.refs_1_) | copy-start | bytes 3145732
  114.6 2.3 %copy-start.9 = (bf16[4,16,64,128]{3,2,1,0:T(8,128)(2,1)}, bf16[4,16,64,128]{3,2,1,0:T(8,128)(2,1)S(1)}, u32[]{:S(2)}) copy-start(bf16[4,16,64,128]{3,2,1,0:T(8,128)(2,1)S(1)} %collective-permute-done.13.refs_2_) | copy-start | bytes 3145732
  116.9 6.4 %collective-permute-start.15 = (bf16[1,128,128]{2,1,0:T(8,128)(2,1)S(1)}, bf16[1,128,128]{2,1,0:T(8,128)(2,1)S(1)}, u32[]{:S(2)}, u32[]{:S(2)}) collective-permute-start(bf16[1,128,128]{2,1,0:T(8,128)(2,1)S(1)} %get-tuple-element.71), channel_id=1, source_target_pairs={{0,16},{16,0},{1,17},{17,1},{2,18},{18,2},{3,19},{19,3},{4,20},{20... | collective-permute-start | bytes 98312 | tf_op jit(solution)/shard_map/ppermute | solution.py:426
  117.7 17.3 %collective-permute-start.16 = (bf16[8,128,128]{2,1,0:T(8,128)(2,1)}, bf16[8,128,128]{2,1,0:T(8,128)(2,1)S(1)}, u32[]{:S(2)}, u32[]{:S(2)}) collective-permute-start(bf16[8,128,128]{2,1,0:T(8,128)(2,1)} %dynamic-slice_bitcast_fusion), channel_id=1, source_target_pairs={{0,16},{16,0},{1,17},{17,1},{2,18},{18,2},{3,19},{19,3},{4,20},{20... | collective-permute-start | bytes 786440 | tf_op jit(solution)/shard_map/ppermute | solution.py:426
  118.2 22.4 %all-to-all-start.1 = ((bf16[16,128,128]{2,1,0:T(8,128)(2,1)}), bf16[16,128,128]{2,1,0:T(8,128)(2,1)S(1)}, u32[]{:S(2)}, u32[]{:S(2)}) async-start(bf16[16,128,128]{2,1,0:T(8,128)(2,1)} %get-tuple-element.72), calls=%async_computation.1 | async-start | bytes 1048576 | tf_op jit(solution)/shard_map/all_to_all | solution.py:480
  123.3 26.1 %collective-permute-start.17 = (bf16[4,16,64,128]{3,2,1,0:T(8,128)(2,1)}, bf16[4,16,64,128]{3,2,1,0:T(8,128)(2,1)}, u32[]{:S(2)}, u32[]{:S(2)}) collective-permute-start(bf16[4,16,64,128]{3,2,1,0:T(8,128)(2,1)} %copy-done.8), channel_id=1, source_target_pairs={{0,4},{4,8},{8,12},{12,0},{1,5},{5,9},{9,13},{13,1},{2,6},{6,10},{... | collective-permute-start | bytes 3145736 | tf_op jit(solution)/shard_map/ppermute | solution.py:405
  123.3 0.9 copy-start.2
  140.6 42.5 %all-to-all-start.2 = ((bf16[16,3,128,128]{3,2,1,0:T(8,128)(2,1)}), bf16[16,3,128,128]{3,2,1,0:T(8,128)(2,1)S(1)}, u32[]{:S(2)}, u32[]{:S(2)}) async-start(bf16[16,3,128,128]{3,2,1,0:T(8,128)(2,1)} %backward.1), calls=%async_computation.2 | async-start | bytes 3145728 | tf_op jit(solution)/shard_map/all_to_all | solution.py:488
  144.2 9.6 %collective-permute-start.22 = (bf16[4,16,64,128]{3,2,1,0:T(8,128)(2,1)}, bf16[4,16,64,128]{3,2,1,0:T(8,128)(2,1)}, u32[]{:S(2)}, u32[]{:S(2)}) collective-permute-start(bf16[4,16,64,128]{3,2,1,0:T(8,128)(2,1)} %copy-done.3), channel_id=1, source_target_pairs={{0,16},{16,0},{1,17},{17,1},{2,18},{18,2},{3,19},{19,3},{4,20},{20... | collective-permute-start | bytes 3145736 | tf_op jit(solution)/shard_map/ppermute | solution.py:426
  144.3 11.1 %collective-permute-start.23 = (bf16[4,16,64,128]{3,2,1,0:T(8,128)(2,1)}, bf16[4,16,64,128]{3,2,1,0:T(8,128)(2,1)}, u32[]{:S(2)}, u32[]{:S(2)}) collective-permute-start(bf16[4,16,64,128]{3,2,1,0:T(8,128)(2,1)} %copy-done.8), channel_id=1, source_target_pairs={{0,16},{16,0},{1,17},{17,1},{2,18},{18,2},{3,19},{19,3},{4,20},{20... | collective-permute-start | bytes 3145736 | tf_op jit(solution)/shard_map/ppermute | solution.py:426
  144.8 12.0 %collective-permute-start.24 = (bf16[4,16,64,128]{3,2,1,0:T(8,128)(2,1)}, bf16[4,16,64,128]{3,2,1,0:T(8,128)(2,1)}, u32[]{:S(2)}, u32[]{:S(2)}) collective-permute-start(bf16[4,16,64,128]{3,2,1,0:T(8,128)(2,1)} %copy-done.9), channel_id=1, source_target_pairs={{0,16},{16,0},{1,17},{17,1},{2,18},{18,2},{3,19},{19,3},{4,20},{20... | collective-permute-start | bytes 3145736 | tf_op jit(solution)/shard_map/ppermute | solution.py:426
  149.4 7.4 %collective-permute-start.25 = (bf16[4,16,64,128]{3,2,1,0:T(8,128)(2,1)}, bf16[4,16,64,128]{3,2,1,0:T(8,128)(2,1)}, u32[]{:S(2)}, u32[]{:S(2)}) collective-permute-start(bf16[4,16,64,128]{3,2,1,0:T(8,128)(2,1)} %collective-permute-done.17.refs_3_), channel_id=1, source_target_pairs={{0,16},{16,0},{1,17},{17,1},{2,18},{18,2},{3,19},{19,3},{4,20},{20... | collective-permute-start | bytes 3145736 | tf_op jit(solution)/shard_map/ppermute | solution.py:426
  150.4 3.1 %collective-permute-start.18 = (bf16[16,128,128]{2,1,0:T(8,128)(2,1)}, bf16[16,128,128]{2,1,0:T(8,128)(2,1)S(1)}, u32[]{:S(2)}, u32[]{:S(2)}) collective-permute-start(bf16[16,128,128]{2,1,0:T(8,128)(2,1)} %get-tuple-element.77), channel_id=1, source_target_pairs={{0,16},{16,0},{1,17},{17,1},{2,18},{18,2},{3,19},{19,3},{4,20},{20... | collective-permute-start | bytes 1572872 | tf_op jit(solution)/shard_map/ppermute | solution.py:426
  153.7 9.1 %collective-permute-start.19 = (bf16[4,128,128]{2,1,0:T(8,128)(2,1)S(1)}, bf16[4,128,128]{2,1,0:T(8,128)(2,1)S(1)}, u32[]{:S(2)}, u32[]{:S(2)}) collective-permute-start(bf16[4,128,128]{2,1,0:T(8,128)(2,1)S(1)} %get-tuple-element.93), channel_id=1, source_target_pairs={{0,4},{4,8},{8,12},{12,0},{1,5},{5,9},{9,13},{13,1},{2,6},{6,10},{... | collective-permute-start | bytes 393224 | tf_op jit(solution)/shard_map/ppermute | solution.py:405
  153.8 9.0 %collective-permute-start.20 = (bf16[4,128,128]{2,1,0:T(8,128)(2,1)S(1)}, bf16[4,128,128]{2,1,0:T(8,128)(2,1)S(1)}, u32[]{:S(2)}, u32[]{:S(2)}) collective-permute-start(bf16[4,128,128]{2,1,0:T(8,128)(2,1)S(1)} %get-tuple-element.92), channel_id=1, source_target_pairs={{0,8},{4,12},{8,0},{12,4},{1,9},{5,13},{9,1},{13,5},{2,10},{6,14},... | collective-permute-start | bytes 393224 | tf_op jit(solution)/shard_map/ppermute | solution.py:405
  155.4 7.6 %collective-permute-start.21 = (bf16[4,128,128]{2,1,0:T(8,128)(2,1)S(1)}, bf16[4,128,128]{2,1,0:T(8,128)(2,1)S(1)}, u32[]{:S(2)}, u32[]{:S(2)}) collective-permute-start(bf16[4,128,128]{2,1,0:T(8,128)(2,1)S(1)} %get-tuple-element.91), channel_id=1, source_target_pairs={{0,12},{4,0},{8,4},{12,8},{1,13},{5,1},{9,5},{13,9},{2,14},{6,2},{... | collective-permute-start | bytes 393224 | tf_op jit(solution)/shard_map/ppermute | solution.py:405
  163.1 5.5 %collective-permute-start.26 = (bf16[4,128,128]{2,1,0:T(8,128)(2,1)S(1)}, bf16[4,128,128]{2,1,0:T(8,128)(2,1)S(1)}, u32[]{:S(2)}, u32[]{:S(2)}) collective-permute-start(bf16[4,128,128]{2,1,0:T(8,128)(2,1)S(1)} %add_convert_fusion.1), channel_id=1, source_target_pairs={{0,1},{1,2},{2,3},{3,0},{4,5},{5,6},{6,7},{7,4},{8,9},{9,10},{10,1... | collective-permute-start | bytes 393224 | tf_op jit(solution)/shard_map/ppermute | solution.py:405
  164.4 7.9 %collective-permute-start.27 = (bf16[4,128,128]{2,1,0:T(8,128)(2,1)S(1)}, bf16[4,128,128]{2,1,0:T(8,128)(2,1)S(1)}, u32[]{:S(2)}, u32[]{:S(2)}) collective-permute-start(bf16[4,128,128]{2,1,0:T(8,128)(2,1)S(1)} %add_convert_fusion.1), channel_id=1, source_target_pairs={{0,2},{1,3},{2,0},{3,1},{4,6},{5,7},{6,4},{7,5},{8,10},{9,11},{10,... | collective-permute-start | bytes 393224 | tf_op jit(solution)/shard_map/ppermute | solution.py:405
  167.2 5.5 %collective-permute-start.28 = (bf16[4,128,128]{2,1,0:T(8,128)(2,1)S(1)}, bf16[4,128,128]{2,1,0:T(8,128)(2,1)S(1)}, u32[]{:S(2)}, u32[]{:S(2)}) collective-permute-start(bf16[4,128,128]{2,1,0:T(8,128)(2,1)S(1)} %add_convert_fusion.1), channel_id=1, source_target_pairs={{0,3},{1,0},{2,1},{3,2},{4,7},{5,4},{6,5},{7,6},{8,11},{9,8},{10,9... | collective-permute-start | bytes 393224 | tf_op jit(solution)/shard_map/ppermute | solution.py:405
  172.8 6.3 %collective-permute-start.29 = (bf16[4,128,128]{2,1,0:T(8,128)(2,1)S(1)}, bf16[4,128,128]{2,1,0:T(8,128)(2,1)S(1)}, u32[]{:S(2)}, u32[]{:S(2)}) collective-permute-start(bf16[4,128,128]{2,1,0:T(8,128)(2,1)S(1)} %multiply_convert_fusion.refs_0_), channel_id=1, source_target_pairs={{0,4},{4,8},{8,12},{12,0},{1,5},{5,9},{9,13},{13,1},{2,6},{6,10},{... | collective-permute-start | bytes 393224 | tf_op jit(solution)/shard_map/ppermute | solution.py:405
  173.5 8.8 %collective-permute-start.30 = (bf16[4,128,128]{2,1,0:T(8,128)(2,1)S(1)}, bf16[4,128,128]{2,1,0:T(8,128)(2,1)S(1)}, u32[]{:S(2)}, u32[]{:S(2)}) collective-permute-start(bf16[4,128,128]{2,1,0:T(8,128)(2,1)S(1)} %multiply_convert_fusion.refs_0_), channel_id=1, source_target_pairs={{0,8},{4,12},{8,0},{12,4},{1,9},{5,13},{9,1},{13,5},{2,10},{6,14},... | collective-permute-start | bytes 393224 | tf_op jit(solution)/shard_map/ppermute | solution.py:405
  177.6 5.5 %collective-permute-start.31 = (bf16[4,128,128]{2,1,0:T(8,128)(2,1)S(1)}, bf16[4,128,128]{2,1,0:T(8,128)(2,1)S(1)}, u32[]{:S(2)}, u32[]{:S(2)}) collective-permute-start(bf16[4,128,128]{2,1,0:T(8,128)(2,1)S(1)} %multiply_convert_fusion.refs_0_), channel_id=1, source_target_pairs={{0,12},{4,0},{8,4},{12,8},{1,13},{5,1},{9,5},{13,9},{2,14},{6,2},{... | collective-permute-start | bytes 393224 | tf_op jit(solution)/shard_map/ppermute | solution.py:405

commit v6 on v5

--- a/solution.py
+++ b/solution.py
@@ -371,33 +371,47 @@
     )(cols, core, mine, *(in_hbm(w) for w in own + other))
 
 
-def unpack_kernel(groups, places_ref, grads_ref, *refs):
-    part_refs = refs[:groups]
-    dq_ref, dk_ref, dv_ref, pg_ref = refs[groups:]
+def unpack_kernel(grads_ref, dq_ref, dk_ref, dv_ref):
     for h in range(grads_ref.shape[0]):
         cols = slice(h * HEAD_DIM, (h + 1) * HEAD_DIM)
         dq_ref[:, cols] = grads_ref[h, 0]
         dk_ref[:, cols] = grads_ref[h, 1]
         dv_ref[:, cols] = grads_ref[h, 2]
-    wide = groups * BLOCK
-    for i in range(groups):
-        for t in range(groups):
+
+
+def unpack(grads):
+    wide = like(BLOCK, grads.shape[0] * HEAD_DIM)
+    return pl.pallas_call(
+        unpack_kernel,
+        out_shape=(wide, wide, wide),
+        in_specs=[VM],
+        out_specs=(VM,) * 3,
+        compiler_params=pltpu.CompilerParams(vmem_limit_bytes=24 * MIB),
+        cost_estimate=cost(2 * MICROSECOND),
+        name="unpack",
+    )(grads)
+
+
+def assemble_kernel(places_ref, *refs):
+    part_refs, pg_ref = refs[:-1], refs[-1]
+    wide = part_refs[0].shape[0] * BLOCK
+    for i, part_ref in enumerate(part_refs):
+        for t in range(part_ref.shape[0]):
             at = pl.ds(pl.multiple_of(places_ref[i] * wide + t * BLOCK, BLOCK), BLOCK)
-            pg_ref[:, at] = part_refs[i][t].astype(F32)
-
-
-def unpack(places, grads, parts):
-    wide = like(BLOCK, grads.shape[0] * HEAD_DIM)
+            pg_ref[:, at] = part_ref[t].astype(F32)
+
+
+def assemble(places, parts):
     groups = len(parts)
     return pl.pallas_call(
-        functools.partial(unpack_kernel, groups),
-        out_shape=(wide, wide, wide, like(HEAD_DIM, groups * groups * BLOCK, dtype=F32)),
-        in_specs=[SM, VM] + [VM] * groups,
-        out_specs=(VM,) * 4,
-        compiler_params=pltpu.CompilerParams(vmem_limit_bytes=24 * MIB),
-        cost_estimate=cost(3 * MICROSECOND),
-        name="unpack",
-    )(places, grads, *parts)
+        assemble_kernel,
+        out_shape=like(HEAD_DIM, groups * parts[0].shape[0] * BLOCK, dtype=F32),
+        in_specs=[SM] + [VM] * groups,
+        out_specs=VM,
+        compiler_params=pltpu.CompilerParams(vmem_limit_bytes=24 * MIB),
+        cost_estimate=cost(MICROSECOND),
+        name="assemble",
+    )(places, *parts)
 
 
 def shifted(value, axis, by):
@@ -499,7 +513,9 @@
     pg = total_of(from_others(total_of(pg_pieces).astype(BF16), "y"))
     pg = (pg * (1.0 / math.sqrt(tokens))).astype(BF16)
     pg_pieces = from_others(pg, "x")
-    dq, dk, dv, proj_grad = unpack((x - index) % groups, grad_rows, pg_pieces)
+    dq, dk, dv = unpack(grad_rows)
+    pg_pieces, dq, dk, dv = lax.optimization_barrier((pg_pieces, dq, dk, dv))
+    proj_grad = assemble((x - index) % groups, pg_pieces)
     return layer[None], dq[None], dk[None], dv[None], proj_grad
 
 

time: 187 us -> 186 us (level)
    ppermute x23, waiting for transfers between devices: 69.1 us -> 63.6 us  [shifted(): lax.ppermute(value, axis, [(i, (i + by) % size) for i in range(size)])]
    all_to_all x1, waiting for transfers between devices: 0.01 us -> 4.35 us  [body(): lax.all_to_all(grads, seq, split_axis=0, concat_axis=0, tiled=True)]
  transfers between devices with their start and end apart: 35 -> 35, of which waited for: 13 -> 11; matrix products, arithmetic and copies ran while one was open for 1% -> 1% of each run, Pallas kernels for 20% -> 21%
where the time goes in v6:
time: 186 us; the launch traced here: 185 us
  waiting for transfers between devices  76.5 us (41%)
  starting transfers between devices  59.4 us (32%)
  Pallas kernels  43.9 us (24%)
  local copies, waits for them, and re-layouts  2.75 us (1%)
    ppermute x23, waiting for transfers between devices, shifted(): lax.ppermute(value, axis, [(i, (i + by) % size) for i in range(size)])  63.6 us
    ppermute x23, starting transfers between devices, shifted(): lax.ppermute(value, axis, [(i, (i + by) % size) for i in range(size)])  31.3 us
    pallas_call x1, Pallas kernels, backward(): pl.pallas_call(backward_kernel, out_shape=like(count, 3, BLOCK, HEAD_DIM)...  10.7 us
    pallas_call x1, Pallas kernels, forward(): pl.pallas_call(forward_kernel, out_shape=(like(count, BLOCK, HEAD_DIM), l...  10.6 us
    all_to_all x1, starting transfers between devices, body(): qkv = lax.all_to_all(qkv_out, seq, split_axis=0, concat_axis=0, tiled=True)  10.1 us
    ppermute x9, starting transfers between devices, swapped(): return lax.ppermute(value, 'c', [(0, 1), (1, 0)])  9.32 us
    pallas_call x2, Pallas kernels, attn_grad(): pl.pallas_call(functools.partial(attn_grad_kernel, parts), out_shape=(lik...  6.12 us
    pallas_call x1, Pallas kernels, project(): pl.pallas_call(functools.partial(project_kernel, pieces), out_shape=like(...  6.03 us
  transfers between devices with their start and end apart: 35, of which 11 were waited for; matrix products, arithmetic and copies ran while one was open for 1% of the time, Pallas kernels for 21%

profile of v6, /device:TPU:1, one launch (start us, length us, event | category | flops | bytes accessed | tf_op | source)
XLA Modules:
  0.0 185.1 jit_solution(12487050133963013625)
XLA Ops:
  0.6 3.1 %pack.1 = (bf16[16,448,128]{2,1,0:T(8,128)(2,1)}, bf16[16,128,128]{2,1,0:T(8,128)(2,1)}) custom-call(s32[1]{0:T(128)} %bitcast.3.place_ref, bf16[128,2048]{1,0:T(8,128)(2,1)} %bitcast.36, bf16[128,2048]{1,0:T(8,128)(2,1)} %bitcast.37, bf16[128,2048]{1,0:T(8,128)(2,1)} %bitcast.38, bf16[128,2048]{1,0:T(8,128)(2,1)} %bitcast.39, bf16[128,2048]{1,0:T(8,128)(2,1)} %mine_ref.3), custom_call_target="tpu_custom_call" | custom-call | flops 3449999872 | tf_op jit(solution)/shard_map/pack/pallas_call | solution.py:77
  3.8 10.1 %all-to-all-start = ((bf16[16,448,128]{2,1,0:T(8,128)(2,1)}), bf16[16,448,128]{2,1,0:T(8,128)(2,1)S(1)}, u32[]{:S(2)}, u32[]{:S(2)}) async-start(bf16[16,448,128]{2,1,0:T(8,128)(2,1)} %get-tuple-element.54), calls=%async_computation | async-start | bytes 3670016 | tf_op jit(solution)/shard_map/all_to_all | solution.py:456
  14.0 1.5 collective-permute-start
  15.4 1.3 collective-permute-start.1
  16.7 51.5 %collective-permute-done.refs_1_ = bf16[16,128,128]{2,1,0:T(8,128)(2,1)} collective-permute-done((bf16[16,128,128]{2,1,0:T(8,128)(2,1)S(1)}, bf16[16,128,128]{2,1,0:T(8,128)(2,1)}, u32[]{:S(2)}, u32[]{:S(2)}) %collective-permute-start) | collective-permute-done | bytes 524320 | tf_op jit(solution)/shard_map/ppermute | solution.py:419
  68.4 2.5 %collective-permute-start.3 = (bf16[16,128,128]{2,1,0:T(8,128)(2,1)}, bf16[16,128,128]{2,1,0:T(8,128)(2,1)}, u32[]{:S(2)}, u32[]{:S(2)}) collective-permute-start(bf16[16,128,128]{2,1,0:T(8,128)(2,1)} %collective-permute-done.1.refs_2_), channel_id=1, source_target_pairs={{0,224},{32,0},{64,32},{96,64},{128,96},{160,128},{192,160},{224,1... | collective-permute-start | bytes 1572872 | tf_op jit(solution)/shard_map/ppermute | solution.py:419
  70.9 1.4 collective-permute-start.4
  72.3 2.7 %collective-permute-start.5 = (bf16[16,64,128]{2,1,0:T(8,128)(2,1)S(1)}, bf16[16,64,128]{2,1,0:T(8,128)(2,1)S(1)}, u32[]{:S(2)}, u32[]{:S(2)}) collective-permute-start(bf16[16,64,128]{2,1,0:T(8,128)(2,1)S(1)} %slice.9), channel_id=1, source_target_pairs={{0,2},{1,3},{2,0},{3,1},{4,6},{5,7},{6,4},{7,5},{8,10},{9,11},{10,... | collective-permute-start | bytes 786440 | tf_op jit(solution)/shard_map/ppermute | solution.py:419
  74.9 1.0 collective-permute-start.6
  76.1 2.7 %collective-permute-done.4 = bf16[16,64,128]{2,1,0:T(8,128)(2,1)S(1)} collective-permute-done((bf16[16,64,128]{2,1,0:T(8,128)(2,1)S(1)}, bf16[16,64,128]{2,1,0:T(8,128)(2,1)S(1)}, u32[]{:S(2)}, u32[]{:S(2)}) %collective-permute-start.4) | collective-permute-done | bytes 262176 | tf_op jit(solution)/shard_map/ppermute | solution.py:419
  78.9 2.9 %collective-permute-start.9 = (bf16[128,2048]{1,0:T(8,128)(2,1)S(1)}, bf16[128,2048]{1,0:T(8,128)(2,1)S(1)}, u32[]{:S(2)}, u32[]{:S(2)}) collective-permute-start(bf16[128,2048]{1,0:T(8,128)(2,1)S(1)} %copy-done), channel_id=1, source_target_pairs={{0,16},{16,0},{1,17},{17,1},{2,18},{18,2},{3,19},{19,3},{4,20},{20... | collective-permute-start | bytes 1572872 | tf_op jit(solution)/shard_map/ppermute | solution.py:440
  81.8 3.7 %collective-permute-done.5 = bf16[16,64,128]{2,1,0:T(8,128)(2,1)S(1)} collective-permute-done((bf16[16,64,128]{2,1,0:T(8,128)(2,1)S(1)}, bf16[16,64,128]{2,1,0:T(8,128)(2,1)S(1)}, u32[]{:S(2)}, u32[]{:S(2)}) %collective-permute-start.5) | collective-permute-done | bytes 262176 | tf_op jit(solution)/shard_map/ppermute | solution.py:419
  85.5 1.1 pad_maximum_fusion.refs_0_
  86.6 1.3 collective-permute-start.12
  87.8 1.5 collective-permute-start.13
  89.3 2.7 %collective-permute-start.8 = (bf16[16,128,128]{2,1,0:T(8,128)(2,1)}, bf16[16,128,128]{2,1,0:T(8,128)(2,1)S(1)}, u32[]{:S(2)}, u32[]{:S(2)}) collective-permute-start(bf16[16,128,128]{2,1,0:T(8,128)(2,1)} %collective-permute-done.3.refs_4_), channel_id=1, source_target_pairs={{0,224},{32,0},{64,32},{96,64},{128,96},{160,128},{192,160},{224,1... | collective-permute-start | bytes 1572872 | tf_op jit(solution)/shard_map/ppermute | solution.py:419
  92.0 10.6 %forward.1 = (bf16[16,128,128]{2,1,0:T(8,128)(2,1)}, bf16[16,128,128]{2,1,0:T(8,128)(2,1)S(1)}, f32[16,1,128]{2,1,0:T(1,128)S(1)}) custom-call(s32[16,8]{1,0:T(8,128)S(1)} %copy.12.blocks_ref, bf16[16,448,128]{2,1,0:T(8,128)(2,1)S(1)} %all-to-all-done.qkv_ref), custom_call_target="tpu_custom_call" | custom-call | flops 13799999488 | tf_op jit(solution)/shard_map/forward/pallas_call | solution.py:136
  102.8 2.9 %collective-permute-start.11 = (bf16[8,128,128]{2,1,0:T(8,128)(2,1)S(1)}, bf16[8,128,128]{2,1,0:T(8,128)(2,1)S(1)}, u32[]{:S(2)}, u32[]{:S(2)}) collective-permute-start(bf16[8,128,128]{2,1,0:T(8,128)(2,1)S(1)} %slice.11), channel_id=1, source_target_pairs={{0,224},{32,0},{64,32},{96,64},{128,96},{160,128},{192,160},{224,1... | collective-permute-start | bytes 786440 | tf_op jit(solution)/shard_map/ppermute | solution.py:419
  105.7 4.6 %attn_grad.2 = (bf16[7,128,128]{2,1,0:T(8,128)(2,1)S(1)}, bf16[7,128,128]{2,1,0:T(8,128)(2,1)}) custom-call(bf16[128,2048]{1,0:T(8,128)(2,1)S(1)} %copy-done, bf16[128,2048]{1,0:T(8,128)(2,1)S(1)} %collective-permute-done.9.theirs_ref, bf16[16,128,128]{2,1,0:T(8,128)(2,1)} %get-tuple-element.55.refs_0_, bf16[16,128,128]{2,1,0:T(8,128)(2,1)} %collective-permute-done.refs_1_, ...), custom_call_target="tpu_custom_call" | custom-call | flops 4600000000 | tf_op jit(solution)/shard_map/attn_grad/pallas_call | solution.py:191
  110.4 4.1 %collective-permute-start.14 = (bf16[7,128,128]{2,1,0:T(8,128)(2,1)}, bf16[7,128,128]{2,1,0:T(8,128)(2,1)}, u32[]{:S(2)}, u32[]{:S(2)}) collective-permute-start(bf16[7,128,128]{2,1,0:T(8,128)(2,1)} %get-tuple-element.73), channel_id=1, source_target_pairs={{0,16},{16,0},{1,17},{17,1},{2,18},{18,2},{3,19},{19,3},{4,20},{20... | collective-permute-start | bytes 688136 | tf_op jit(solution)/shard_map/ppermute | solution.py:440
  114.6 0.6 copy-done.11
  115.3 1.5 attn_grad.3
  117.0 0.7 dynamic-slice_bitcast_fusion
  117.7 0.5 collective-permute-start.16
  118.2 5.1 %all-to-all-start.1 = ((bf16[16,128,128]{2,1,0:T(8,128)(2,1)}), bf16[16,128,128]{2,1,0:T(8,128)(2,1)S(1)}, u32[]{:S(2)}, u32[]{:S(2)}) async-start(bf16[16,128,128]{2,1,0:T(8,128)(2,1)} %get-tuple-element.78), calls=%async_computation.1 | async-start | bytes 1048576 | tf_op jit(solution)/shard_map/all_to_all | solution.py:494
  123.3 0.9 copy-done.2
  124.2 10.7 %backward.1 = bf16[16,3,128,128]{3,2,1,0:T(8,128)(2,1)} custom-call(s32[16,8]{1,0:T(8,128)S(1)} %copy.12.blocks_ref, s32[10]{0:T(128)S(1)} %pad_add_fusion.place_ref, bf16[16,448,128]{2,1,0:T(8,128)(2,1)S(1)} %all-to-all-done.qkv_ref, bf16[16,128,128]{2,1,0:T(8,128)(2,1)S(1)} %get-tuple-element.57.attn_t_ref.attn_ref, ...), custom_call_target="tpu_custom_call" | custom-call | flops 14949999616 | tf_op jit(solution)/shard_map/backward/pallas_call | solution.py:315
  135.0 5.6 %all-to-all-done.1.mine_ref = bf16[16,128,128]{2,1,0:T(8,128)(2,1)S(1)} async-done(((bf16[16,128,128]{2,1,0:T(8,128)(2,1)}), bf16[16,128,128]{2,1,0:T(8,128)(2,1)S(1)}, u32[]{:S(2)}, u32[]{:S(2)}) %all-to-all-start.1) | async-done | bytes 524320 | tf_op jit(solution)/shard_map/all_to_all | solution.py:494
  140.6 3.6 %all-to-all-start.2 = ((bf16[16,3,128,128]{3,2,1,0:T(8,128)(2,1)}), bf16[16,3,128,128]{3,2,1,0:T(8,128)(2,1)S(1)}, u32[]{:S(2)}, u32[]{:S(2)}) async-start(bf16[16,3,128,128]{3,2,1,0:T(8,128)(2,1)} %backward.1), calls=%async_computation.2 | async-start | bytes 3145728 | tf_op jit(solution)/shard_map/all_to_all | solution.py:502
  144.3 0.5 collective-permute-start.23
  144.9 4.0 %weight_grad.1 = (bf16[16,128,128]{2,1,0:T(8,128)(2,1)S(1)}, bf16[16,128,128]{2,1,0:T(8,128)(2,1)}) custom-call(s32[10]{0:T(128)S(1)} %pad_add_fusion.place_ref, bf16[16,128,128]{2,1,0:T(8,128)(2,1)S(1)} %get-tuple-element.57.attn_t_ref.attn_ref, bf16[8,128,128]{2,1,0:T(8,128)(2,1)S(1)} %collective-permute-done.16.other_ref, ...), custom_call_target="tpu_custom_call" | custom-call | flops 4600000000 | tf_op jit(solution)/shard_map/weight_grad/pallas_call | solution.py:236
  148.9 0.4 collective-permute-done.17.refs_3_
  149.4 1.0 collective-permute-start.25
  150.6 2.9 %collective-permute-done.18 = bf16[16,128,128]{2,1,0:T(8,128)(2,1)S(1)} collective-permute-done((bf16[16,128,128]{2,1,0:T(8,128)(2,1)}, bf16[16,128,128]{2,1,0:T(8,128)(2,1)S(1)}, u32[]{:S(2)}, u32[]{:S(2)}) %collective-permute-start.18) | collective-permute-done | bytes 524320 | tf_op jit(solution)/shard_map/ppermute | solution.py:440
  153.8 1.6 collective-permute-start.20
  155.4 1.3 collective-permute-start.21
  156.8 6.0 %project.1 = bf16[128,2048]{1,0:T(8,128)(2,1)} custom-call(s32[16]{0:T(128)S(1)} %add.120.cols_ref, s32[1]{0:T(128)} %bitcast.1.core_ref, bf16[16,128,128]{2,1,0:T(8,128)(2,1)S(1)} %all-to-all-done.1.mine_ref, bf16[4,16,64,128]{3,2,1,0:T(8,128)(2,1)} %copy-done.3, bf16[4,16,64,128]{3,2,1,0:T(8,128)(2,1)} %copy-done.8, bf16[4,16,64,128]{3,2,1,0:T(8,128)(2,1)} %copy-done.9, ...), custom_call_target="tpu_custom_call" | custom-call | flops 6899999744 | tf_op jit(solution)/shard_map/project/pallas_call | solution.py:362
  163.1 1.2 collective-permute-start.26
  164.4 2.8 %collective-permute-start.27 = (bf16[4,128,128]{2,1,0:T(8,128)(2,1)S(1)}, bf16[4,128,128]{2,1,0:T(8,128)(2,1)S(1)}, u32[]{:S(2)}, u32[]{:S(2)}) collective-permute-start(bf16[4,128,128]{2,1,0:T(8,128)(2,1)S(1)} %add_convert_fusion.1), channel_id=1, source_target_pairs={{0,2},{1,3},{2,0},{3,1},{4,6},{5,7},{6,4},{7,5},{8,10},{9,11},{10,... | collective-permute-start | bytes 393224 | tf_op jit(solution)/shard_map/ppermute | solution.py:419
  167.2 0.4 collective-permute-start.28
  167.6 1.0 collective-permute-done.26
  168.7 3.6 %collective-permute-done.27 = bf16[4,128,128]{2,1,0:T(8,128)(2,1)S(1)} collective-permute-done((bf16[4,128,128]{2,1,0:T(8,128)(2,1)S(1)}, bf16[4,128,128]{2,1,0:T(8,128)(2,1)S(1)}, u32[]{:S(2)}, u32[]{:S(2)}) %collective-permute-start.27) | collective-permute-done | bytes 131104 | tf_op jit(solution)/shard_map/ppermute | solution.py:419
  172.2 0.5 collective-permute-done.28
  172.8 0.7 collective-permute-start.29
  173.5 4.1 %collective-permute-start.30 = (bf16[4,128,128]{2,1,0:T(8,128)(2,1)S(1)}, bf16[4,128,128]{2,1,0:T(8,128)(2,1)S(1)}, u32[]{:S(2)}, u32[]{:S(2)}) collective-permute-start(bf16[4,128,128]{2,1,0:T(8,128)(2,1)S(1)} %multiply_convert_fusion.refs_0_), channel_id=1, source_target_pairs={{0,8},{4,12},{8,0},{12,4},{1,9},{5,13},{9,1},{13,5},{2,10},{6,14},... | collective-permute-start | bytes 393224 | tf_op jit(solution)/shard_map/ppermute | solution.py:419
  177.6 4.4 %all-to-all-done.2.grads_ref = bf16[16,3,128,128]{3,2,1,0:T(8,128)(2,1)S(1)} async-done(((bf16[16,3,128,128]{3,2,1,0:T(8,128)(2,1)}), bf16[16,3,128,128]{3,2,1,0:T(8,128)(2,1)S(1)}, u32[]{:S(2)}, u32[]{:S(2)}) %all-to-all-start.2) | async-done | bytes 1572896 | tf_op jit(solution)/shard_map/all_to_all | solution.py:502
  181.9 1.6 unpack.1
  183.5 1.6 assemble.1
  (72 shorter events, 1.9 us)
Async XLA Ops:
  3.8 10.2 %copy-start.10 = (bf16[16,128,128]{2,1,0:T(8,128)(2,1)S(1)}, bf16[16,128,128]{2,1,0:T(8,128)(2,1)}, u32[]{:S(2)}) copy-start(bf16[16,128,128]{2,1,0:T(8,128)(2,1)} %get-tuple-element.55.refs_0_) | copy-start | bytes 1572868
  3.8 72.2 %copy-start.6 = (s32[1,16,8]{1,2,0:T(8,128)S(1)}, s32[1,16,8]{1,2,0:T(8,128)}, u32[]{:S(2)}) copy-start(s32[1,16,8]{1,2,0:T(8,128)} %param.12) | copy-start | bytes 1540
  3.8 72.2 %copy-start.7 = (s32[8]{0:T(128)S(1)}, s32[8]{0:T(128)}, u32[]{:S(2)}) copy-start(s32[8]{0:T(128)} %constant.87.clone) | copy-start | bytes 100
  3.8 75.0 %copy-start = (bf16[128,2048]{1,0:T(8,128)(2,1)S(1)}, bf16[128,2048]{1,0:T(8,128)(2,1)}, u32[]{:S(2)}) copy-start(bf16[128,2048]{1,0:T(8,128)(2,1)} %mine_ref.3) | copy-start | bytes 1572868
  3.8 64.4 %all-to-all-start = ((bf16[16,448,128]{2,1,0:T(8,128)(2,1)}), bf16[16,448,128]{2,1,0:T(8,128)(2,1)S(1)}, u32[]{:S(2)}, u32[]{:S(2)}) async-start(bf16[16,448,128]{2,1,0:T(8,128)(2,1)} %get-tuple-element.54), calls=%async_computation | async-start | bytes 3670016 | tf_op jit(solution)/shard_map/all_to_all | solution.py:456
  14.0 54.2 %collective-permute-start = (bf16[16,128,128]{2,1,0:T(8,128)(2,1)S(1)}, bf16[16,128,128]{2,1,0:T(8,128)(2,1)}, u32[]{:S(2)}, u32[]{:S(2)}) collective-permute-start(bf16[16,128,128]{2,1,0:T(8,128)(2,1)S(1)} %copy-done.10), channel_id=1, source_target_pairs={{0,32},{32,64},{64,96},{96,128},{128,160},{160,192},{192,224},{224... | collective-permute-start | bytes 1572872 | tf_op jit(solution)/shard_map/ppermute | solution.py:419
  15.4 52.8 %collective-permute-start.1 = (bf16[16,128,128]{2,1,0:T(8,128)(2,1)S(1)}, bf16[16,128,128]{2,1,0:T(8,128)(2,1)}, u32[]{:S(2)}, u32[]{:S(2)}) collective-permute-start(bf16[16,128,128]{2,1,0:T(8,128)(2,1)S(1)} %copy-done.10), channel_id=1, source_target_pairs={{0,224},{32,0},{64,32},{96,64},{128,96},{160,128},{192,160},{224,1... | collective-permute-start | bytes 1572872 | tf_op jit(solution)/shard_map/ppermute | solution.py:419
  68.2 17.3 %collective-permute-start.2 = (bf16[16,128,128]{2,1,0:T(8,128)(2,1)}, bf16[16,128,128]{2,1,0:T(8,128)(2,1)}, u32[]{:S(2)}, u32[]{:S(2)}) collective-permute-start(bf16[16,128,128]{2,1,0:T(8,128)(2,1)} %collective-permute-done.refs_1_), channel_id=1, source_target_pairs={{0,32},{32,64},{64,96},{96,128},{128,160},{160,192},{192,224},{224... | collective-permute-start | bytes 1572872 | tf_op jit(solution)/shard_map/ppermute | solution.py:419
  68.4 17.0 %collective-permute-start.3 = (bf16[16,128,128]{2,1,0:T(8,128)(2,1)}, bf16[16,128,128]{2,1,0:T(8,128)(2,1)}, u32[]{:S(2)}, u32[]{:S(2)}) collective-permute-start(bf16[16,128,128]{2,1,0:T(8,128)(2,1)} %collective-permute-done.1.refs_2_), channel_id=1, source_target_pairs={{0,224},{32,0},{64,32},{96,64},{128,96},{160,128},{192,160},{224,1... | collective-permute-start | bytes 1572872 | tf_op jit(solution)/shard_map/ppermute | solution.py:419
  70.9 8.0 %collective-permute-start.4 = (bf16[16,64,128]{2,1,0:T(8,128)(2,1)S(1)}, bf16[16,64,128]{2,1,0:T(8,128)(2,1)S(1)}, u32[]{:S(2)}, u32[]{:S(2)}) collective-permute-start(bf16[16,64,128]{2,1,0:T(8,128)(2,1)S(1)} %slice.9), channel_id=1, source_target_pairs={{0,1},{1,2},{2,3},{3,0},{4,5},{5,6},{6,7},{7,4},{8,9},{9,10},{10,1... | collective-permute-start | bytes 786440 | tf_op jit(solution)/shard_map/ppermute | solution.py:419
  72.3 13.2 %collective-permute-start.5 = (bf16[16,64,128]{2,1,0:T(8,128)(2,1)S(1)}, bf16[16,64,128]{2,1,0:T(8,128)(2,1)S(1)}, u32[]{:S(2)}, u32[]{:S(2)}) collective-permute-start(bf16[16,64,128]{2,1,0:T(8,128)(2,1)S(1)} %slice.9), channel_id=1, source_target_pairs={{0,2},{1,3},{2,0},{3,1},{4,6},{5,7},{6,4},{7,5},{8,10},{9,11},{10,... | collective-permute-start | bytes 786440 | tf_op jit(solution)/shard_map/ppermute | solution.py:419
  74.9 10.5 %collective-permute-start.6 = (bf16[16,64,128]{2,1,0:T(8,128)(2,1)S(1)}, bf16[16,64,128]{2,1,0:T(8,128)(2,1)}, u32[]{:S(2)}, u32[]{:S(2)}) collective-permute-start(bf16[16,64,128]{2,1,0:T(8,128)(2,1)S(1)} %slice.9), channel_id=1, source_target_pairs={{0,3},{1,0},{2,1},{3,2},{4,7},{5,4},{6,5},{7,6},{8,11},{9,8},{10,9... | collective-permute-start | bytes 786440 | tf_op jit(solution)/shard_map/ppermute | solution.py:419
  78.9 26.9 %collective-permute-start.9 = (bf16[128,2048]{1,0:T(8,128)(2,1)S(1)}, bf16[128,2048]{1,0:T(8,128)(2,1)S(1)}, u32[]{:S(2)}, u32[]{:S(2)}) collective-permute-start(bf16[128,2048]{1,0:T(8,128)(2,1)S(1)} %copy-done), channel_id=1, source_target_pairs={{0,16},{16,0},{1,17},{17,1},{2,18},{18,2},{3,19},{19,3},{4,20},{20... | collective-permute-start | bytes 1572872 | tf_op jit(solution)/shard_map/ppermute | solution.py:440
  86.5 16.1 %copy-start.3 = (bf16[4,16,64,128]{3,2,1,0:T(8,128)(2,1)}, bf16[4,16,64,128]{3,2,1,0:T(8,128)(2,1)S(1)}, u32[]{:S(2)}) copy-start(bf16[4,16,64,128]{3,2,1,0:T(8,128)(2,1)S(1)} %pad_maximum_fusion.refs_0_) | copy-start | bytes 3145732
  86.6 28.0 %collective-permute-start.12 = (bf16[4,16,64,128]{3,2,1,0:T(8,128)(2,1)S(1)}, bf16[4,16,64,128]{3,2,1,0:T(8,128)(2,1)S(1)}, u32[]{:S(2)}, u32[]{:S(2)}) collective-permute-start(bf16[4,16,64,128]{3,2,1,0:T(8,128)(2,1)S(1)} %pad_maximum_fusion.refs_0_), channel_id=1, source_target_pairs={{0,4},{4,8},{8,12},{12,0},{1,5},{5,9},{9,13},{13,1},{2,6},{6,10},{... | collective-permute-start | bytes 3145736 | tf_op jit(solution)/shard_map/ppermute | solution.py:419
  87.8 26.7 %collective-permute-start.13 = (bf16[4,16,64,128]{3,2,1,0:T(8,128)(2,1)S(1)}, bf16[4,16,64,128]{3,2,1,0:T(8,128)(2,1)S(1)}, u32[]{:S(2)}, u32[]{:S(2)}) collective-permute-start(bf16[4,16,64,128]{3,2,1,0:T(8,128)(2,1)S(1)} %pad_maximum_fusion.refs_0_), channel_id=1, source_target_pairs={{0,12},{4,0},{8,4},{12,8},{1,13},{5,1},{9,5},{13,9},{2,14},{6,2},{... | collective-permute-start | bytes 3145736 | tf_op jit(solution)/shard_map/ppermute | solution.py:419
  89.3 13.3 %collective-permute-start.7 = (bf16[16,128,128]{2,1,0:T(8,128)(2,1)}, bf16[16,128,128]{2,1,0:T(8,128)(2,1)S(1)}, u32[]{:S(2)}, u32[]{:S(2)}) collective-permute-start(bf16[16,128,128]{2,1,0:T(8,128)(2,1)} %collective-permute-done.2.refs_3_), channel_id=1, source_target_pairs={{0,32},{32,64},{64,96},{96,128},{128,160},{160,192},{192,224},{224... | collective-permute-start | bytes 1572872 | tf_op jit(solution)/shard_map/ppermute | solution.py:419
  89.3 13.3 %collective-permute-start.8 = (bf16[16,128,128]{2,1,0:T(8,128)(2,1)}, bf16[16,128,128]{2,1,0:T(8,128)(2,1)S(1)}, u32[]{:S(2)}, u32[]{:S(2)}) collective-permute-start(bf16[16,128,128]{2,1,0:T(8,128)(2,1)} %collective-permute-done.3.refs_4_), channel_id=1, source_target_pairs={{0,224},{32,0},{64,32},{96,64},{128,96},{160,128},{192,160},{224,1... | collective-permute-start | bytes 1572872 | tf_op jit(solution)/shard_map/ppermute | solution.py:419
  102.6 3.1 %copy-start.4 = (bf16[16,128,128]{2,1,0:T(8,128)(2,1)}, bf16[16,128,128]{2,1,0:T(8,128)(2,1)S(1)}, u32[]{:S(2)}) copy-start(bf16[16,128,128]{2,1,0:T(8,128)(2,1)S(1)} %collective-permute-done.7.refs_5_) | copy-start | bytes 1572868
  102.6 3.1 %copy-start.5 = (bf16[16,128,128]{2,1,0:T(8,128)(2,1)}, bf16[16,128,128]{2,1,0:T(8,128)(2,1)S(1)}, u32[]{:S(2)}) copy-start(bf16[16,128,128]{2,1,0:T(8,128)(2,1)S(1)} %collective-permute-done.8.refs_6_) | copy-start | bytes 1572868
  102.7 11.8 %collective-permute-start.10 = (bf16[8,128,128]{2,1,0:T(8,128)(2,1)S(1)}, bf16[8,128,128]{2,1,0:T(8,128)(2,1)S(1)}, u32[]{:S(2)}, u32[]{:S(2)}) collective-permute-start(bf16[8,128,128]{2,1,0:T(8,128)(2,1)S(1)} %slice.10), channel_id=1, source_target_pairs={{0,32},{32,64},{64,96},{96,128},{128,160},{160,192},{192,224},{224... | collective-permute-start | bytes 786440 | tf_op jit(solution)/shard_map/ppermute | solution.py:419
  102.8 11.7 %collective-permute-start.11 = (bf16[8,128,128]{2,1,0:T(8,128)(2,1)S(1)}, bf16[8,128,128]{2,1,0:T(8,128)(2,1)S(1)}, u32[]{:S(2)}, u32[]{:S(2)}) collective-permute-start(bf16[8,128,128]{2,1,0:T(8,128)(2,1)S(1)} %slice.11), channel_id=1, source_target_pairs={{0,224},{32,0},{64,32},{96,64},{128,96},{160,128},{192,160},{224,1... | collective-permute-start | bytes 786440 | tf_op jit(solution)/shard_map/ppermute | solution.py:419
  110.4 6.5 %copy-start.1 = (bf16[7,128,128]{2,1,0:T(8,128)(2,1)}, bf16[7,128,128]{2,1,0:T(8,128)(2,1)S(1)}, u32[]{:S(2)}) copy-start(bf16[7,128,128]{2,1,0:T(8,128)(2,1)S(1)} %get-tuple-element.72.early_ref) | copy-start | bytes 688132
  110.4 12.9 %collective-permute-start.14 = (bf16[7,128,128]{2,1,0:T(8,128)(2,1)}, bf16[7,128,128]{2,1,0:T(8,128)(2,1)}, u32[]{:S(2)}, u32[]{:S(2)}) collective-permute-start(bf16[7,128,128]{2,1,0:T(8,128)(2,1)} %get-tuple-element.73), channel_id=1, source_target_pairs={{0,16},{16,0},{1,17},{17,1},{2,18},{18,2},{3,19},{19,3},{4,20},{20... | collective-permute-start | bytes 688136 | tf_op jit(solution)/shard_map/ppermute | solution.py:440
  114.5 0.7 copy-start.11
  114.5 0.8 copy-start.12
  114.5 2.3 %copy-start.8 = (bf16[4,16,64,128]{3,2,1,0:T(8,128)(2,1)}, bf16[4,16,64,128]{3,2,1,0:T(8,128)(2,1)S(1)}, u32[]{:S(2)}) copy-start(bf16[4,16,64,128]{3,2,1,0:T(8,128)(2,1)S(1)} %collective-permute-done.12.refs_1_) | copy-start | bytes 3145732
  114.6 2.3 %copy-start.9 = (bf16[4,16,64,128]{3,2,1,0:T(8,128)(2,1)}, bf16[4,16,64,128]{3,2,1,0:T(8,128)(2,1)S(1)}, u32[]{:S(2)}) copy-start(bf16[4,16,64,128]{3,2,1,0:T(8,128)(2,1)S(1)} %collective-permute-done.13.refs_2_) | copy-start | bytes 3145732
  116.9 6.4 %collective-permute-start.15 = (bf16[1,128,128]{2,1,0:T(8,128)(2,1)S(1)}, bf16[1,128,128]{2,1,0:T(8,128)(2,1)S(1)}, u32[]{:S(2)}, u32[]{:S(2)}) collective-permute-start(bf16[1,128,128]{2,1,0:T(8,128)(2,1)S(1)} %get-tuple-element.77), channel_id=1, source_target_pairs={{0,16},{16,0},{1,17},{17,1},{2,18},{18,2},{3,19},{19,3},{4,20},{20... | collective-permute-start | bytes 98312 | tf_op jit(solution)/shard_map/ppermute | solution.py:440
  117.7 17.3 %collective-permute-start.16 = (bf16[8,128,128]{2,1,0:T(8,128)(2,1)}, bf16[8,128,128]{2,1,0:T(8,128)(2,1)S(1)}, u32[]{:S(2)}, u32[]{:S(2)}) collective-permute-start(bf16[8,128,128]{2,1,0:T(8,128)(2,1)} %dynamic-slice_bitcast_fusion), channel_id=1, source_target_pairs={{0,16},{16,0},{1,17},{17,1},{2,18},{18,2},{3,19},{19,3},{4,20},{20... | collective-permute-start | bytes 786440 | tf_op jit(solution)/shard_map/ppermute | solution.py:440
  118.2 22.4 %all-to-all-start.1 = ((bf16[16,128,128]{2,1,0:T(8,128)(2,1)}), bf16[16,128,128]{2,1,0:T(8,128)(2,1)S(1)}, u32[]{:S(2)}, u32[]{:S(2)}) async-start(bf16[16,128,128]{2,1,0:T(8,128)(2,1)} %get-tuple-element.78), calls=%async_computation.1 | async-start | bytes 1048576 | tf_op jit(solution)/shard_map/all_to_all | solution.py:494
  123.3 26.1 %collective-permute-start.17 = (bf16[4,16,64,128]{3,2,1,0:T(8,128)(2,1)}, bf16[4,16,64,128]{3,2,1,0:T(8,128)(2,1)}, u32[]{:S(2)}, u32[]{:S(2)}) collective-permute-start(bf16[4,16,64,128]{3,2,1,0:T(8,128)(2,1)} %copy-done.8), channel_id=1, source_target_pairs={{0,4},{4,8},{8,12},{12,0},{1,5},{5,9},{9,13},{13,1},{2,6},{6,10},{... | collective-permute-start | bytes 3145736 | tf_op jit(solution)/shard_map/ppermute | solution.py:419
  123.3 0.9 copy-start.2
  140.6 41.4 %all-to-all-start.2 = ((bf16[16,3,128,128]{3,2,1,0:T(8,128)(2,1)}), bf16[16,3,128,128]{3,2,1,0:T(8,128)(2,1)S(1)}, u32[]{:S(2)}, u32[]{:S(2)}) async-start(bf16[16,3,128,128]{3,2,1,0:T(8,128)(2,1)} %backward.1), calls=%async_computation.2 | async-start | bytes 3145728 | tf_op jit(solution)/shard_map/all_to_all | solution.py:502
  144.2 9.6 %collective-permute-start.22 = (bf16[4,16,64,128]{3,2,1,0:T(8,128)(2,1)}, bf16[4,16,64,128]{3,2,1,0:T(8,128)(2,1)}, u32[]{:S(2)}, u32[]{:S(2)}) collective-permute-start(bf16[4,16,64,128]{3,2,1,0:T(8,128)(2,1)} %copy-done.3), channel_id=1, source_target_pairs={{0,16},{16,0},{1,17},{17,1},{2,18},{18,2},{3,19},{19,3},{4,20},{20... | collective-permute-start | bytes 3145736 | tf_op jit(solution)/shard_map/ppermute | solution.py:440
  144.3 11.1 %collective-permute-start.23 = (bf16[4,16,64,128]{3,2,1,0:T(8,128)(2,1)}, bf16[4,16,64,128]{3,2,1,0:T(8,128)(2,1)}, u32[]{:S(2)}, u32[]{:S(2)}) collective-permute-start(bf16[4,16,64,128]{3,2,1,0:T(8,128)(2,1)} %copy-done.8), channel_id=1, source_target_pairs={{0,16},{16,0},{1,17},{17,1},{2,18},{18,2},{3,19},{19,3},{4,20},{20... | collective-permute-start | bytes 3145736 | tf_op jit(solution)/shard_map/ppermute | solution.py:440
  144.8 12.0 %collective-permute-start.24 = (bf16[4,16,64,128]{3,2,1,0:T(8,128)(2,1)}, bf16[4,16,64,128]{3,2,1,0:T(8,128)(2,1)}, u32[]{:S(2)}, u32[]{:S(2)}) collective-permute-start(bf16[4,16,64,128]{3,2,1,0:T(8,128)(2,1)} %copy-done.9), channel_id=1, source_target_pairs={{0,16},{16,0},{1,17},{17,1},{2,18},{18,2},{3,19},{19,3},{4,20},{20... | collective-permute-start | bytes 3145736 | tf_op jit(solution)/shard_map/ppermute | solution.py:440
  149.4 7.4 %collective-permute-start.25 = (bf16[4,16,64,128]{3,2,1,0:T(8,128)(2,1)}, bf16[4,16,64,128]{3,2,1,0:T(8,128)(2,1)}, u32[]{:S(2)}, u32[]{:S(2)}) collective-permute-start(bf16[4,16,64,128]{3,2,1,0:T(8,128)(2,1)} %collective-permute-done.17.refs_3_), channel_id=1, source_target_pairs={{0,16},{16,0},{1,17},{17,1},{2,18},{18,2},{3,19},{19,3},{4,20},{20... | collective-permute-start | bytes 3145736 | tf_op jit(solution)/shard_map/ppermute | solution.py:440
  150.4 3.1 %collective-permute-start.18 = (bf16[16,128,128]{2,1,0:T(8,128)(2,1)}, bf16[16,128,128]{2,1,0:T(8,128)(2,1)S(1)}, u32[]{:S(2)}, u32[]{:S(2)}) collective-permute-start(bf16[16,128,128]{2,1,0:T(8,128)(2,1)} %get-tuple-element.83), channel_id=1, source_target_pairs={{0,16},{16,0},{1,17},{17,1},{2,18},{18,2},{3,19},{19,3},{4,20},{20... | collective-permute-start | bytes 1572872 | tf_op jit(solution)/shard_map/ppermute | solution.py:440
  153.7 9.1 %collective-permute-start.19 = (bf16[4,128,128]{2,1,0:T(8,128)(2,1)S(1)}, bf16[4,128,128]{2,1,0:T(8,128)(2,1)S(1)}, u32[]{:S(2)}, u32[]{:S(2)}) collective-permute-start(bf16[4,128,128]{2,1,0:T(8,128)(2,1)S(1)} %get-tuple-element.105), channel_id=1, source_target_pairs={{0,4},{4,8},{8,12},{12,0},{1,5},{5,9},{9,13},{13,1},{2,6},{6,10},{... | collective-permute-start | bytes 393224 | tf_op jit(solution)/shard_map/ppermute | solution.py:419
  153.8 9.0 %collective-permute-start.20 = (bf16[4,128,128]{2,1,0:T(8,128)(2,1)S(1)}, bf16[4,128,128]{2,1,0:T(8,128)(2,1)S(1)}, u32[]{:S(2)}, u32[]{:S(2)}) collective-permute-start(bf16[4,128,128]{2,1,0:T(8,128)(2,1)S(1)} %get-tuple-element.104), channel_id=1, source_target_pairs={{0,8},{4,12},{8,0},{12,4},{1,9},{5,13},{9,1},{13,5},{2,10},{6,14},... | collective-permute-start | bytes 393224 | tf_op jit(solution)/shard_map/ppermute | solution.py:419
  155.4 7.6 %collective-permute-start.21 = (bf16[4,128,128]{2,1,0:T(8,128)(2,1)S(1)}, bf16[4,128,128]{2,1,0:T(8,128)(2,1)S(1)}, u32[]{:S(2)}, u32[]{:S(2)}) collective-permute-start(bf16[4,128,128]{2,1,0:T(8,128)(2,1)S(1)} %get-tuple-element.103), channel_id=1, source_target_pairs={{0,12},{4,0},{8,4},{12,8},{1,13},{5,1},{9,5},{13,9},{2,14},{6,2},{... | collective-permute-start | bytes 393224 | tf_op jit(solution)/shard_map/ppermute | solution.py:419
  163.1 5.5 %collective-permute-start.26 = (bf16[4,128,128]{2,1,0:T(8,128)(2,1)S(1)}, bf16[4,128,128]{2,1,0:T(8,128)(2,1)S(1)}, u32[]{:S(2)}, u32[]{:S(2)}) collective-permute-start(bf16[4,128,128]{2,1,0:T(8,128)(2,1)S(1)} %add_convert_fusion.1), channel_id=1, source_target_pairs={{0,1},{1,2},{2,3},{3,0},{4,5},{5,6},{6,7},{7,4},{8,9},{9,10},{10,1... | collective-permute-start | bytes 393224 | tf_op jit(solution)/shard_map/ppermute | solution.py:419
  164.4 7.9 %collective-permute-start.27 = (bf16[4,128,128]{2,1,0:T(8,128)(2,1)S(1)}, bf16[4,128,128]{2,1,0:T(8,128)(2,1)S(1)}, u32[]{:S(2)}, u32[]{:S(2)}) collective-permute-start(bf16[4,128,128]{2,1,0:T(8,128)(2,1)S(1)} %add_convert_fusion.1), channel_id=1, source_target_pairs={{0,2},{1,3},{2,0},{3,1},{4,6},{5,7},{6,4},{7,5},{8,10},{9,11},{10,... | collective-permute-start | bytes 393224 | tf_op jit(solution)/shard_map/ppermute | solution.py:419
  167.2 5.5 %collective-permute-start.28 = (bf16[4,128,128]{2,1,0:T(8,128)(2,1)S(1)}, bf16[4,128,128]{2,1,0:T(8,128)(2,1)S(1)}, u32[]{:S(2)}, u32[]{:S(2)}) collective-permute-start(bf16[4,128,128]{2,1,0:T(8,128)(2,1)S(1)} %add_convert_fusion.1), channel_id=1, source_target_pairs={{0,3},{1,0},{2,1},{3,2},{4,7},{5,4},{6,5},{7,6},{8,11},{9,8},{10,9... | collective-permute-start | bytes 393224 | tf_op jit(solution)/shard_map/ppermute | solution.py:419
  172.8 10.7 %collective-permute-start.29 = (bf16[4,128,128]{2,1,0:T(8,128)(2,1)S(1)}, bf16[4,128,128]{2,1,0:T(8,128)(2,1)S(1)}, u32[]{:S(2)}, u32[]{:S(2)}) collective-permute-start(bf16[4,128,128]{2,1,0:T(8,128)(2,1)S(1)} %multiply_convert_fusion.refs_0_), channel_id=1, source_target_pairs={{0,4},{4,8},{8,12},{12,0},{1,5},{5,9},{9,13},{13,1},{2,6},{6,10},{... | collective-permute-start | bytes 393224 | tf_op jit(solution)/shard_map/ppermute | solution.py:419
  173.5 10.1 %collective-permute-start.30 = (bf16[4,128,128]{2,1,0:T(8,128)(2,1)S(1)}, bf16[4,128,128]{2,1,0:T(8,128)(2,1)S(1)}, u32[]{:S(2)}, u32[]{:S(2)}) collective-permute-start(bf16[4,128,128]{2,1,0:T(8,128)(2,1)S(1)} %multiply_convert_fusion.refs_0_), channel_id=1, source_target_pairs={{0,8},{4,12},{8,0},{12,4},{1,9},{5,13},{9,1},{13,5},{2,10},{6,14},... | collective-permute-start | bytes 393224 | tf_op jit(solution)/shard_map/ppermute | solution.py:419
  177.6 5.9 %collective-permute-start.31 = (bf16[4,128,128]{2,1,0:T(8,128)(2,1)S(1)}, bf16[4,128,128]{2,1,0:T(8,128)(2,1)S(1)}, u32[]{:S(2)}, u32[]{:S(2)}) collective-permute-start(bf16[4,128,128]{2,1,0:T(8,128)(2,1)S(1)} %multiply_convert_fusion.refs_0_), channel_id=1, source_target_pairs={{0,12},{4,0},{8,4},{12,8},{1,13},{5,1},{9,5},{13,9},{2,14},{6,2},{... | collective-permute-start | bytes 393224 | tf_op jit(solution)/shard_map/ppermute | solution.py:419
